TPU v7x, 256 devices: a whole 4x4x8 slice. The times are simulated.
256 devices in a mesh: ctx: 16 (over z, core), exp: 16 (over x, y).
Axes of the slice: x: 4, y: 4, z: 8, core: 2. Of those that a mesh axis runs over, the one named last changes fastest.
Arguments:
- x_inner: bfloat16 [16384, 4096], P('ctx', 'exp'), may hold values from -6 to 6
- bc_input: bfloat16 [16384, 256], P('ctx'), may hold values from -6 to 6
- gate_input: bfloat16 [16384, 4096], P('ctx', 'exp'), may hold values from -22 to 22
- conv_weight: float32 [4, 4096], P(None, 'exp'), may hold values from -3 to 3
- bc_conv_weight: float32 [4, 256], replicated, may hold values from -3 to 3
- step_size: float32 [16384, 64], P('ctx', 'exp'), may hold values from 0.002 to 0.05
- log_decay: float32 [16384, 64], P('ctx', 'exp'), may hold values from -1 to 0
- skip_gain: float32 [64], P('exp'), may hold values from 0.5 to 1.5
- norm_gain: float32 [4096], P('exp'), may hold values from 0.25 to 1.75
- out_weight: bfloat16 [4096, 2048], P('exp'), may hold values from -0.09375 to 0.09375
- residual: bfloat16 [16384, 2048], P(('ctx', 'exp')), may hold values from -6 to 6
- moe_gain: float32 [2048], replicated, may hold values from 0.25 to 1.75
- expert_ids: int32 [16384, 4], P(('ctx', 'exp')), may hold values from 0 to 31, all different within a row; in each aligned block of 64 rows (0 to 63, 64 to 127, ...) at most 9 rows name the same one
- route_weights: float32 [16384, 4], P(('ctx', 'exp')), may hold values from 0.1 to 0.6
- gate_up_weight: bfloat16 [32, 2048, 1408], P('exp', 'ctx'), may hold values from -0.125 to 0.125
- down_weight: bfloat16 [32, 704, 2048], P('exp', None, 'ctx'), may hold values from -0.21875 to 0.21875
- out_grad: bfloat16 [16384, 2048], P(('ctx', 'exp')), may hold values from -6 to 6
Outputs:
- layer_output: bfloat16 [16384, 2048], P(('ctx', 'exp'))
- residual_grad: bfloat16 [16384, 2048], P(('ctx', 'exp'))
- route_grads: float32 [16384, 4], P(('ctx', 'exp'))
Inputs may be any that keep to these rules, and one draw needn't show every extreme that they name: `expert_ids`: within the rows of one device (aligned blocks of 64 tokens) no expert is named by more than 9 rows, a bound that some block reaches; each row names 4 different experts.
All inputs are finite; a program needn't handle non-finite values.
Results may differ from a plain program's by a relative error of at most 0.03.
Values may be sent and summed in bfloat16 or wider, within the bound.
No kernel may reach another device: no remote copies, remote signals or barrier semaphores. Data moves between devices by JAX's collectives and lax.ppermute only.
A program may use at most 128 MiB of HBM per device.

v0:
```python
import jax
import jax.numpy as jnp
from jax import lax
from jax.experimental import pallas as pl
from jax.experimental.pallas import tpu as pltpu
from jax.sharding import Mesh
from jax.sharding import PartitionSpec as P

F32 = jnp.float32
BF16 = jnp.bfloat16
HIGH = lax.Precision.HIGHEST
SPAN = 128
CAP = 9
LANES = 128


def mm(a, b, dims, precision=None):
    return lax.dot_general(a, b, (dims, ((), ())), precision=precision, preferred_element_type=F32)


NN = ((1,), (0,))
NT = ((1,), (1,))
TN = ((0,), (0,))


def silu(v):
    return v * (1.0 / (1.0 + jnp.exp(-v)))


def call(kernel, outs, scratch=()):
    return pl.pallas_call(
        kernel,
        out_shape=outs,
        scratch_shapes=list(scratch),
        compiler_params=pltpu.CompilerParams(vmem_limit_bytes=58 << 20),
    )


def spread(values, first, heads, head_width):
    rows = values.shape[0]
    per = LANES // head_width
    lane = lax.broadcasted_iota(jnp.int32, (rows, LANES), 1)
    parts = []
    for group in range(heads // per):
        out = jnp.broadcast_to(values[:, first + group * per : first + group * per + 1], (rows, LANES))
        for i in range(1, per):
            col = first + group * per + i
            out = jnp.where(
                lane < i * head_width, out, jnp.broadcast_to(values[:, col : col + 1], (rows, LANES))
            )
        parts.append(out)
    return jnp.concatenate(parts, axis=1)


def mixer_local(x_inner, bc_input, rim, weight, sl, slt, skip_row, heads, ctx_count):
    rows, channels = x_inner.shape
    state_size = bc_input.shape[1] // 2
    width = channels + 2 * state_size
    head_width = channels // heads
    blocks = rows // SPAN
    chunk = state_size // ctx_count
    kernel_len = weight.shape[0]

    def kernel(x_ref, bc_ref, rim_ref, w_ref, sl_ref, slt_ref, skip_ref, y_ref, c_ref, e_ref, send_ref, pad_ref, held_ref, tot_ref):
        row_i = lax.broadcasted_iota(jnp.int32, (SPAN, SPAN), 0)
        col_i = lax.broadcasted_iota(jnp.int32, (SPAN, SPAN), 1)
        causal = row_i >= col_i
        lower = jnp.where(causal, 1.0, 0.0).astype(F32)
        upper = jnp.where(row_i <= col_i, 1.0, 0.0).astype(F32)
        lane = lax.broadcasted_iota(jnp.int32, (SPAN, LANES), 1)
        pad_ref[0:8, :] = rim_ref[...].astype(F32)
        held_ref[...] = jnp.zeros_like(held_ref)
        tot_ref[...] = jnp.zeros_like(tot_ref)

        def block(j, carry):
            at = pl.multiple_of(j * SPAN, SPAN)
            pad_ref[8:, :channels] = x_ref[pl.ds(at, SPAN), :].astype(F32)
            pad_ref[8:, channels:] = bc_ref[pl.ds(at, SPAN), :].astype(F32)
            summed = jnp.zeros((SPAN, width), F32)
            for k in range(kernel_len):
                begin = 8 - kernel_len + 1 + k
                summed = summed + w_ref[k : k + 1, :] * pad_ref[begin : begin + SPAN, :]
            tail_rows = pad_ref[SPAN : SPAN + 8, :]
            pad_ref[0:8, :] = tail_rows
            conv = silu(summed).astype(BF16)
            x_b = conv[:, :channels]
            b_b = conv[:, channels : channels + state_size]
            c_b = conv[:, channels + state_size :]
            x_f = x_b.astype(F32)
            sl_b = sl_ref[pl.ds(at, SPAN), :]
            cum = mm(lower, sl_b, NN, HIGH)
            slt_b = slt_ref[:, pl.ds(at, SPAN)]
            cum_t = mm(slt_b, upper, NN, HIGH)
            scores = mm(c_b, b_b, NT)
            within = []
            per = LANES // head_width
            for group in range(channels // LANES):
                x_g = x_b[:, group * LANES : (group + 1) * LANES]
                out = None
                for i in range(per):
                    h = group * per + i
                    gap = cum[:, heads + h : heads + h + 1] - cum_t[heads + h : heads + h + 1, :]
                    w = jnp.exp(jnp.where(causal, gap, -1e30)) * scores * slt_b[h : h + 1, :]
                    y_h = mm(w.astype(BF16), x_g, NN)
                    out = y_h if out is None else jnp.where(lane < i * head_width, out, y_h)
                within.append(out)
            within = jnp.concatenate(within, axis=1)
            held = held_ref[...]
            carried = mm(c_b, held.astype(BF16), NN) * spread(jnp.exp(cum), heads, heads, head_width)
            y_ref[pl.ds(at, SPAN), :] = within + carried + skip_ref[...] * x_f
            c_ref[pl.ds(at, SPAN), :] = c_b
            tot = tot_ref[0:1, :]
            e_ref[pl.ds(at, SPAN), :] = jnp.exp(jnp.minimum(tot + cum, 0.0))
            last = cum[SPAN - 1 : SPAN, :]
            tail = spread(jnp.exp(jnp.minimum(last - cum, 0.0)), heads, heads, head_width)
            step = spread(sl_b, 0, heads, head_width)
            x_t = (x_f * tail * step).astype(BF16)
            decay = spread(jnp.exp(jnp.minimum(last, 0.0)), heads, heads, head_width)
            held_ref[...] = decay * held + mm(b_b, x_t, TN)
            tot_ref[0:1, :] = tot + last
            return carry

        lax.fori_loop(0, blocks, block, 0)
        held = held_ref[...]
        total = spread(tot_ref[...], heads, heads, head_width)[0:1, :]
        hi = total.astype(BF16).astype(F32)
        mid = (total - hi).astype(BF16).astype(F32)
        low = total - hi - mid
        pick = lax.broadcasted_iota(jnp.int32, (8, channels), 0)
        extra = jnp.where(pick == 0, hi, jnp.where(pick == 1, mid, jnp.where(pick == 2, low, 0.0)))
        for d in range(ctx_count):
            part = jnp.concatenate([held[d * chunk : (d + 1) * chunk], extra], axis=0)
            send_ref[d] = part.astype(BF16)

    return call(
        kernel,
        (
            jax.ShapeDtypeStruct((rows, channels), F32),
            jax.ShapeDtypeStruct((rows, state_size), BF16),
            jax.ShapeDtypeStruct((rows, 2 * heads), F32),
            jax.ShapeDtypeStruct((ctx_count, chunk + 8, channels), BF16),
        ),
        (
            pltpu.VMEM((SPAN + 8, width), F32),
            pltpu.VMEM((state_size, channels), F32),
            pltpu.VMEM((8, 2 * heads), F32),
        ),
    )(x_inner, bc_input, rim, weight, sl, slt, skip_row)


def state_scan(received, chunk):
    count, _, channels = received.shape

    def kernel(r_ref, o_ref):
        arriving = jnp.zeros((chunk, channels), F32)
        for s in range(count):
            part = r_ref[s].astype(F32)
            o_ref[s] = arriving
            total = part[chunk : chunk + 1] + part[chunk + 1 : chunk + 2] + part[chunk + 2 : chunk + 3]
            arriving = jnp.exp(jnp.minimum(total, 0.0)) * arriving + part[:chunk]

    return call(kernel, jax.ShapeDtypeStruct((count, chunk, channels), F32))(received)


def gate_rows(y_local, c_rows, e_rows, arriving, gate_input, heads, x_count, y_count):
    rows, channels = y_local.shape
    head_width = channels // heads
    own = rows // (x_count * y_count)

    def kernel(y_ref, c_ref, e_ref, a_ref, g_ref, o_ref):
        state = a_ref[...].astype(BF16)
        for x in range(x_count):
            at = x * y_count * own
            size = y_count * own
            carried = mm(c_ref[at : at + size, :], state, NN) * spread(
                e_ref[at : at + size, :], heads, heads, head_width
            )
            gated = (y_ref[at : at + size, :] + carried) * silu(g_ref[at : at + size, :].astype(F32))
            for y in range(y_count):
                o_ref[y, x * own : (x + 1) * own, :] = gated[y * own : (y + 1) * own].astype(BF16)

    return call(kernel, jax.ShapeDtypeStruct((y_count, x_count * own, channels), BF16))(
        y_local, c_rows, e_rows, arriving, gate_input
    )


def project(gated, pieces, where, x_count):
    y_count, rows, channels = gated.shape
    out_width = pieces[0].shape[1]
    own = rows // x_count

    def kernel(where_ref, g_ref, *refs):
        o_ref = refs[-1]
        w_refs = refs[:-1]
        total = jnp.zeros((rows, out_width), F32)
        first = 0
        squares = jnp.zeros((rows, 1), F32)
        for y in range(y_count):
            part = g_ref[y].astype(F32)
            squares = squares + jnp.sum(part * part, axis=1, keepdims=True)
        for i, w_ref in enumerate(w_refs):
            size = w_ref.shape[0]
            lhs = g_ref[where_ref[i]]
            total = total + mm(lhs[:, first : first + size], w_ref[...], NN)
            first = (first + size) % channels
        hi = squares.astype(BF16).astype(F32)
        mid = (squares - hi).astype(BF16).astype(F32)
        low = squares - hi - mid
        lane = lax.broadcasted_iota(jnp.int32, (rows, LANES), 1)
        extra = jnp.where(lane == 0, hi, jnp.where(lane == 1, mid, jnp.where(lane == 2, low, 0.0)))
        for x in range(x_count):
            o_ref[x, :, :out_width] = total[x * own : (x + 1) * own].astype(BF16)
            o_ref[x, :, out_width:] = extra[x * own : (x + 1) * own].astype(BF16)

    vmem = pl.BlockSpec(memory_space=pltpu.VMEM)
    return pl.pallas_call(
        kernel,
        out_shape=jax.ShapeDtypeStruct((x_count, own, out_width + LANES), BF16),
        in_specs=[pl.BlockSpec(memory_space=pltpu.SMEM), vmem] + [vmem] * len(pieces),
        out_specs=vmem,
        compiler_params=pltpu.CompilerParams(vmem_limit_bytes=58 << 20),
    )(where, gated, *pieces)


def expert_of(row, owners, local_count):
    dest = (row * 7282) >> 16
    core = dest // owners
    return local_count * (dest - core * owners) + core, row - dest * CAP


def routing_rows(ids, expert_total, owners, local_count):
    tokens, top = ids.shape
    slots = expert_total * CAP
    member = jnp.zeros((tokens, expert_total), F32)
    for k in range(top):
        lane = lax.broadcasted_iota(jnp.int32, (tokens, expert_total), 1)
        member = member + jnp.where(lane == ids[:, k : k + 1], 1.0, 0.0)
    member = member.astype(BF16)
    earlier = lax.broadcasted_iota(jnp.int32, (tokens, tokens), 0) > lax.broadcasted_iota(
        jnp.int32, (tokens, tokens), 1
    )
    rank = mm(jnp.where(earlier, 1.0, 0.0).astype(BF16), member, NN)
    row = lax.broadcasted_iota(jnp.int32, (slots, expert_total), 0)
    expert, _ = expert_of(row, owners, local_count)
    spreading = jnp.where(
        expert == lax.broadcasted_iota(jnp.int32, (slots, expert_total), 1), 1.0, 0.0
    ).astype(BF16)
    hit = mm(spreading, member, NT)
    rank_of = mm(spreading, rank.astype(BF16), NT)
    _, slot = expert_of(lax.broadcasted_iota(jnp.int32, (slots, tokens), 0), owners, local_count)
    return jnp.where(rank_of == slot.astype(F32), hit, 0.0).astype(BF16)


def slot_masks(ids, expert_total, owners, local_count):
    tokens, top = ids.shape
    slots = expert_total * CAP
    lane = lax.broadcasted_iota(jnp.int32, (tokens, expert_total), 1)
    member = jnp.zeros((tokens, expert_total), F32)
    for k in range(top):
        member = member + jnp.where(lane == ids[:, k : k + 1], 1.0, 0.0)
    member = member.astype(BF16)
    earlier = lax.broadcasted_iota(jnp.int32, (tokens, tokens), 0) > lax.broadcasted_iota(
        jnp.int32, (tokens, tokens), 1
    )
    rank = mm(jnp.where(earlier, 1.0, 0.0).astype(BF16), member, NN)
    row = lax.broadcasted_iota(jnp.int32, (expert_total, slots), 1)
    expert, _ = expert_of(row, owners, local_count)
    spreading = jnp.where(
        expert == lax.broadcasted_iota(jnp.int32, (expert_total, slots), 0), 1.0, 0.0
    ).astype(BF16)
    rank_of = mm(rank.astype(BF16), spreading, NN)
    expert, slot = expert_of(lax.broadcasted_iota(jnp.int32, (tokens, slots), 1), owners, local_count)
    fits = rank_of == slot.astype(F32)
    return [fits & (expert == ids[:, k : k + 1]) for k in range(top)]


def to_tiles(scratch, rows, value, first=0):
    count = scratch.shape[0] // rows
    for i in range(value.shape[1] // LANES):
        scratch[pl.ds(first + i, rows, stride=count), :] = value[:, i * LANES : (i + 1) * LANES]


def dispatch_grads(ids, out_grad, expert_total, owners, local_count):
    tokens, width = out_grad.shape
    slots = expert_total * CAP
    count = width // LANES

    def kernel(i_ref, g_ref, o_ref, s_ref):
        pick = routing_rows(i_ref[...], expert_total, owners, local_count)
        to_tiles(s_ref, slots, mm(pick, g_ref[...], NN))
        o_ref[...] = s_ref[...].astype(BF16)

    return call(
        kernel,
        jax.ShapeDtypeStruct((slots * count, LANES), BF16),
        (pltpu.VMEM((slots * count, LANES), F32),),
    )(ids, out_grad)


def normalise(parts, residual, moe_gain, ids, inner_total, expert_total, owners, local_count):
    x_count, tokens, _ = parts.shape
    width = residual.shape[1]
    slots = expert_total * CAP
    count = width // LANES

    def kernel(p_ref, r_ref, m_ref, i_ref, o_ref, h_ref, v_ref, s_ref):
        summed = p_ref[0].astype(F32)
        for x in range(1, x_count):
            summed = summed + p_ref[x].astype(F32)
        squares = summed[:, width : width + 1] + summed[:, width + 1 : width + 2] + summed[:, width + 2 : width + 3]
        hidden = r_ref[...].astype(F32) + summed[:, :width] * lax.rsqrt(squares / inner_total + 1e-05)
        hidden = hidden.astype(BF16)
        h_ref[...] = hidden
        hidden = hidden.astype(F32)
        inv = lax.rsqrt(jnp.mean(hidden * hidden, axis=1, keepdims=True) + 1e-06)
        v_ref[...] = jnp.broadcast_to(inv, (tokens, LANES))
        normed = (hidden * inv * m_ref[...]).astype(BF16)
        pick = routing_rows(i_ref[...], expert_total, owners, local_count)
        to_tiles(s_ref, slots, mm(pick, normed, NN))
        o_ref[...] = s_ref[...].astype(BF16)

    return call(
        kernel,
        (
            jax.ShapeDtypeStruct((slots * count, LANES), BF16),
            jax.ShapeDtypeStruct((tokens, width), BF16),
            jax.ShapeDtypeStruct((tokens, LANES), F32),
        ),
        (pltpu.VMEM((slots * count, LANES), F32),),
    )(parts, residual, moe_gain, ids)


def gate_up_of(ref, lead, ff_tiles, rows):
    tiles = [ref[lead + (slice(i * rows, (i + 1) * rows), slice(None))] for i in range(ff_tiles)]
    return jnp.concatenate(tiles, axis=1)


def experts(rows_in, grads_in, weights, ff_width, gu_rows):
    count = weights.shape[0] * weights.shape[1]
    z_count, cores = weights.shape[:2]
    slots = rows_in.shape[0] // count
    ff_tiles = 2 * ff_width // LANES
    block = gu_rows // ff_tiles

    def kernel(x_ref, g_ref, w_ref, o_ref, b_ref, x_s, g_s):
        x_s[...] = x_ref[...].astype(F32)
        g_s[...] = g_ref[...].astype(F32)
        projected = jnp.zeros((slots, 2 * ff_width), F32)
        hidden_grad = jnp.zeros((slots, ff_width), F32)

        def columns(ref, z):
            return jnp.concatenate(
                [ref[pl.ds(z * cores + c, slots, stride=count), :].astype(BF16) for c in range(cores)],
                axis=1,
            )

        def gate_up(z):
            return jnp.concatenate([gate_up_of(w_ref, (z, c), ff_tiles, block) for c in range(cores)], axis=0)

        def down(z):
            return jnp.concatenate([w_ref[z, c, gu_rows:, :] for c in range(cores)], axis=1)

        for z in range(z_count):
            projected = projected + mm(columns(x_s, z), gate_up(z), NN)
            hidden_grad = hidden_grad + mm(columns(g_s, z), down(z), NT)
        pre_gate = projected[:, :ff_width]
        pre_up = projected[:, ff_width:]
        sig = 1.0 / (1.0 + jnp.exp(-pre_gate))
        act = pre_gate * sig
        activated = (act * pre_up).astype(BF16)
        grad_gate = hidden_grad * pre_up * sig * (1.0 + pre_gate * (1.0 - sig))
        grad_up = hidden_grad * act
        grad_both = jnp.concatenate([grad_gate, grad_up], axis=1).astype(BF16)
        for z in range(z_count):
            to_tiles(x_s, slots, mm(activated, down(z), NN), z * cores)
            to_tiles(g_s, slots, mm(grad_both, gate_up(z), NT), z * cores)
        o_ref[...] = x_s[...].astype(BF16)
        b_ref[...] = g_s[...].astype(BF16)

    shape = jax.ShapeDtypeStruct(rows_in.shape, BF16)
    return call(kernel, (shape, shape), (pltpu.VMEM(rows_in.shape, F32), pltpu.VMEM(rows_in.shape, F32)))(
        rows_in, grads_in, weights
    )


def combine(outs_back, grads_back, hidden, inv_rms, out_grad, moe_gain, ids, route_weights, expert_total, owners, local_count):
    tokens, width = hidden.shape
    top = ids.shape[1]
    count = width // LANES
    slots = expert_total * CAP

    def kernel(o_ref, b_ref, h_ref, v_ref, g_ref, m_ref, i_ref, w_ref, layer_ref, res_ref, route_ref, o_s, b_s):
        o_s[...] = o_ref[...].astype(F32)
        b_s[...] = b_ref[...].astype(F32)
        masks = slot_masks(i_ref[...], expert_total, owners, local_count)
        weight = jnp.zeros((tokens, slots), F32)
        for k in range(top):
            weight = weight + jnp.where(masks[k], w_ref[:, k : k + 1], 0.0)
        hi = weight.astype(BF16)
        both = jnp.concatenate([hi, (weight - hi.astype(F32)).astype(BF16)], axis=0)

        def rows_of(ref):
            return jnp.concatenate(
                [ref[pl.ds(i, slots, stride=count), :].astype(BF16) for i in range(count)], axis=1
            )

        hidden = h_ref[...].astype(F32)
        grad = g_ref[...]
        outs = rows_of(o_s)
        mixed = mm(both, outs, NN)
        layer_ref[...] = (hidden + (mixed[:tokens] + mixed[tokens:])).astype(BF16)
        dots = mm(grad, outs, NT)
        lane = lax.broadcasted_iota(jnp.int32, (tokens, top), 1)
        route = jnp.zeros((tokens, top), F32)
        for k in range(top):
            one = jnp.sum(jnp.where(masks[k], dots, 0.0), axis=1, keepdims=True)
            route = jnp.where(lane == k, one, route)
        route_ref[...] = route
        mixed = mm(both, rows_of(b_s), NN)
        inv = v_ref[:, 0:1]
        unit_grad = (mixed[:tokens] + mixed[tokens:]) * m_ref[...]
        unit_rows = hidden * inv
        mean = jnp.mean(unit_grad * unit_rows, axis=1, keepdims=True)
        res_ref[...] = (grad.astype(F32) + inv * (unit_grad - unit_rows * mean)).astype(BF16)

    shape = jax.ShapeDtypeStruct((tokens, width), BF16)
    return call(
        kernel,
        (shape, shape, jax.ShapeDtypeStruct((tokens, top), F32)),
        (pltpu.VMEM((slots * count, LANES), F32), pltpu.VMEM((slots * count, LANES), F32)),
    )(outs_back, grads_back, hidden, inv_rms, out_grad, moe_gain, ids, route_weights)


def ring_route(count, shift):
    return [(i, (i + shift) % count) for i in range(count)]


def local(
    x_inner,
    bc_input,
    gate_input,
    conv_weight,
    bc_conv_weight,
    step_size,
    log_decay,
    skip_gain,
    norm_gain,
    out_weight,
    residual,
    moe_gain,
    expert_ids,
    route_weights,
    gate_up_weight,
    down_weight,
    out_grad,
):
    ctx = ("z", "core")
    ctx_count = lax.axis_size("z") * lax.axis_size("core")
    x_count, y_count = lax.axis_size("x"), lax.axis_size("y")
    owners = x_count * y_count
    heads = step_size.shape[1]
    channels = x_inner.shape[1]
    head_width = channels // heads
    state_size = bc_input.shape[1] // 2
    local_count, d_local, ff_both = gate_up_weight.shape
    ff_width = down_weight.shape[1]
    expert_total = local_count * owners
    tokens, width = residual.shape
    exchange = ("core", "x", "y")

    last = jnp.concatenate([x_inner[-8:], bc_input[-8:]], axis=1)
    rim = lax.ppermute(last, ctx, [(i, i + 1) for i in range(ctx_count - 1)])

    tiles = ff_both // LANES
    packed = jnp.concatenate(
        [
            gate_up_weight.reshape(local_count, d_local, tiles, LANES).transpose(0, 2, 1, 3).reshape(local_count, tiles * d_local, LANES),
            down_weight,
        ],
        axis=1,
    )
    swapped = lax.all_to_all(packed, "core", split_axis=0, concat_axis=0, tiled=True)
    weights = lax.all_gather(swapped, "z", axis=0, tiled=False)

    folded = (out_weight.astype(F32) * norm_gain[:, None]).astype(BF16)
    half = folded.shape[0] // 2
    from_prev = lax.ppermute(folded, "y", ring_route(y_count, 1))
    from_next = lax.ppermute(folded, "y", ring_route(y_count, -1))
    far_a = lax.ppermute(from_prev[:half], "y", ring_route(y_count, 1))
    far_b = lax.ppermute(from_next[half:], "y", ring_route(y_count, -1))
    y_at = lax.axis_index("y")
    where = jnp.stack([y_at, (y_at + y_count - 1) % y_count, (y_at + 1) % y_count, (y_at + 2) % y_count, (y_at + 2) % y_count]).astype(jnp.int32)

    sent_grads = dispatch_grads(expert_ids, out_grad, expert_total, owners, local_count)
    grads_in = lax.all_to_all(
        sent_grads.reshape(expert_total, -1, LANES), exchange, split_axis=0, concat_axis=0, tiled=True
    )

    sl = jnp.concatenate([step_size, log_decay], axis=1)
    joint = jnp.concatenate([conv_weight, bc_conv_weight], axis=1)
    skip_row = jnp.repeat(skip_gain, head_width)[None, :]
    y_local, c_rows, e_rows, sent = mixer_local(
        x_inner, bc_input, rim, joint, sl, sl.T, skip_row, heads, ctx_count
    )
    received = lax.all_to_all(sent, ctx, split_axis=0, concat_axis=0, tiled=True)
    scanned = state_scan(received, state_size // ctx_count)
    arriving = lax.all_to_all(scanned, ctx, split_axis=0, concat_axis=0, tiled=True).reshape(state_size, channels)
    gated = gate_rows(y_local, c_rows, e_rows, arriving, gate_input, heads, x_count, y_count)
    gated = lax.all_to_all(gated, "y", split_axis=0, concat_axis=0, tiled=True)
    parts = project(gated, [folded, from_prev, from_next, far_a, far_b], where, x_count)
    parts = lax.all_to_all(parts, "x", split_axis=0, concat_axis=0, tiled=True)
    sent_rows, hidden, inv_rms = normalise(
        parts, residual, moe_gain[None, :], expert_ids, channels * owners, expert_total, owners, local_count
    )
    rows_in = lax.all_to_all(
        sent_rows.reshape(expert_total, -1, LANES), exchange, split_axis=0, concat_axis=0, tiled=True
    )
    outs, grads = experts(
        rows_in.reshape(-1, LANES), grads_in.reshape(-1, LANES), weights, ff_width, tiles * d_local
    )
    outs_back = lax.all_to_all(
        outs.reshape(expert_total, -1, LANES), exchange, split_axis=0, concat_axis=0, tiled=True
    )
    grads_back = lax.all_to_all(
        grads.reshape(expert_total, -1, LANES), exchange, split_axis=0, concat_axis=0, tiled=True
    )
    return combine(
        outs_back.reshape(-1, LANES),
        grads_back.reshape(-1, LANES),
        hidden,
        inv_rms,
        out_grad,
        moe_gain[None, :],
        expert_ids,
        route_weights,
        expert_total,
        owners,
        local_count,
    )


def solution(mesh):
    ctx_count, exp_count = mesh.devices.shape
    side = int(round(exp_count**0.5))
    devices = mesh.devices.reshape(ctx_count // 2, 2, side, exp_count // side)
    fine = Mesh(devices, ("z", "core", "x", "y"))
    ctx, exp = ("z", "core"), ("x", "y")
    token = P(ctx + exp, None)
    return jax.shard_map(
        local,
        mesh=fine,
        in_specs=(
            P(ctx, exp),
            P(ctx, None),
            P(ctx, exp),
            P(None, exp),
            P(),
            P(ctx, exp),
            P(ctx, exp),
            P(exp),
            P(exp),
            P(exp, None),
            token,
            P(),
            token,
            token,
            P(exp, ctx, None),
            P(exp, None, ctx),
            token,
        ),
        out_specs=(token, token, token),
        check_vma=False,
    )
```

profile of v0, /device:TPU:1, one launch (start us, length us, event | category | flops | bytes accessed | tf_op | source)
XLA Modules:
  0.0 235.6 jit_solution(3749577152964658975)
XLA Ops:
  9.2 8.4 %all_to_all.45 = bf16[2,2112,128]{2,1,0:T(8,128)(2,1)} all-to-all(bf16[2,2112,128]{2,1,0:T(8,128)(2,1)S(1)} %pad_maximum_fusion), channel_id=1, replica_groups=mesh['z'=8,'core'=2,'x'=4,'y'=4] {'core'}, dimensions={0} | all-to-all | bytes 2162688 | tf_op jit(solution)/shard_map/all_to_all | solution.py:482
  18.0 2.7 %collective-permute-start.2 = (bf16[256,2048]{1,0:T(8,128)(2,1)S(1)}, bf16[256,2048]{1,0:T(8,128)(2,1)S(1)}, u32[]{:S(2)}, u32[]{:S(2)}) collective-permute-start(bf16[256,2048]{1,0:T(8,128)(2,1)S(1)} %multiply_convert_fusion.refs_0_), channel_id=1, source_target_pairs={{0,3},{1,0},{2,1},{3,2},{4,7},{5,4},{6,5},{7,6},{8,11},{9,8},{10,9... | collective-permute-start | bytes 3145736 | tf_op jit(solution)/shard_map/ppermute | solution.py:488
  20.7 2.7 %collective-permute-start = (bf16[8,512]{1,0:T(8,128)(2,1)S(1)}, bf16[8,512]{1,0:T(8,128)(2,1)S(1)}, u32[]{:S(2)}, u32[]{:S(2)}) collective-permute-start(bf16[8,512]{1,0:T(8,128)(2,1)S(1)} %pad_maximum_fusion.2), channel_id=1, source_target_pairs={{0,16},{16,32},{32,48},{48,64},{64,80},{80,96},{96,112},{112,128},... | collective-permute-start | bytes 24584 | tf_op jit(solution)/shard_map/ppermute | solution.py:472
  26.9 8.7 %shard_map.184 = (f32[1024,256]{1,0:T(8,128)}, bf16[1024,128]{1,0:T(8,128)(2,1)}, f32[1024,8]{1,0:T(8,128)}, bf16[16,16,256]{2,1,0:T(8,128)(2,1)}) custom-call(bf16[1024,256]{1,0:T(8,128)(2,1)} %x_ref.1, bf16[1024,256]{1,0:T(8,128)(2,1)} %bc_ref.1, bf16[8,512]{1,0:T(8,128)(2,1)} %copy-done.13, f32[4,512]{1,0:T(4,128)} %pad_maximum_fusion.3.w_ref, ...), custom_call_target="tpu_custom_call" | custom-call | tf_op jit(solution)/shard_map/pallas_call | solution.py:135
  35.6 19.1 %all_to_all.46.r_ref = bf16[16,16,256]{2,1,0:T(8,128)(2,1)} all-to-all(bf16[16,16,256]{2,1,0:T(8,128)(2,1)} %get-tuple-element.15), channel_id=1, replica_groups=mesh['z'=8,'core'=2,'x'=4,'y'=4] {'z','core'}, dimensions={0} | all-to-all | bytes 262144 | tf_op jit(solution)/shard_map/all_to_all | solution.py:505
  56.3 3.4 %all-to-all-start.1 = ((f32[16,8,256]{2,1,0:T(8,128)}), f32[16,8,256]{2,1,0:T(8,128)S(1)}, u32[]{:S(2)}, u32[]{:S(2)}) async-start(f32[16,8,256]{2,1,0:T(8,128)} %shard_map.185), calls=%async_computation.1 | async-start | bytes 262144 | tf_op jit(solution)/shard_map/all_to_all | solution.py:507
  60.8 2.7 %collective-permute-start.4 = (bf16[128,2048]{1,0:T(8,128)(2,1)S(1)}, bf16[128,2048]{1,0:T(8,128)(2,1)S(1)}, u32[]{:S(2)}, u32[]{:S(2)}) collective-permute-start(bf16[128,2048]{1,0:T(8,128)(2,1)S(1)} %slice.17), channel_id=1, source_target_pairs={{0,3},{1,0},{2,1},{3,2},{4,7},{5,4},{6,5},{7,6},{8,11},{9,8},{10,9... | collective-permute-start | bytes 1572872 | tf_op jit(solution)/shard_map/ppermute | solution.py:490
  63.4 6.9 %all-to-all-done.1 = f32[16,8,256]{2,1,0:T(8,128)S(1)} async-done(((f32[16,8,256]{2,1,0:T(8,128)}), f32[16,8,256]{2,1,0:T(8,128)S(1)}, u32[]{:S(2)}, u32[]{:S(2)}) %all-to-all-start.1) | async-done | bytes 131104 | tf_op jit(solution)/shard_map/all_to_all | solution.py:507
  71.0 3.2 %shard_map.186 = bf16[4,256,256]{2,1,0:T(8,128)(2,1)} custom-call(f32[1024,256]{1,0:T(8,128)} %get-tuple-element.12.y_ref, bf16[1024,128]{1,0:T(8,128)(2,1)} %get-tuple-element.13.c_ref, f32[1024,8]{1,0:T(8,128)} %get-tuple-element.14.e_ref, f32[128,256]{1,0:T(8,128)} %bitcast.31, bf16[1024,256]{1,0:T(8,128)(2,1)} %g_ref.3), custom_call_target="tpu_custom_call" | custom-call | tf_op jit(solution)/shard_map/pallas_call | solution.py:182
  74.2 3.5 %all-to-all-start.2 = ((bf16[4,256,256]{2,1,0:T(8,128)(2,1)}), bf16[4,256,256]{2,1,0:T(8,128)(2,1)S(1)}, u32[]{:S(2)}, u32[]{:S(2)}) async-start(bf16[4,256,256]{2,1,0:T(8,128)(2,1)} %shard_map.186), calls=%async_computation.2 | async-start | bytes 1048576 | tf_op jit(solution)/shard_map/all_to_all | solution.py:509
  78.4 8.9 %all-to-all-done.2.g_ref = bf16[4,256,256]{2,1,0:T(8,128)(2,1)S(1)} async-done(((bf16[4,256,256]{2,1,0:T(8,128)(2,1)}), bf16[4,256,256]{2,1,0:T(8,128)(2,1)S(1)}, u32[]{:S(2)}, u32[]{:S(2)}) %all-to-all-start.2) | async-done | bytes 524320 | tf_op jit(solution)/shard_map/all_to_all | solution.py:509
  88.9 4.9 %shard_map.187 = bf16[4,64,2176]{2,1,0:T(8,128)(2,1)} custom-call(s32[5]{0:T(128)} %stack.20.where_ref, bf16[4,256,256]{2,1,0:T(8,128)(2,1)} %copy-done.6, bf16[256,2048]{1,0:T(8,128)(2,1)} %copy-done.3, bf16[256,2048]{1,0:T(8,128)(2,1)} %copy-done.4, bf16[256,2048]{1,0:T(8,128)(2,1)} %copy-done.5, bf16[128,2048]{1,0:T(8,128)(2,1)} %collective-permute-done.3.refs_3_, ...), custom_call_target="tpu_custom_call" | custom-call | tf_op jit(solution)/shard_map/pallas_call | solution.py:216
  93.8 4.1 %all-to-all-start.3 = ((bf16[4,64,2176]{2,1,0:T(8,128)(2,1)}), bf16[4,64,2176]{2,1,0:T(8,128)(2,1)S(1)}, u32[]{:S(2)}, u32[]{:S(2)}) async-start(bf16[4,64,2176]{2,1,0:T(8,128)(2,1)} %shard_map.187), calls=%async_computation.3 | async-start | bytes 2228224 | tf_op jit(solution)/shard_map/all_to_all | solution.py:511
  98.6 3.4 %shard_map.189 = bf16[4608,128]{1,0:T(8,128)(2,1)} custom-call(s32[64,4]{1,0:T(8,128)} %copy.43.i_ref, bf16[64,2048]{1,0:T(8,128)(2,1)} %g_ref.5), custom_call_target="tpu_custom_call" | custom-call | tf_op jit(solution)/shard_map/pallas_call | solution.py:293
  102.0 10.7 %all-to-all-done.3.p_ref = bf16[4,64,2176]{2,1,0:T(8,128)(2,1)S(1)} async-done(((bf16[4,64,2176]{2,1,0:T(8,128)(2,1)}), bf16[4,64,2176]{2,1,0:T(8,128)(2,1)S(1)}, u32[]{:S(2)}, u32[]{:S(2)}) %all-to-all-start.3) | async-done | bytes 1114144 | tf_op jit(solution)/shard_map/all_to_all | solution.py:511
  113.6 5.7 %all-to-all-start.5 = ((bf16[32,144,128]{2,1,0:T(8,128)(2,1)}), bf16[32,144,128]{2,1,0:T(8,128)(2,1)S(1)}, u32[]{:S(2)}, u32[]{:S(2)}) async-start(bf16[32,144,128]{2,1,0:T(8,128)(2,1)} %bitcast.22), calls=%async_computation.5 | async-start | bytes 2359296 | tf_op jit(solution)/shard_map/all_to_all | solution.py:495
  119.3 3.8 %shard_map.188 = (bf16[4608,128]{1,0:T(8,128)(2,1)}, bf16[64,2048]{1,0:T(8,128)(2,1)}, f32[64,128]{1,0:T(8,128)}) custom-call(bf16[4,64,2176]{2,1,0:T(8,128)(2,1)} %copy-done.2, bf16[64,2048]{1,0:T(8,128)(2,1)} %r_ref.1, f32[1,2048]{1,0:T(1,128)} %bitcast.32, s32[64,4]{1,0:T(8,128)} %copy.43.i_ref), custom_call_target="tpu_custom_call" | custom-call | tf_op jit(solution)/shard_map/pallas_call | solution.py:322
  123.2 14.0 %all-to-all-done.5 = bf16[32,144,128]{2,1,0:T(8,128)(2,1)S(1)} async-done(((bf16[32,144,128]{2,1,0:T(8,128)(2,1)}), bf16[32,144,128]{2,1,0:T(8,128)(2,1)S(1)}, u32[]{:S(2)}, u32[]{:S(2)}) %all-to-all-start.5) | async-done | bytes 1179680 | tf_op jit(solution)/shard_map/all_to_all | solution.py:495
  137.1 24.6 %all_to_all.47 = bf16[32,144,128]{2,1,0:T(8,128)(2,1)} all-to-all(bf16[32,144,128]{2,1,0:T(8,128)(2,1)} %bitcast.29), channel_id=1, replica_groups=mesh['z'=8,'core'=2,'x'=4,'y'=4] {'core','x','y'}, dimensions={0} | all-to-all | bytes 2359296 | tf_op jit(solution)/shard_map/all_to_all | solution.py:515
  161.7 13.2 %shard_map.190 = (bf16[4608,128]{1,0:T(8,128)(2,1)}, bf16[4608,128]{1,0:T(8,128)(2,1)}) custom-call(bf16[4608,128]{1,0:T(8,128)(2,1)} %bitcast.26, bf16[4608,128]{1,0:T(8,128)(2,1)} %bitcast.23, bf16[8,2,2112,128]{3,2,1,0:T(8,128)(2,1)} %bitcast.21), custom_call_target="tpu_custom_call" | custom-call | tf_op jit(solution)/shard_map/pallas_call | solution.py:381
  174.9 24.0 %all_to_all.48 = bf16[32,144,128]{2,1,0:T(8,128)(2,1)} all-to-all(bf16[32,144,128]{2,1,0:T(8,128)(2,1)} %bitcast.30), channel_id=1, replica_groups=mesh['z'=8,'core'=2,'x'=4,'y'=4] {'core','x','y'}, dimensions={0} | all-to-all | bytes 2359296 | tf_op jit(solution)/shard_map/all_to_all | solution.py:521
  198.9 4.6 %all-to-all-start.8 = ((bf16[32,144,128]{2,1,0:T(8,128)(2,1)}), bf16[32,144,128]{2,1,0:T(8,128)(2,1)S(1)}, u32[]{:S(2)}, u32[]{:S(2)}) async-start(bf16[32,144,128]{2,1,0:T(8,128)(2,1)} %bitcast.17), calls=%async_computation.8 | async-start | bytes 2359296 | tf_op jit(solution)/shard_map/all_to_all | solution.py:524
  204.2 17.0 %all-to-all-done.8 = bf16[32,144,128]{2,1,0:T(8,128)(2,1)S(1)} async-done(((bf16[32,144,128]{2,1,0:T(8,128)(2,1)}), bf16[32,144,128]{2,1,0:T(8,128)(2,1)S(1)}, u32[]{:S(2)}, u32[]{:S(2)}) %all-to-all-start.8) | async-done | bytes 1179680 | tf_op jit(solution)/shard_map/all_to_all | solution.py:524
  222.3 5.0 %shard_map.191 = (bf16[64,2048]{1,0:T(8,128)(2,1)}, bf16[64,2048]{1,0:T(8,128)(2,1)}, f32[64,4]{1,0:T(8,128)}) custom-call(bf16[4608,128]{1,0:T(8,128)(2,1)} %bitcast.24, bf16[4608,128]{1,0:T(8,128)(2,1)} %bitcast.25, bf16[64,2048]{1,0:T(8,128)(2,1)} %get-tuple-element.19.h_ref, f32[64,128]{1,0:T(8,128)} %get-tuple-element.20.v_ref, bf16[64,2048]{1,0:T(8,128)(2,1)} %g_ref.5, ...), custom_call_target="tpu_custom_call" | custom-call | tf_op jit(solution)/shard_map/pallas_call | solution.py:427
  (71 shorter events, 16.3 us)
Async XLA Ops:
  7.2 154.5 %all-gather.3.cloned.1.call-start = ((), (), s32[]{:S(2)}) async-start(), calls=%async_computation.9 | async-start | bytes 9732096 | tf_op jit(solution)/shard_map/all_gather | solution.py:483
  9.2 8.4 %copy-start.7 = (bf16[256,2048]{1,0:T(8,128)(2,1)S(1)}, bf16[256,2048]{1,0:T(8,128)(2,1)}, u32[]{:S(2)}) copy-start(bf16[256,2048]{1,0:T(8,128)(2,1)} %param.26) | copy-start | bytes 3145732
  9.2 8.4 %copy-start.18 = (f32[256]{0:T(256)S(1)}, f32[256]{0:T(256)}, u32[]{:S(2)}) copy-start(f32[256]{0:T(256)} %param.25) | copy-start | bytes 3076
  17.6 5.7 %copy-start.11 = (f32[1024,4]{0,1:T(4,128)S(1)}, f32[1024,4]{0,1:T(4,128)}, u32[]{:S(2)}) copy-start(f32[1024,4]{0,1:T(4,128)} %param.23) | copy-start | bytes 49156
  17.6 5.7 %copy-start.12 = (f32[1024,4]{0,1:T(4,128)S(1)}, f32[1024,4]{0,1:T(4,128)}, u32[]{:S(2)}) copy-start(f32[1024,4]{0,1:T(4,128)} %param.22) | copy-start | bytes 49156
  17.6 6.4 %copy-start.14 = (f32[4,256]{1,0:T(4,128)S(1)}, f32[4,256]{1,0:T(4,128)}, u32[]{:S(2)}) copy-start(f32[4,256]{1,0:T(4,128)} %param.21) | copy-start | bytes 12292
  17.7 6.4 %copy-start.15 = (f32[4,256]{1,0:T(4,128)S(1)}, f32[4,256]{1,0:T(4,128)}, u32[]{:S(2)}) copy-start(f32[4,256]{1,0:T(4,128)} %param.20) | copy-start | bytes 12292
  17.7 7.9 %copy-start.19 = (f32[4]{0:T(128)S(1)}, f32[4]{0:T(128)}, u32[]{:S(2)}) copy-start(f32[4]{0:T(128)} %param.24) | copy-start | bytes 52
  17.9 36.7 %copy-start.3 = (bf16[256,2048]{1,0:T(8,128)(2,1)}, bf16[256,2048]{1,0:T(8,128)(2,1)S(1)}, u32[]{:S(2)}) copy-start(bf16[256,2048]{1,0:T(8,128)(2,1)S(1)} %multiply_convert_fusion.refs_0_) | copy-start | bytes 3145732
  17.9 41.8 %collective-permute-start.1 = (bf16[256,2048]{1,0:T(8,128)(2,1)S(1)}, bf16[256,2048]{1,0:T(8,128)(2,1)S(1)}, u32[]{:S(2)}, u32[]{:S(2)}) collective-permute-start(bf16[256,2048]{1,0:T(8,128)(2,1)S(1)} %multiply_convert_fusion.refs_0_), channel_id=1, source_target_pairs={{0,1},{1,2},{2,3},{3,0},{4,5},{5,6},{6,7},{7,4},{8,9},{9,10},{10,1... | collective-permute-start | bytes 3145736 | tf_op jit(solution)/shard_map/ppermute | solution.py:487
  18.0 42.7 %collective-permute-start.2 = (bf16[256,2048]{1,0:T(8,128)(2,1)S(1)}, bf16[256,2048]{1,0:T(8,128)(2,1)S(1)}, u32[]{:S(2)}, u32[]{:S(2)}) collective-permute-start(bf16[256,2048]{1,0:T(8,128)(2,1)S(1)} %multiply_convert_fusion.refs_0_), channel_id=1, source_target_pairs={{0,3},{1,0},{2,1},{3,2},{4,7},{5,4},{6,5},{7,6},{8,11},{9,8},{10,9... | collective-permute-start | bytes 3145736 | tf_op jit(solution)/shard_map/ppermute | solution.py:488
  20.7 5.6 %collective-permute-start = (bf16[8,512]{1,0:T(8,128)(2,1)S(1)}, bf16[8,512]{1,0:T(8,128)(2,1)S(1)}, u32[]{:S(2)}, u32[]{:S(2)}) collective-permute-start(bf16[8,512]{1,0:T(8,128)(2,1)S(1)} %pad_maximum_fusion.2), channel_id=1, source_target_pairs={{0,16},{16,32},{32,48},{48,64},{64,80},{80,96},{96,112},{112,128},... | collective-permute-start | bytes 24584 | tf_op jit(solution)/shard_map/ppermute | solution.py:472
  56.3 14.0 %all-to-all-start.1 = ((f32[16,8,256]{2,1,0:T(8,128)}), f32[16,8,256]{2,1,0:T(8,128)S(1)}, u32[]{:S(2)}, u32[]{:S(2)}) async-start(f32[16,8,256]{2,1,0:T(8,128)} %shard_map.185), calls=%async_computation.1 | async-start | bytes 262144 | tf_op jit(solution)/shard_map/all_to_all | solution.py:507
  59.7 14.5 %copy-start.4 = (bf16[256,2048]{1,0:T(8,128)(2,1)}, bf16[256,2048]{1,0:T(8,128)(2,1)S(1)}, u32[]{:S(2)}) copy-start(bf16[256,2048]{1,0:T(8,128)(2,1)S(1)} %collective-permute-done.1.refs_1_) | copy-start | bytes 3145732
  60.6 26.6 %collective-permute-start.3 = (bf16[128,2048]{1,0:T(8,128)(2,1)}, bf16[128,2048]{1,0:T(8,128)(2,1)}, u32[]{:S(2)}, u32[]{:S(2)}) collective-permute-start(bf16[128,2048]{1,0:T(8,128)(2,1)} %slice.16), channel_id=1, source_target_pairs={{0,1},{1,2},{2,3},{3,0},{4,5},{5,6},{6,7},{7,4},{8,9},{9,10},{10,1... | collective-permute-start | bytes 1572872 | tf_op jit(solution)/shard_map/ppermute | solution.py:489
  60.7 13.5 %copy-start.5 = (bf16[256,2048]{1,0:T(8,128)(2,1)}, bf16[256,2048]{1,0:T(8,128)(2,1)S(1)}, u32[]{:S(2)}) copy-start(bf16[256,2048]{1,0:T(8,128)(2,1)S(1)} %collective-permute-done.2.refs_2_) | copy-start | bytes 3145732
  60.8 26.5 %collective-permute-start.4 = (bf16[128,2048]{1,0:T(8,128)(2,1)S(1)}, bf16[128,2048]{1,0:T(8,128)(2,1)S(1)}, u32[]{:S(2)}, u32[]{:S(2)}) collective-permute-start(bf16[128,2048]{1,0:T(8,128)(2,1)S(1)} %slice.17), channel_id=1, source_target_pairs={{0,3},{1,0},{2,1},{3,2},{4,7},{5,4},{6,5},{7,6},{8,11},{9,8},{10,9... | collective-permute-start | bytes 1572872 | tf_op jit(solution)/shard_map/ppermute | solution.py:490
  74.2 13.0 %all-to-all-start.2 = ((bf16[4,256,256]{2,1,0:T(8,128)(2,1)}), bf16[4,256,256]{2,1,0:T(8,128)(2,1)S(1)}, u32[]{:S(2)}, u32[]{:S(2)}) async-start(bf16[4,256,256]{2,1,0:T(8,128)(2,1)} %shard_map.186), calls=%async_computation.2 | async-start | bytes 1048576 | tf_op jit(solution)/shard_map/all_to_all | solution.py:509
  93.8 4.1 %copy-start.16 = (s32[64,4]{0,1:T(4,128)S(1)}, s32[64,4]{0,1:T(4,128)}, u32[]{:S(2)}) copy-start(s32[64,4]{0,1:T(4,128)} %param.29) | copy-start | bytes 3076
  93.8 18.9 %all-to-all-start.3 = ((bf16[4,64,2176]{2,1,0:T(8,128)(2,1)}), bf16[4,64,2176]{2,1,0:T(8,128)(2,1)S(1)}, u32[]{:S(2)}, u32[]{:S(2)}) async-start(bf16[4,64,2176]{2,1,0:T(8,128)(2,1)} %shard_map.187), calls=%async_computation.3 | async-start | bytes 2228224 | tf_op jit(solution)/shard_map/all_to_all | solution.py:511
  113.6 23.5 %all-to-all-start.5 = ((bf16[32,144,128]{2,1,0:T(8,128)(2,1)}), bf16[32,144,128]{2,1,0:T(8,128)(2,1)S(1)}, u32[]{:S(2)}, u32[]{:S(2)}) async-start(bf16[32,144,128]{2,1,0:T(8,128)(2,1)} %bitcast.22), calls=%async_computation.5 | async-start | bytes 2359296 | tf_op jit(solution)/shard_map/all_to_all | solution.py:495
  137.1 24.6 %copy-start = (bf16[32,144,128]{2,1,0:T(8,128)(2,1)}, bf16[32,144,128]{2,1,0:T(8,128)(2,1)S(1)}, u32[]{:S(2)}) copy-start(bf16[32,144,128]{2,1,0:T(8,128)(2,1)S(1)} %all-to-all-done.5) | copy-start | bytes 3538948
  198.9 4.6 %copy-start.17 = (f32[64,4]{0,1:T(4,128)S(1)}, f32[64,4]{0,1:T(4,128)}, u32[]{:S(2)}) copy-start(f32[64,4]{0,1:T(4,128)} %param.30) | copy-start | bytes 3076
  198.9 22.4 %all-to-all-start.8 = ((bf16[32,144,128]{2,1,0:T(8,128)(2,1)}), bf16[32,144,128]{2,1,0:T(8,128)(2,1)S(1)}, u32[]{:S(2)}, u32[]{:S(2)}) async-start(bf16[32,144,128]{2,1,0:T(8,128)(2,1)} %bitcast.17), calls=%async_computation.8 | async-start | bytes 2359296 | tf_op jit(solution)/shard_map/all_to_all | solution.py:524
  (9 other events, 13.0 us)
Sparse Core Ops, SparseCore 0:
  17.7 102.9 all-gather.2
where the time goes:
time: 237 us; the launch traced here: 236 us
  blocking collectives  76 us (32%)
  waiting for transfers between devices  57.5 us (24%)
  Pallas kernels  43.8 us (18%)
  starting transfers between devices  29.5 us (12%)
  between operations  14.3 us (6%)
  local copies, waits for them, and re-layouts  12.9 us (5%)
    all_to_all x1, blocking collectives, local(): lax.all_to_all(sent_rows.reshape(expert_total, -1, LANES), exchange, spli...  24.6 us
    all_to_all x1, blocking collectives, local(): lax.all_to_all(outs.reshape(expert_total, -1, LANES), exchange, split_axi...  24 us
    all_to_all x1, blocking collectives, local(): lax.all_to_all(sent, ctx, split_axis=0, concat_axis=0, tiled=True)  19.1 us
    all_to_all x1, waiting for transfers between devices, local(): lax.all_to_all(grads.reshape(expert_total, -1, LANES), exchange, split_ax...  17 us
    all_to_all x1, waiting for transfers between devices, local(): lax.all_to_all(sent_grads.reshape(expert_total, -1, LANES), exchange, spl...  14 us
    pallas_call x1, Pallas kernels, experts(): call(kernel, (shape, shape), (pltpu.VMEM(rows_in.shape, F32), pltpu.VMEM(...  13.2 us
    all_to_all x1, waiting for transfers between devices, local(): parts = lax.all_to_all(parts, 'x', split_axis=0, concat_axis=0, tiled=True)  10.7 us
    all_to_all x1, waiting for transfers between devices, local(): gated = lax.all_to_all(gated, 'y', split_axis=0, concat_axis=0, tiled=True)  8.86 us
  transfers between devices with their start and end apart: 11, of which 5 were waited for; matrix products, arithmetic and copies ran while one was open for 3% of the time, Pallas kernels for 11%

commit v1 on v0

--- a/solution.py
+++ b/solution.py
@@ -52,22 +52,27 @@
     return jnp.concatenate(parts, axis=1)
 
 
-def mixer_local(x_inner, bc_input, rim, weight, sl, slt, skip_row, heads, ctx_count):
+def columns_of(transposed, eye):
+    return mm(eye, transposed, NT, HIGH)
+
+
+def mixer_state(x_inner, bc_input, rim, conv_weight, bc_weight, step_t, decay_t, ctx_count):
     rows, channels = x_inner.shape
+    heads = step_t.shape[0]
     state_size = bc_input.shape[1] // 2
     width = channels + 2 * state_size
     head_width = channels // heads
     blocks = rows // SPAN
     chunk = state_size // ctx_count
-    kernel_len = weight.shape[0]
-
-    def kernel(x_ref, bc_ref, rim_ref, w_ref, sl_ref, slt_ref, skip_ref, y_ref, c_ref, e_ref, send_ref, pad_ref, held_ref, tot_ref):
+    kernel_len = conv_weight.shape[0]
+
+    def kernel(x_ref, bc_ref, rim_ref, wx_ref, wb_ref, step_ref, ld_ref, conv_ref, in_ref, send_ref, pad_ref, held_ref, tot_ref):
         row_i = lax.broadcasted_iota(jnp.int32, (SPAN, SPAN), 0)
         col_i = lax.broadcasted_iota(jnp.int32, (SPAN, SPAN), 1)
-        causal = row_i >= col_i
-        lower = jnp.where(causal, 1.0, 0.0).astype(F32)
-        upper = jnp.where(row_i <= col_i, 1.0, 0.0).astype(F32)
-        lane = lax.broadcasted_iota(jnp.int32, (SPAN, LANES), 1)
+        later = jnp.where(row_i < col_i, 1.0, 0.0).astype(F32)
+        eye = jnp.where(row_i == col_i, 1.0, 0.0).astype(F32)
+        ones = jnp.ones((SPAN, SPAN), F32)
+        weight = jnp.concatenate([wx_ref[...], wb_ref[...]], axis=1)
         pad_ref[0:8, :] = rim_ref[...].astype(F32)
         held_ref[...] = jnp.zeros_like(held_ref)
         tot_ref[...] = jnp.zeros_like(tot_ref)
@@ -79,50 +84,29 @@
             summed = jnp.zeros((SPAN, width), F32)
             for k in range(kernel_len):
                 begin = 8 - kernel_len + 1 + k
-                summed = summed + w_ref[k : k + 1, :] * pad_ref[begin : begin + SPAN, :]
+                summed = summed + weight[k : k + 1, :] * pad_ref[begin : begin + SPAN, :]
             tail_rows = pad_ref[SPAN : SPAN + 8, :]
             pad_ref[0:8, :] = tail_rows
             conv = silu(summed).astype(BF16)
-            x_b = conv[:, :channels]
+            conv_ref[pl.ds(at, SPAN), :] = conv
+            x_f = conv[:, :channels].astype(F32)
             b_b = conv[:, channels : channels + state_size]
-            c_b = conv[:, channels + state_size :]
-            x_f = x_b.astype(F32)
-            sl_b = sl_ref[pl.ds(at, SPAN), :]
-            cum = mm(lower, sl_b, NN, HIGH)
-            slt_b = slt_ref[:, pl.ds(at, SPAN)]
-            cum_t = mm(slt_b, upper, NN, HIGH)
-            scores = mm(c_b, b_b, NT)
-            within = []
-            per = LANES // head_width
-            for group in range(channels // LANES):
-                x_g = x_b[:, group * LANES : (group + 1) * LANES]
-                out = None
-                for i in range(per):
-                    h = group * per + i
-                    gap = cum[:, heads + h : heads + h + 1] - cum_t[heads + h : heads + h + 1, :]
-                    w = jnp.exp(jnp.where(causal, gap, -1e30)) * scores * slt_b[h : h + 1, :]
-                    y_h = mm(w.astype(BF16), x_g, NN)
-                    out = y_h if out is None else jnp.where(lane < i * head_width, out, y_h)
-                within.append(out)
-            within = jnp.concatenate(within, axis=1)
+            ld_b = ld_ref[:, pl.ds(at, SPAN)]
+            left = mm(later, ld_b, NT, HIGH)
+            step = columns_of(step_ref[:, pl.ds(at, SPAN)], eye)
+            tail = spread(jnp.exp(jnp.minimum(left, 0.0)) * step, 0, heads, head_width)
+            x_t = (x_f * tail).astype(BF16)
+            last = mm(ones, ld_b, NT, HIGH)
+            decay = spread(jnp.exp(jnp.minimum(last, 0.0)), 0, heads, head_width)
             held = held_ref[...]
-            carried = mm(c_b, held.astype(BF16), NN) * spread(jnp.exp(cum), heads, heads, head_width)
-            y_ref[pl.ds(at, SPAN), :] = within + carried + skip_ref[...] * x_f
-            c_ref[pl.ds(at, SPAN), :] = c_b
-            tot = tot_ref[0:1, :]
-            e_ref[pl.ds(at, SPAN), :] = jnp.exp(jnp.minimum(tot + cum, 0.0))
-            last = cum[SPAN - 1 : SPAN, :]
-            tail = spread(jnp.exp(jnp.minimum(last - cum, 0.0)), heads, heads, head_width)
-            step = spread(sl_b, 0, heads, head_width)
-            x_t = (x_f * tail * step).astype(BF16)
-            decay = spread(jnp.exp(jnp.minimum(last, 0.0)), heads, heads, head_width)
+            in_ref[pl.ds(at, SPAN), :] = held.astype(BF16)
             held_ref[...] = decay * held + mm(b_b, x_t, TN)
-            tot_ref[0:1, :] = tot + last
+            tot_ref[...] = tot_ref[...] + last[0:8, :]
             return carry
 
         lax.fori_loop(0, blocks, block, 0)
         held = held_ref[...]
-        total = spread(tot_ref[...], heads, heads, head_width)[0:1, :]
+        total = spread(tot_ref[...], 0, heads, head_width)[0:1, :]
         hi = total.astype(BF16).astype(F32)
         mid = (total - hi).astype(BF16).astype(F32)
         low = total - hi - mid
@@ -135,17 +119,86 @@
     return call(
         kernel,
         (
-            jax.ShapeDtypeStruct((rows, channels), F32),
-            jax.ShapeDtypeStruct((rows, state_size), BF16),
-            jax.ShapeDtypeStruct((rows, 2 * heads), F32),
+            jax.ShapeDtypeStruct((rows, width), BF16),
+            jax.ShapeDtypeStruct((blocks * state_size, channels), BF16),
             jax.ShapeDtypeStruct((ctx_count, chunk + 8, channels), BF16),
         ),
         (
             pltpu.VMEM((SPAN + 8, width), F32),
             pltpu.VMEM((state_size, channels), F32),
-            pltpu.VMEM((8, 2 * heads), F32),
+            pltpu.VMEM((8, heads), F32),
         ),
-    )(x_inner, bc_input, rim, weight, sl, slt, skip_row)
+    )(x_inner, bc_input, rim, conv_weight, bc_weight, step_t, decay_t)
+
+
+def mixer_rows(conv, entering, step_t, decay_t, skip_gain, channels):
+    rows = conv.shape[0]
+    heads = step_t.shape[0]
+    state_size = (conv.shape[1] - channels) // 2
+    head_width = channels // heads
+    blocks = rows // SPAN
+
+    def kernel(skip_ref, conv_ref, in_ref, step_ref, ld_ref, y_ref, e_ref, tot_ref):
+        row_i = lax.broadcasted_iota(jnp.int32, (SPAN, SPAN), 0)
+        col_i = lax.broadcasted_iota(jnp.int32, (SPAN, SPAN), 1)
+        causal = row_i >= col_i
+        lower = jnp.where(causal, 1.0, 0.0).astype(F32)
+        upper = jnp.where(row_i <= col_i, 1.0, 0.0).astype(F32)
+        lane = lax.broadcasted_iota(jnp.int32, (SPAN, LANES), 1)
+        lane_row = lax.broadcasted_iota(jnp.int32, (1, LANES), 1)
+        per = LANES // head_width
+        skip = []
+        for group in range(channels // LANES):
+            out = jnp.full((1, LANES), skip_ref[group * per], F32)
+            for i in range(1, per):
+                out = jnp.where(lane_row < i * head_width, out, skip_ref[group * per + i])
+            skip.append(out)
+        skip = jnp.concatenate(skip, axis=1)
+        tot_ref[...] = jnp.zeros_like(tot_ref)
+
+        def block(j, carry):
+            at = pl.multiple_of(j * SPAN, SPAN)
+            x_b = conv_ref[pl.ds(at, SPAN), :channels]
+            b_b = conv_ref[pl.ds(at, SPAN), channels : channels + state_size]
+            c_b = conv_ref[pl.ds(at, SPAN), channels + state_size :]
+            ld_b = ld_ref[:, pl.ds(at, SPAN)]
+            step_b = step_ref[:, pl.ds(at, SPAN)]
+            cum = mm(lower, ld_b, NT, HIGH)
+            cum_t = mm(ld_b, upper, NN, HIGH)
+            scores = mm(c_b, b_b, NT)
+            within = []
+            for group in range(channels // LANES):
+                x_g = x_b[:, group * LANES : (group + 1) * LANES]
+                out = None
+                for i in range(per):
+                    h = group * per + i
+                    gap = cum[:, h : h + 1] - cum_t[h : h + 1, :]
+                    w = jnp.exp(jnp.where(causal, gap, -1e30)) * scores * step_b[h : h + 1, :]
+                    y_h = mm(w.astype(BF16), x_g, NN)
+                    out = y_h if out is None else jnp.where(lane < i * head_width, out, y_h)
+                within.append(out)
+            within = jnp.concatenate(within, axis=1)
+            carried = mm(c_b, in_ref[pl.ds(at, SPAN), :], NN) * spread(jnp.exp(cum), 0, heads, head_width)
+            y_ref[pl.ds(at, SPAN), :] = within + carried + skip * x_b.astype(F32)
+            tot = tot_ref[0:1, :]
+            e_ref[pl.ds(at, SPAN), :] = jnp.exp(jnp.minimum(tot + cum, 0.0))
+            tot_ref[...] = tot_ref[...] + cum[SPAN - 1 : SPAN, :]
+            return carry
+
+        lax.fori_loop(0, blocks, block, 0)
+
+    vmem = pl.BlockSpec(memory_space=pltpu.VMEM)
+    return pl.pallas_call(
+        kernel,
+        out_shape=(
+            jax.ShapeDtypeStruct((rows, channels), F32),
+            jax.ShapeDtypeStruct((rows, heads), F32),
+        ),
+        in_specs=[pl.BlockSpec(memory_space=pltpu.SMEM)] + [vmem] * 4,
+        out_specs=(vmem, vmem),
+        scratch_shapes=[pltpu.VMEM((8, heads), F32)],
+        compiler_params=pltpu.CompilerParams(vmem_limit_bytes=58 << 20),
+    )(skip_gain, conv, entering, step_t, decay_t)
 
 
 def state_scan(received, chunk):
@@ -162,8 +215,10 @@
     return call(kernel, jax.ShapeDtypeStruct((count, chunk, channels), F32))(received)
 
 
-def gate_rows(y_local, c_rows, e_rows, arriving, gate_input, heads, x_count, y_count):
+def gate_rows(y_local, conv, e_rows, arriving, gate_input, x_count, y_count):
     rows, channels = y_local.shape
+    heads = e_rows.shape[1]
+    state_size = arriving.shape[0]
     head_width = channels // heads
     own = rows // (x_count * y_count)
 
@@ -172,15 +227,15 @@
         for x in range(x_count):
             at = x * y_count * own
             size = y_count * own
-            carried = mm(c_ref[at : at + size, :], state, NN) * spread(
-                e_ref[at : at + size, :], heads, heads, head_width
+            carried = mm(c_ref[at : at + size, channels + state_size :], state, NN) * spread(
+                e_ref[at : at + size, :], 0, heads, head_width
             )
             gated = (y_ref[at : at + size, :] + carried) * silu(g_ref[at : at + size, :].astype(F32))
             for y in range(y_count):
                 o_ref[y, x * own : (x + 1) * own, :] = gated[y * own : (y + 1) * own].astype(BF16)
 
     return call(kernel, jax.ShapeDtypeStruct((y_count, x_count * own, channels), BF16))(
-        y_local, c_rows, e_rows, arriving, gate_input
+        y_local, conv, e_rows, arriving, gate_input
     )
 
 
@@ -228,8 +283,19 @@
     return local_count * (dest - core * owners) + core, row - dest * CAP
 
 
-def routing_rows(ids, expert_total, owners, local_count):
-    tokens, top = ids.shape
+def id_columns(ids_t):
+    tokens = ids_t.shape[1]
+    eye = jnp.where(
+        lax.broadcasted_iota(jnp.int32, (tokens, tokens), 0) == lax.broadcasted_iota(jnp.int32, (tokens, tokens), 1),
+        1.0,
+        0.0,
+    )
+    return columns_of(ids_t.astype(F32), eye), eye
+
+
+def routing_rows(ids_t, expert_total, owners, local_count):
+    top, tokens = ids_t.shape
+    ids = (id_columns(ids_t)[0] + 0.5).astype(jnp.int32)
     slots = expert_total * CAP
     member = jnp.zeros((tokens, expert_total), F32)
     for k in range(top):
@@ -251,8 +317,9 @@
     return jnp.where(rank_of == slot.astype(F32), hit, 0.0).astype(BF16)
 
 
-def slot_masks(ids, expert_total, owners, local_count):
-    tokens, top = ids.shape
+def slot_masks(ids_t, expert_total, owners, local_count):
+    top, tokens = ids_t.shape
+    ids = (id_columns(ids_t)[0] + 0.5).astype(jnp.int32)
     slots = expert_total * CAP
     lane = lax.broadcasted_iota(jnp.int32, (tokens, expert_total), 1)
     member = jnp.zeros((tokens, expert_total), F32)
@@ -330,39 +397,71 @@
     )(parts, residual, moe_gain, ids)
 
 
-def gate_up_of(ref, lead, ff_tiles, rows):
-    tiles = [ref[lead + (slice(i * rows, (i + 1) * rows), slice(None))] for i in range(ff_tiles)]
-    return jnp.concatenate(tiles, axis=1)
-
-
-def experts(rows_in, grads_in, weights, ff_width, gu_rows):
-    count = weights.shape[0] * weights.shape[1]
-    z_count, cores = weights.shape[:2]
+def pack_weights(core, gate_up, down):
+    local_count, d_local, ff_both = gate_up.shape
+    ff_width = down.shape[1]
+    tiles = ff_both // LANES
+    height = tiles * d_local + ff_width
+
+    def kernel(core_ref, g_ref, d_ref, keep_ref, send_ref):
+        for out_ref, e in ((keep_ref, core_ref[0]), (send_ref, 1 - core_ref[0])):
+            for i in range(tiles):
+                out_ref[i * d_local : (i + 1) * d_local, :] = g_ref[e, :, i * LANES : (i + 1) * LANES]
+            out_ref[tiles * d_local :, :] = d_ref[e]
+
+    vmem = pl.BlockSpec(memory_space=pltpu.VMEM)
+    shape = jax.ShapeDtypeStruct((height, LANES), BF16)
+    return pl.pallas_call(
+        kernel,
+        out_shape=(shape, shape),
+        in_specs=[pl.BlockSpec(memory_space=pltpu.SMEM), vmem, vmem],
+        out_specs=(vmem, vmem),
+        compiler_params=pltpu.CompilerParams(vmem_limit_bytes=58 << 20),
+    )(core, gate_up, down)
+
+
+def experts(core, rows_in, grads_in, weights, ff_width, gu_rows):
+    z_count, cores, height, _ = weights.shape
+    count = z_count * cores
     slots = rows_in.shape[0] // count
+    dests = slots // CAP
     ff_tiles = 2 * ff_width // LANES
     block = gu_rows // ff_tiles
-
-    def kernel(x_ref, g_ref, w_ref, o_ref, b_ref, x_s, g_s):
+    each = CAP * count
+
+    def kernel(core_ref, x_ref, g_ref, w_hbm, o_ref, x_s, g_s, xb_s, gb_s, w_ref, sems):
+        copies = [pltpu.make_async_copy(w_hbm.at[z], w_ref.at[z], sems.at[z]) for z in range(z_count)]
+        for copy in copies:
+            copy.start()
+        core = core_ref[0]
         x_s[...] = x_ref[...].astype(F32)
         g_s[...] = g_ref[...].astype(F32)
-        projected = jnp.zeros((slots, 2 * ff_width), F32)
-        hidden_grad = jnp.zeros((slots, ff_width), F32)
-
-        def columns(ref, z):
-            return jnp.concatenate(
-                [ref[pl.ds(z * cores + c, slots, stride=count), :].astype(BF16) for c in range(cores)],
-                axis=1,
+        order = [(z, s, z * cores + (core if s == 0 else 1 - core)) for z in range(z_count) for s in range(cores)]
+        for i, (z, s, c) in enumerate(order):
+            xb_s[:, i * LANES : (i + 1) * LANES] = x_s[pl.ds(c, slots, stride=count), :].astype(BF16)
+            gb_s[:, i * LANES : (i + 1) * LANES] = g_s[pl.ds(c, slots, stride=count), :].astype(BF16)
+
+        def tile(z, s, i):
+            return w_ref[z, s, i * block : (i + 1) * block, :]
+
+        for copy in copies:
+            copy.wait()
+        projected = []
+        for first in range(0, ff_tiles, 2):
+            used = range(first, min(first + 2, ff_tiles))
+            rhs = jnp.concatenate(
+                [jnp.concatenate([tile(z, s, i) for i in used], axis=1) for z, s, _ in order], axis=0
             )
-
-        def gate_up(z):
-            return jnp.concatenate([gate_up_of(w_ref, (z, c), ff_tiles, block) for c in range(cores)], axis=0)
-
-        def down(z):
-            return jnp.concatenate([w_ref[z, c, gu_rows:, :] for c in range(cores)], axis=1)
-
-        for z in range(z_count):
-            projected = projected + mm(columns(x_s, z), gate_up(z), NN)
-            hidden_grad = hidden_grad + mm(columns(g_s, z), down(z), NT)
+            projected.append(mm(xb_s[...], rhs, NN))
+        projected = jnp.concatenate(projected, axis=1)
+        hidden_grad = []
+        for first in range(0, ff_width, 256):
+            size = min(256, ff_width - first)
+            rhs = jnp.concatenate(
+                [w_ref[z, s, gu_rows + first : gu_rows + first + size, :] for z, s, _ in order], axis=1
+            )
+            hidden_grad.append(mm(gb_s[...], rhs, NT))
+        hidden_grad = jnp.concatenate(hidden_grad, axis=1)
         pre_gate = projected[:, :ff_width]
         pre_up = projected[:, ff_width:]
         sig = 1.0 / (1.0 + jnp.exp(-pre_gate))
@@ -372,30 +471,55 @@
         grad_up = hidden_grad * act
         grad_both = jnp.concatenate([grad_gate, grad_up], axis=1).astype(BF16)
         for z in range(z_count):
-            to_tiles(x_s, slots, mm(activated, down(z), NN), z * cores)
-            to_tiles(g_s, slots, mm(grad_both, gate_up(z), NT), z * cores)
-        o_ref[...] = x_s[...].astype(BF16)
-        b_ref[...] = g_s[...].astype(BF16)
-
-    shape = jax.ShapeDtypeStruct(rows_in.shape, BF16)
-    return call(kernel, (shape, shape), (pltpu.VMEM(rows_in.shape, F32), pltpu.VMEM(rows_in.shape, F32)))(
-        rows_in, grads_in, weights
-    )
-
-
-def combine(outs_back, grads_back, hidden, inv_rms, out_grad, moe_gain, ids, route_weights, expert_total, owners, local_count):
+            rhs = jnp.concatenate([w_ref[z, s, gu_rows:, :] for s in range(cores)], axis=1)
+            out = mm(activated, rhs, NN)
+            rhs = jnp.concatenate(
+                [jnp.concatenate([tile(z, s, i) for i in range(ff_tiles)], axis=1) for s in range(cores)], axis=0
+            )
+            grad = mm(grad_both, rhs, NT)
+            for s in range(cores):
+                c = z * cores + (core if s == 0 else 1 - core)
+                x_s[pl.ds(c, slots, stride=count), :] = out[:, s * LANES : (s + 1) * LANES]
+                g_s[pl.ds(c, slots, stride=count), :] = grad[:, s * LANES : (s + 1) * LANES]
+        for d in range(dests):
+            o_ref[d, :each, :] = x_s[d * each : (d + 1) * each, :].astype(BF16)
+            o_ref[d, each:, :] = g_s[d * each : (d + 1) * each, :].astype(BF16)
+
+    vmem = pl.BlockSpec(memory_space=pltpu.VMEM)
+    return pl.pallas_call(
+        kernel,
+        out_shape=jax.ShapeDtypeStruct((dests, 2 * each, LANES), BF16),
+        in_specs=[pl.BlockSpec(memory_space=pltpu.SMEM), vmem, vmem, pl.BlockSpec(memory_space=pl.ANY)],
+        out_specs=vmem,
+        scratch_shapes=[
+            pltpu.VMEM(rows_in.shape, F32),
+            pltpu.VMEM(rows_in.shape, F32),
+            pltpu.VMEM((slots, count * LANES), BF16),
+            pltpu.VMEM((slots, count * LANES), BF16),
+            pltpu.VMEM(weights.shape, BF16),
+            pltpu.SemaphoreType.DMA((z_count,)),
+        ],
+        compiler_params=pltpu.CompilerParams(vmem_limit_bytes=58 << 20),
+    )(core, rows_in, grads_in, weights)
+
+
+def combine(back, hidden, inv_rms, out_grad, moe_gain, ids_t, route_t, expert_total, owners, local_count):
     tokens, width = hidden.shape
-    top = ids.shape[1]
+    top = ids_t.shape[0]
     count = width // LANES
     slots = expert_total * CAP
-
-    def kernel(o_ref, b_ref, h_ref, v_ref, g_ref, m_ref, i_ref, w_ref, layer_ref, res_ref, route_ref, o_s, b_s):
-        o_s[...] = o_ref[...].astype(F32)
-        b_s[...] = b_ref[...].astype(F32)
+    each = CAP * count
+
+    def kernel(r_ref, h_ref, v_ref, g_ref, m_ref, i_ref, w_ref, layer_ref, res_ref, route_ref, o_s, b_s):
+        for d in range(expert_total):
+            o_s[d * each : (d + 1) * each, :] = r_ref[d, :each, :].astype(F32)
+            b_s[d * each : (d + 1) * each, :] = r_ref[d, each:, :].astype(F32)
         masks = slot_masks(i_ref[...], expert_total, owners, local_count)
+        eye = id_columns(i_ref[...])[1]
+        routes = columns_of(w_ref[...], eye)
         weight = jnp.zeros((tokens, slots), F32)
         for k in range(top):
-            weight = weight + jnp.where(masks[k], w_ref[:, k : k + 1], 0.0)
+            weight = weight + jnp.where(masks[k], routes[:, k : k + 1], 0.0)
         hi = weight.astype(BF16)
         both = jnp.concatenate([hi, (weight - hi.astype(F32)).astype(BF16)], axis=0)
 
@@ -415,7 +539,7 @@
         for k in range(top):
             one = jnp.sum(jnp.where(masks[k], dots, 0.0), axis=1, keepdims=True)
             route = jnp.where(lane == k, one, route)
-        route_ref[...] = route
+        route_ref[...] = mm(route, eye, TN, HIGH)
         mixed = mm(both, rows_of(b_s), NN)
         inv = v_ref[:, 0:1]
         unit_grad = (mixed[:tokens] + mixed[tokens:]) * m_ref[...]
@@ -426,9 +550,9 @@
     shape = jax.ShapeDtypeStruct((tokens, width), BF16)
     return call(
         kernel,
-        (shape, shape, jax.ShapeDtypeStruct((tokens, top), F32)),
+        (shape, shape, jax.ShapeDtypeStruct((top, tokens), F32)),
         (pltpu.VMEM((slots * count, LANES), F32), pltpu.VMEM((slots * count, LANES), F32)),
-    )(outs_back, grads_back, hidden, inv_rms, out_grad, moe_gain, ids, route_weights)
+    )(back, hidden, inv_rms, out_grad, moe_gain, ids_t, route_t)
 
 
 def ring_route(count, shift):
@@ -468,75 +592,60 @@
     tokens, width = residual.shape
     exchange = ("core", "x", "y")
 
+    ids_t, route_t = expert_ids.T, route_weights.T
+    step_t, decay_t = step_size.T, log_decay.T
+    core = lax.axis_index("core").astype(jnp.int32).reshape(1)
+
     last = jnp.concatenate([x_inner[-8:], bc_input[-8:]], axis=1)
     rim = lax.ppermute(last, ctx, [(i, i + 1) for i in range(ctx_count - 1)])
 
-    tiles = ff_both // LANES
-    packed = jnp.concatenate(
-        [
-            gate_up_weight.reshape(local_count, d_local, tiles, LANES).transpose(0, 2, 1, 3).reshape(local_count, tiles * d_local, LANES),
-            down_weight,
-        ],
-        axis=1,
-    )
-    swapped = lax.all_to_all(packed, "core", split_axis=0, concat_axis=0, tiled=True)
-    weights = lax.all_gather(swapped, "z", axis=0, tiled=False)
+    kept, other = pack_weights(core, gate_up_weight, down_weight)
+    swapped = lax.ppermute(other, "core", [(0, 1), (1, 0)])
+    weights = lax.all_gather(jnp.stack([kept, swapped]), "z", axis=0, tiled=False)
+    gu_rows = kept.shape[0] - ff_width
+
+    sent_grads = dispatch_grads(ids_t, out_grad, expert_total, owners, local_count)
+    rim, sent_grads = lax.optimization_barrier((rim, sent_grads))
+
+    conv, held_in, sent = mixer_state(
+        x_inner, bc_input, rim, conv_weight, bc_conv_weight, step_t, decay_t, ctx_count
+    )
+    received = lax.all_to_all(sent, ctx, split_axis=0, concat_axis=0, tiled=True)
+    grads_in = lax.all_to_all(
+        sent_grads.reshape(expert_total, -1, LANES), exchange, split_axis=0, concat_axis=0, tiled=True
+    )
 
     folded = (out_weight.astype(F32) * norm_gain[:, None]).astype(BF16)
+    folded, rim = lax.optimization_barrier((folded, rim))
     half = folded.shape[0] // 2
     from_prev = lax.ppermute(folded, "y", ring_route(y_count, 1))
     from_next = lax.ppermute(folded, "y", ring_route(y_count, -1))
+    y_local, e_rows = mixer_rows(conv, held_in, step_t, decay_t, skip_gain, channels)
+    received, from_prev, from_next, y_local = lax.optimization_barrier((received, from_prev, from_next, y_local))
     far_a = lax.ppermute(from_prev[:half], "y", ring_route(y_count, 1))
     far_b = lax.ppermute(from_next[half:], "y", ring_route(y_count, -1))
     y_at = lax.axis_index("y")
     where = jnp.stack([y_at, (y_at + y_count - 1) % y_count, (y_at + 1) % y_count, (y_at + 2) % y_count, (y_at + 2) % y_count]).astype(jnp.int32)
 
-    sent_grads = dispatch_grads(expert_ids, out_grad, expert_total, owners, local_count)
-    grads_in = lax.all_to_all(
-        sent_grads.reshape(expert_total, -1, LANES), exchange, split_axis=0, concat_axis=0, tiled=True
-    )
-
-    sl = jnp.concatenate([step_size, log_decay], axis=1)
-    joint = jnp.concatenate([conv_weight, bc_conv_weight], axis=1)
-    skip_row = jnp.repeat(skip_gain, head_width)[None, :]
-    y_local, c_rows, e_rows, sent = mixer_local(
-        x_inner, bc_input, rim, joint, sl, sl.T, skip_row, heads, ctx_count
-    )
-    received = lax.all_to_all(sent, ctx, split_axis=0, concat_axis=0, tiled=True)
     scanned = state_scan(received, state_size // ctx_count)
     arriving = lax.all_to_all(scanned, ctx, split_axis=0, concat_axis=0, tiled=True).reshape(state_size, channels)
-    gated = gate_rows(y_local, c_rows, e_rows, arriving, gate_input, heads, x_count, y_count)
+    arriving, grads_in = lax.optimization_barrier((arriving, grads_in))
+    gated = gate_rows(y_local, conv, e_rows, arriving, gate_input, x_count, y_count)
     gated = lax.all_to_all(gated, "y", split_axis=0, concat_axis=0, tiled=True)
     parts = project(gated, [folded, from_prev, from_next, far_a, far_b], where, x_count)
     parts = lax.all_to_all(parts, "x", split_axis=0, concat_axis=0, tiled=True)
     sent_rows, hidden, inv_rms = normalise(
-        parts, residual, moe_gain[None, :], expert_ids, channels * owners, expert_total, owners, local_count
+        parts, residual, moe_gain[None, :], ids_t, channels * owners, expert_total, owners, local_count
     )
     rows_in = lax.all_to_all(
         sent_rows.reshape(expert_total, -1, LANES), exchange, split_axis=0, concat_axis=0, tiled=True
     )
-    outs, grads = experts(
-        rows_in.reshape(-1, LANES), grads_in.reshape(-1, LANES), weights, ff_width, tiles * d_local
-    )
-    outs_back = lax.all_to_all(
-        outs.reshape(expert_total, -1, LANES), exchange, split_axis=0, concat_axis=0, tiled=True
-    )
-    grads_back = lax.all_to_all(
-        grads.reshape(expert_total, -1, LANES), exchange, split_axis=0, concat_axis=0, tiled=True
-    )
-    return combine(
-        outs_back.reshape(-1, LANES),
-        grads_back.reshape(-1, LANES),
-        hidden,
-        inv_rms,
-        out_grad,
-        moe_gain[None, :],
-        expert_ids,
-        route_weights,
-        expert_total,
-        owners,
-        local_count,
-    )
+    back = experts(core, rows_in.reshape(-1, LANES), grads_in.reshape(-1, LANES), weights, ff_width, gu_rows)
+    back = lax.all_to_all(back, exchange, split_axis=0, concat_axis=0, tiled=True)
+    layer, res, route = combine(
+        back, hidden, inv_rms, out_grad, moe_gain[None, :], ids_t, route_t, expert_total, owners, local_count
+    )
+    return layer, res, route.T
 
 
 def solution(mesh):

time: 237 us -> 248 us (1.046)
  blocking collectives: 76 us -> 99.2 us
  waiting for transfers between devices: 57.5 us -> 46.7 us
  Pallas kernels: 43.8 us -> 54.5 us
  local copies, waits for them, and re-layouts: 12.9 us -> 5.18 us
  starting transfers between devices: 29.5 us -> 25.2 us
    ppermute x1, waiting for transfers between devices: 0.01 us -> 29.1 us  [local(): from_prev = lax.ppermute(folded, 'y', ring_route(y_count, 1))]
    all_to_all x2 -> x0, waiting for transfers between devices: 27.7 us -> none  [the longest x1 17 us: local(): lax.all_to_all(grads.reshape(expert_total, -1, LANES), exchange, split_ax...]
    all_to_all x2, blocking collectives: 32.4 us -> 55.3 us  [the longest x1 36.4 us: local(): lax.all_to_all(back, exchange, split_axis=0, concat_axis=0, tiled=True)]
    all_to_all x1, waiting for transfers between devices: 14 us -> 0.01 us  [local(): lax.all_to_all(sent_grads.reshape(expert_total, -1, LANES), exchange, spl...]
    pallas_call x3 -> x5, Pallas kernels: 26.9 us -> 37.1 us  [the longest x1 14.4 us: experts(): pl.pallas_call(kernel, out_shape=jax.ShapeDtypeStruct((dests, 2 * each, L...]
    all_to_all x2 -> x0, starting transfers between devices: 8.72 us -> none  [the longest x1 4.61 us: local(): lax.all_to_all(grads.reshape(expert_total, -1, LANES), exchange, split_ax...]
    unnamed x43 -> x22, local copies, waits for them, and re-layouts: 7.87 us -> 3.64 us
    ppermute x0 -> x1, starting transfers between devices: none -> 3.2 us  [local(): swapped = lax.ppermute(other, 'core', [(0, 1), (1, 0)])]
  transfers between devices with their start and end apart: 11 -> 10, of which waited for: 5 -> 4; matrix products, arithmetic and copies ran while one was open for 3% -> 1% of each run, Pallas kernels for 11% -> 13%
where the time goes in v1:
time: 248 us; the launch traced here: 247 us
  blocking collectives  99.2 us (40%)
  Pallas kernels  54.5 us (22%)
  waiting for transfers between devices  46.7 us (19%)
  starting transfers between devices  25.2 us (10%)
  between operations  14.2 us (6%)
  local copies, waits for them, and re-layouts  5.18 us (2%)
    all_to_all x1, blocking collectives, local(): lax.all_to_all(back, exchange, split_axis=0, concat_axis=0, tiled=True)  36.4 us
    ppermute x1, waiting for transfers between devices, local(): from_prev = lax.ppermute(folded, 'y', ring_route(y_count, 1))  29.1 us
    all_to_all x1, blocking collectives, local(): lax.all_to_all(sent_rows.reshape(expert_total, -1, LANES), exchange, spli...  25.4 us
    all_to_all x1, blocking collectives, local(): parts = lax.all_to_all(parts, 'x', split_axis=0, concat_axis=0, tiled=True)  18.9 us
    all_to_all x1, blocking collectives, local(): lax.all_to_all(sent, ctx, split_axis=0, concat_axis=0, tiled=True)  18.6 us
    pallas_call x1, Pallas kernels, experts(): pl.pallas_call(kernel, out_shape=jax.ShapeDtypeStruct((dests, 2 * each, L...  14.4 us
    all_to_all x1, waiting for transfers between devices, local(): gated = lax.all_to_all(gated, 'y', split_axis=0, concat_axis=0, tiled=True)  8.79 us
    pallas_call x1, Pallas kernels, mixer_state(): call(kernel, (jax.ShapeDtypeStruct((rows, width), BF16), jax.ShapeDtypeSt...  8 us
  transfers between devices with their start and end apart: 10, of which 4 were waited for; matrix products, arithmetic and copies ran while one was open for 1% of the time, Pallas kernels for 13%

profile of v1, /device:TPU:1, one launch (start us, length us, event | category | flops | bytes accessed | tf_op | source)
XLA Modules:
  0.0 247.4 jit_solution(6932335778695721844)
XLA Ops:
  7.2 2.3 shard_map.191
  9.6 3.2 %collective-permute-start.5 = (bf16[2112,128]{1,0:T(8,128)(2,1)}, bf16[2112,128]{1,0:T(8,128)(2,1)S(1)}, u32[]{:S(2)}, u32[]{:S(2)}) collective-permute-start(bf16[2112,128]{1,0:T(8,128)(2,1)} %get-tuple-element.41), channel_id=1, source_target_pairs={{0,16},{16,0},{1,17},{17,1},{2,18},{18,2},{3,19},{19,3},{4,20},{20... | collective-permute-start | bytes 1622024 | tf_op jit(solution)/shard_map/ppermute | solution.py:603
  12.8 1.8 collective-permute-done.5
  14.5 2.2 pad_maximum_fusion
  16.7 2.1 collective-permute-start
  18.8 3.5 %shard_map.184 = bf16[4608,128]{1,0:T(8,128)(2,1)} custom-call(s32[4,64]{1,0:T(4,128)} %bitcast.32, bf16[64,2048]{1,0:T(8,128)(2,1)} %g_ref.7), custom_call_target="tpu_custom_call" | custom-call | tf_op jit(solution)/shard_map/pallas_call | solution.py:360
  22.9 8.0 %shard_map.185 = (bf16[1024,512]{1,0:T(8,128)(2,1)}, bf16[1024,256]{1,0:T(8,128)(2,1)}, bf16[16,16,256]{2,1,0:T(8,128)(2,1)}) custom-call(bf16[1024,256]{1,0:T(8,128)(2,1)} %x_ref.1, bf16[1024,256]{1,0:T(8,128)(2,1)} %bc_ref.1, bf16[8,512]{1,0:T(8,128)(2,1)} %copy-done.9, f32[4,256]{1,0:T(4,128)} %wx_ref.1, f32[4,256]{1,0:T(4,128)} %wb_ref.1, ...), custom_call_target="tpu_custom_call" | custom-call | tf_op jit(solution)/shard_map/pallas_call | solution.py:119
  30.9 18.6 %all_to_all.35.r_ref = bf16[16,16,256]{2,1,0:T(8,128)(2,1)} all-to-all(bf16[16,16,256]{2,1,0:T(8,128)(2,1)} %get-tuple-element.26), channel_id=1, replica_groups=mesh['z'=8,'core'=2,'x'=4,'y'=4] {'z','core'}, dimensions={0} | all-to-all | bytes 262144 | tf_op jit(solution)/shard_map/all_to_all | solution.py:613
  49.5 7.3 %all-to-all-start.2 = ((bf16[32,144,128]{2,1,0:T(8,128)(2,1)}), bf16[32,144,128]{2,1,0:T(8,128)(2,1)S(1)}, u32[]{:S(2)}, u32[]{:S(2)}) async-start(bf16[32,144,128]{2,1,0:T(8,128)(2,1)} %bitcast.9), calls=%async_computation.2 | async-start | bytes 2359296 | tf_op jit(solution)/shard_map/all_to_all | solution.py:614
  59.8 6.5 %shard_map.186 = (f32[1024,256]{1,0:T(8,128)}, f32[1024,4]{1,0:T(8,128)}) custom-call(f32[4]{0:T(128)} %skip_ref.1, bf16[1024,512]{1,0:T(8,128)(2,1)} %get-tuple-element.28.conv_ref.c_ref, bf16[1024,256]{1,0:T(8,128)(2,1)} %get-tuple-element.29.in_ref, f32[4,1024]{1,0:T(4,128)} %bitcast.27, f32[4,1024]{1,0:T(4,128)} %bitcast.29), custom_call_target="tpu_custom_call" | custom-call | tf_op jit(solution)/shard_map/pallas_call | solution.py:191
  66.3 29.1 %collective-permute-done.1.refs_1_ = bf16[256,2048]{1,0:T(8,128)(2,1)S(1)} collective-permute-done((bf16[256,2048]{1,0:T(8,128)(2,1)S(1)}, bf16[256,2048]{1,0:T(8,128)(2,1)S(1)}, u32[]{:S(2)}, u32[]{:S(2)}) %collective-permute-start.1) | collective-permute-done | bytes 1048608 | tf_op jit(solution)/shard_map/ppermute | solution.py:621
  98.0 4.2 %all-to-all-start.1 = ((f32[16,8,256]{2,1,0:T(8,128)}), f32[16,8,256]{2,1,0:T(8,128)S(1)}, u32[]{:S(2)}, u32[]{:S(2)}) async-start(f32[16,8,256]{2,1,0:T(8,128)} %shard_map.187), calls=%async_computation.1 | async-start | bytes 262144 | tf_op jit(solution)/shard_map/all_to_all | solution.py:631
  103.6 2.2 collective-permute-start.4
  105.8 7.1 %all-to-all-done.1 = f32[16,8,256]{2,1,0:T(8,128)S(1)} async-done(((f32[16,8,256]{2,1,0:T(8,128)}), f32[16,8,256]{2,1,0:T(8,128)S(1)}, u32[]{:S(2)}, u32[]{:S(2)}) %all-to-all-start.1) | async-done | bytes 131104 | tf_op jit(solution)/shard_map/all_to_all | solution.py:631
  113.6 3.4 %shard_map.188 = bf16[4,256,256]{2,1,0:T(8,128)(2,1)} custom-call(f32[1024,256]{1,0:T(8,128)} %get-tuple-element.31.y_ref, bf16[1024,512]{1,0:T(8,128)(2,1)} %get-tuple-element.28.conv_ref.c_ref, f32[1024,4]{1,0:T(8,128)} %get-tuple-element.32.e_ref, f32[128,256]{1,0:T(8,128)} %bitcast.25, bf16[1024,256]{1,0:T(8,128)(2,1)} %g_ref.5), custom_call_target="tpu_custom_call" | custom-call | tf_op jit(solution)/shard_map/pallas_call | solution.py:237
  117.0 3.5 %all-to-all-start.3 = ((bf16[4,256,256]{2,1,0:T(8,128)(2,1)}), bf16[4,256,256]{2,1,0:T(8,128)(2,1)S(1)}, u32[]{:S(2)}, u32[]{:S(2)}) async-start(bf16[4,256,256]{2,1,0:T(8,128)(2,1)} %shard_map.188), calls=%async_computation.3 | async-start | bytes 1048576 | tf_op jit(solution)/shard_map/all_to_all | solution.py:634
  121.2 8.8 %all-to-all-done.3.g_ref = bf16[4,256,256]{2,1,0:T(8,128)(2,1)S(1)} async-done(((bf16[4,256,256]{2,1,0:T(8,128)(2,1)}), bf16[4,256,256]{2,1,0:T(8,128)(2,1)S(1)}, u32[]{:S(2)}, u32[]{:S(2)}) %all-to-all-start.3) | async-done | bytes 524320 | tf_op jit(solution)/shard_map/all_to_all | solution.py:634
  130.7 4.9 %shard_map.189 = bf16[4,64,2176]{2,1,0:T(8,128)(2,1)} custom-call(s32[5]{0:T(128)} %stack.29.where_ref, bf16[4,256,256]{2,1,0:T(8,128)(2,1)} %copy-done.5, bf16[256,2048]{1,0:T(8,128)(2,1)} %copy-done.1, bf16[256,2048]{1,0:T(8,128)(2,1)} %copy-done.2, bf16[256,2048]{1,0:T(8,128)(2,1)} %copy-done.3, bf16[128,2048]{1,0:T(8,128)(2,1)} %collective-permute-done.3.refs_3_, ...), custom_call_target="tpu_custom_call" | custom-call | tf_op jit(solution)/shard_map/pallas_call | solution.py:271
  135.6 18.9 %all_to_all.36.p_ref = bf16[4,64,2176]{2,1,0:T(8,128)(2,1)} all-to-all(bf16[4,64,2176]{2,1,0:T(8,128)(2,1)} %shard_map.189), channel_id=1, replica_groups=mesh['z'=8,'core'=2,'x'=4,'y'=4] {'x'}, dimensions={0} | all-to-all | bytes 2228224 | tf_op jit(solution)/shard_map/all_to_all | solution.py:636
  154.5 4.0 %shard_map.190 = (bf16[4608,128]{1,0:T(8,128)(2,1)}, bf16[64,2048]{1,0:T(8,128)(2,1)}, f32[64,128]{1,0:T(8,128)}) custom-call(bf16[4,64,2176]{2,1,0:T(8,128)(2,1)} %all_to_all.36.p_ref, bf16[64,2048]{1,0:T(8,128)(2,1)} %r_ref.1, f32[1,2048]{1,0:T(1,128)} %bitcast.30, s32[4,64]{1,0:T(4,128)} %bitcast.33), custom_call_target="tpu_custom_call" | custom-call | tf_op jit(solution)/shard_map/pallas_call | solution.py:389
  158.5 25.4 %all_to_all.37 = bf16[32,144,128]{2,1,0:T(8,128)(2,1)} all-to-all(bf16[32,144,128]{2,1,0:T(8,128)(2,1)} %bitcast.22), channel_id=1, replica_groups=mesh['z'=8,'core'=2,'x'=4,'y'=4] {'core','x','y'}, dimensions={0} | all-to-all | bytes 2359296 | tf_op jit(solution)/shard_map/all_to_all | solution.py:640
  183.9 14.4 %shard_map.192 = bf16[32,288,128]{2,1,0:T(8,128)(2,1)} custom-call(s32[1]{0:T(128)} %bitcast.core_ref, bf16[4608,128]{1,0:T(8,128)(2,1)} %bitcast.21, bf16[4608,128]{1,0:T(8,128)(2,1)} %bitcast.20, bf16[8,2,2112,128]{3,2,1,0:T(8,128)(2,1)} %bitcast.19), custom_call_target="tpu_custom_call" | custom-call | tf_op jit(solution)/shard_map/pallas_call | solution.py:489
  198.4 36.4 %all_to_all.38.r_ref = bf16[32,288,128]{2,1,0:T(8,128)(2,1)} all-to-all(bf16[32,288,128]{2,1,0:T(8,128)(2,1)} %shard_map.192), channel_id=1, replica_groups=mesh['z'=8,'core'=2,'x'=4,'y'=4] {'core','x','y'}, dimensions={0} | all-to-all | bytes 4718592 | tf_op jit(solution)/shard_map/all_to_all | solution.py:644
  234.7 5.9 %shard_map.193 = (bf16[64,2048]{1,0:T(8,128)(2,1)}, bf16[64,2048]{1,0:T(8,128)(2,1)}, f32[4,64]{1,0:T(4,128)}) custom-call(bf16[32,288,128]{2,1,0:T(8,128)(2,1)} %all_to_all.38.r_ref, bf16[64,2048]{1,0:T(8,128)(2,1)} %get-tuple-element.42.h_ref, f32[64,128]{1,0:T(8,128)} %get-tuple-element.43.v_ref, bf16[64,2048]{1,0:T(8,128)(2,1)} %g_ref.7, ...), custom_call_target="tpu_custom_call" | custom-call | tf_op jit(solution)/shard_map/pallas_call | solution.py:551
  (43 shorter events, 9.9 us)
Async XLA Ops:
  7.2 176.8 %all-gather.3.cloned.1.call-start = ((), (), s32[]{:S(2)}) async-start(), calls=%async_computation.7 | async-start | bytes 9732096 | tf_op jit(solution)/shard_map/all_gather | solution.py:604
  9.6 5.0 %collective-permute-start.5 = (bf16[2112,128]{1,0:T(8,128)(2,1)}, bf16[2112,128]{1,0:T(8,128)(2,1)S(1)}, u32[]{:S(2)}, u32[]{:S(2)}) collective-permute-start(bf16[2112,128]{1,0:T(8,128)(2,1)} %get-tuple-element.41), channel_id=1, source_target_pairs={{0,16},{16,0},{1,17},{17,1},{2,18},{18,2},{3,19},{19,3},{4,20},{20... | collective-permute-start | bytes 1622024 | tf_op jit(solution)/shard_map/ppermute | solution.py:603
  14.5 2.2 slice-start
  14.5 2.2 slice-start.1
  16.7 5.6 %collective-permute-start = (bf16[8,512]{1,0:T(8,128)(2,1)S(1)}, bf16[8,512]{1,0:T(8,128)(2,1)S(1)}, u32[]{:S(2)}, u32[]{:S(2)}) collective-permute-start(bf16[8,512]{1,0:T(8,128)(2,1)S(1)} %pad_maximum_fusion.1), channel_id=1, source_target_pairs={{0,16},{16,32},{32,48},{48,64},{64,80},{80,96},{96,112},{112,128},... | collective-permute-start | bytes 24584 | tf_op jit(solution)/shard_map/ppermute | solution.py:600
  22.3 0.6 copy-start.9
  49.5 7.3 %copy-start.6 = (bf16[256,2048]{1,0:T(8,128)(2,1)S(1)}, bf16[256,2048]{1,0:T(8,128)(2,1)}, u32[]{:S(2)}) copy-start(bf16[256,2048]{1,0:T(8,128)(2,1)} %param.26) | copy-start | bytes 3145732
  49.5 7.4 %copy-start.10 = (f32[256]{0:T(256)S(1)}, f32[256]{0:T(256)}, u32[]{:S(2)}) copy-start(f32[256]{0:T(256)} %param.25) | copy-start | bytes 3076
  49.5 48.5 %all-to-all-start.2 = ((bf16[32,144,128]{2,1,0:T(8,128)(2,1)}), bf16[32,144,128]{2,1,0:T(8,128)(2,1)S(1)}, u32[]{:S(2)}, u32[]{:S(2)}) async-start(bf16[32,144,128]{2,1,0:T(8,128)(2,1)} %bitcast.9), calls=%async_computation.2 | async-start | bytes 2359296 | tf_op jit(solution)/shard_map/all_to_all | solution.py:614
  57.1 45.9 %copy-start.1 = (bf16[256,2048]{1,0:T(8,128)(2,1)}, bf16[256,2048]{1,0:T(8,128)(2,1)S(1)}, u32[]{:S(2)}) copy-start(bf16[256,2048]{1,0:T(8,128)(2,1)S(1)} %multiply_convert_fusion.refs_0_) | copy-start | bytes 3145732
  57.1 38.3 %collective-permute-start.1 = (bf16[256,2048]{1,0:T(8,128)(2,1)S(1)}, bf16[256,2048]{1,0:T(8,128)(2,1)S(1)}, u32[]{:S(2)}, u32[]{:S(2)}) collective-permute-start(bf16[256,2048]{1,0:T(8,128)(2,1)S(1)} %multiply_convert_fusion.refs_0_), channel_id=1, source_target_pairs={{0,1},{1,2},{2,3},{3,0},{4,5},{5,6},{6,7},{7,4},{8,9},{9,10},{10,1... | collective-permute-start | bytes 3145736 | tf_op jit(solution)/shard_map/ppermute | solution.py:621
  58.5 36.9 %collective-permute-start.2 = (bf16[256,2048]{1,0:T(8,128)(2,1)S(1)}, bf16[256,2048]{1,0:T(8,128)(2,1)S(1)}, u32[]{:S(2)}, u32[]{:S(2)}) collective-permute-start(bf16[256,2048]{1,0:T(8,128)(2,1)S(1)} %multiply_convert_fusion.refs_0_), channel_id=1, source_target_pairs={{0,3},{1,0},{2,1},{3,2},{4,7},{5,4},{6,5},{7,6},{8,11},{9,8},{10,9... | collective-permute-start | bytes 3145736 | tf_op jit(solution)/shard_map/ppermute | solution.py:622
  95.4 8.3 %copy-start.2 = (bf16[256,2048]{1,0:T(8,128)(2,1)}, bf16[256,2048]{1,0:T(8,128)(2,1)S(1)}, u32[]{:S(2)}) copy-start(bf16[256,2048]{1,0:T(8,128)(2,1)S(1)} %collective-permute-done.1.refs_1_) | copy-start | bytes 3145732
  95.4 1.0 copy-start.3
  98.0 14.9 %copy-start = (bf16[32,144,128]{2,1,0:T(8,128)(2,1)}, bf16[32,144,128]{2,1,0:T(8,128)(2,1)S(1)}, u32[]{:S(2)}) copy-start(bf16[32,144,128]{2,1,0:T(8,128)(2,1)S(1)} %all-to-all-done.2) | copy-start | bytes 3538948
  98.0 14.9 %all-to-all-start.1 = ((f32[16,8,256]{2,1,0:T(8,128)}), f32[16,8,256]{2,1,0:T(8,128)S(1)}, u32[]{:S(2)}, u32[]{:S(2)}) async-start(f32[16,8,256]{2,1,0:T(8,128)} %shard_map.187), calls=%async_computation.1 | async-start | bytes 262144 | tf_op jit(solution)/shard_map/all_to_all | solution.py:631
  102.2 1.4 copy-start.4
  103.0 18.1 %collective-permute-start.3 = (bf16[128,2048]{1,0:T(8,128)(2,1)}, bf16[128,2048]{1,0:T(8,128)(2,1)}, u32[]{:S(2)}, u32[]{:S(2)}) collective-permute-start(bf16[128,2048]{1,0:T(8,128)(2,1)} %slice.14), channel_id=1, source_target_pairs={{0,1},{1,2},{2,3},{3,0},{4,5},{5,6},{6,7},{7,4},{8,9},{9,10},{10,1... | collective-permute-start | bytes 1572872 | tf_op jit(solution)/shard_map/ppermute | solution.py:625
  103.6 17.5 %collective-permute-start.4 = (bf16[128,2048]{1,0:T(8,128)(2,1)S(1)}, bf16[128,2048]{1,0:T(8,128)(2,1)S(1)}, u32[]{:S(2)}, u32[]{:S(2)}) collective-permute-start(bf16[128,2048]{1,0:T(8,128)(2,1)S(1)} %slice.15), channel_id=1, source_target_pairs={{0,3},{1,0},{2,1},{3,2},{4,7},{5,4},{6,5},{7,6},{8,11},{9,8},{10,9... | collective-permute-start | bytes 1572872 | tf_op jit(solution)/shard_map/ppermute | solution.py:626
  112.9 0.7 copy-start.8
  117.0 13.0 %all-to-all-start.3 = ((bf16[4,256,256]{2,1,0:T(8,128)(2,1)}), bf16[4,256,256]{2,1,0:T(8,128)(2,1)S(1)}, u32[]{:S(2)}, u32[]{:S(2)}) async-start(bf16[4,256,256]{2,1,0:T(8,128)(2,1)} %shard_map.188), calls=%async_computation.3 | async-start | bytes 1048576 | tf_op jit(solution)/shard_map/all_to_all | solution.py:634
  121.1 8.8 %copy-start.7 = (bf16[128,2048]{1,0:T(8,128)(2,1)}, bf16[128,2048]{1,0:T(8,128)(2,1)S(1)}, u32[]{:S(2)}) copy-start(bf16[128,2048]{1,0:T(8,128)(2,1)S(1)} %collective-permute-done.4.refs_4_) | copy-start | bytes 1572868
  129.9 0.8 copy-start.5
Sparse Core Ops, SparseCore 0:
  16.8 103.0 all-gather.2

commit v2 on v1

--- a/solution.py
+++ b/solution.py
@@ -5,6 +5,7 @@
 from jax.experimental.pallas import tpu as pltpu
 from jax.sharding import Mesh
 from jax.sharding import PartitionSpec as P
+
 
 F32 = jnp.float32
 BF16 = jnp.bfloat16
@@ -56,78 +57,75 @@
     return mm(eye, transposed, NT, HIGH)
 
 
-def mixer_state(x_inner, bc_input, rim, conv_weight, bc_weight, step_t, decay_t, ctx_count):
+def stack_blocks(values, blocks):
+    return jnp.concatenate([values[:, j * SPAN : (j + 1) * SPAN] for j in range(blocks)], axis=0)
+
+
+def three_rows(total, rows):
+    hi = total.astype(BF16).astype(F32)
+    mid = (total - hi).astype(BF16).astype(F32)
+    low = total - hi - mid
+    pick = lax.broadcasted_iota(jnp.int32, (rows, total.shape[1]), 0)
+    return jnp.where(pick == 0, hi, jnp.where(pick == 1, mid, jnp.where(pick == 2, low, 0.0)))
+
+
+def mixer_state(x_inner, bc_input, rim, conv_weight, bc_weight, step_t, decay_t):
     rows, channels = x_inner.shape
     heads = step_t.shape[0]
     state_size = bc_input.shape[1] // 2
     width = channels + 2 * state_size
     head_width = channels // heads
     blocks = rows // SPAN
-    chunk = state_size // ctx_count
     kernel_len = conv_weight.shape[0]
 
-    def kernel(x_ref, bc_ref, rim_ref, wx_ref, wb_ref, step_ref, ld_ref, conv_ref, in_ref, send_ref, pad_ref, held_ref, tot_ref):
+    def kernel(x_ref, bc_ref, rim_ref, wx_ref, wb_ref, step_ref, ld_ref, conv_ref, in_ref, send_ref, pad_ref):
         row_i = lax.broadcasted_iota(jnp.int32, (SPAN, SPAN), 0)
         col_i = lax.broadcasted_iota(jnp.int32, (SPAN, SPAN), 1)
         later = jnp.where(row_i < col_i, 1.0, 0.0).astype(F32)
         eye = jnp.where(row_i == col_i, 1.0, 0.0).astype(F32)
-        ones = jnp.ones((SPAN, SPAN), F32)
+        ones = jnp.ones((8, SPAN), F32)
+        ld = stack_blocks(ld_ref[...], blocks)
+        left = jnp.exp(jnp.minimum(mm(later, ld, NT, HIGH), 0.0))
+        tails = left * columns_of(stack_blocks(step_ref[...], blocks), eye)
+        lasts = mm(ones, ld, NT, HIGH)
+        decays = jnp.exp(jnp.minimum(lasts, 0.0))
         weight = jnp.concatenate([wx_ref[...], wb_ref[...]], axis=1)
+        held = None
+        total = None
         pad_ref[0:8, :] = rim_ref[...].astype(F32)
-        held_ref[...] = jnp.zeros_like(held_ref)
-        tot_ref[...] = jnp.zeros_like(tot_ref)
-
-        def block(j, carry):
-            at = pl.multiple_of(j * SPAN, SPAN)
-            pad_ref[8:, :channels] = x_ref[pl.ds(at, SPAN), :].astype(F32)
-            pad_ref[8:, channels:] = bc_ref[pl.ds(at, SPAN), :].astype(F32)
-            summed = jnp.zeros((SPAN, width), F32)
+        for j in range(blocks):
+            at = j * SPAN
+            pad_ref[8 + at : 8 + at + SPAN, :channels] = x_ref[at : at + SPAN, :].astype(F32)
+            pad_ref[8 + at : 8 + at + SPAN, channels:] = bc_ref[at : at + SPAN, :].astype(F32)
+            summed = None
             for k in range(kernel_len):
-                begin = 8 - kernel_len + 1 + k
-                summed = summed + weight[k : k + 1, :] * pad_ref[begin : begin + SPAN, :]
-            tail_rows = pad_ref[SPAN : SPAN + 8, :]
-            pad_ref[0:8, :] = tail_rows
+                begin = at + 8 - kernel_len + 1 + k
+                term = weight[k : k + 1, :] * pad_ref[begin : begin + SPAN, :]
+                summed = term if summed is None else summed + term
             conv = silu(summed).astype(BF16)
-            conv_ref[pl.ds(at, SPAN), :] = conv
-            x_f = conv[:, :channels].astype(F32)
-            b_b = conv[:, channels : channels + state_size]
-            ld_b = ld_ref[:, pl.ds(at, SPAN)]
-            left = mm(later, ld_b, NT, HIGH)
-            step = columns_of(step_ref[:, pl.ds(at, SPAN)], eye)
-            tail = spread(jnp.exp(jnp.minimum(left, 0.0)) * step, 0, heads, head_width)
-            x_t = (x_f * tail).astype(BF16)
-            last = mm(ones, ld_b, NT, HIGH)
-            decay = spread(jnp.exp(jnp.minimum(last, 0.0)), 0, heads, head_width)
-            held = held_ref[...]
-            in_ref[pl.ds(at, SPAN), :] = held.astype(BF16)
-            held_ref[...] = decay * held + mm(b_b, x_t, TN)
-            tot_ref[...] = tot_ref[...] + last[0:8, :]
-            return carry
-
-        lax.fori_loop(0, blocks, block, 0)
-        held = held_ref[...]
-        total = spread(tot_ref[...], 0, heads, head_width)[0:1, :]
-        hi = total.astype(BF16).astype(F32)
-        mid = (total - hi).astype(BF16).astype(F32)
-        low = total - hi - mid
-        pick = lax.broadcasted_iota(jnp.int32, (8, channels), 0)
-        extra = jnp.where(pick == 0, hi, jnp.where(pick == 1, mid, jnp.where(pick == 2, low, 0.0)))
-        for d in range(ctx_count):
-            part = jnp.concatenate([held[d * chunk : (d + 1) * chunk], extra], axis=0)
-            send_ref[d] = part.astype(BF16)
+            conv_ref[at : at + SPAN, :] = conv
+            x_t = (conv[:, :channels].astype(F32) * spread(tails, j * heads, heads, head_width)).astype(BF16)
+            state = mm(conv[:, channels : channels + state_size], x_t, TN)
+            if j == 0:
+                in_ref[at : at + SPAN, :] = jnp.zeros((state_size, channels), BF16)
+                held = state
+                total = lasts[:, :heads]
+            else:
+                in_ref[at : at + SPAN, :] = held.astype(BF16)
+                held = spread(decays, j * heads, heads, head_width)[0:1, :] * held + state
+                total = total + lasts[:, j * heads : (j + 1) * heads]
+        send_ref[:state_size, :] = held.astype(BF16)
+        extra = three_rows(spread(total, 0, heads, head_width)[0:1, :], 16)
+        send_ref[state_size:, :] = extra.astype(BF16)
 
     return call(
         kernel,
         (
             jax.ShapeDtypeStruct((rows, width), BF16),
             jax.ShapeDtypeStruct((blocks * state_size, channels), BF16),
-            jax.ShapeDtypeStruct((ctx_count, chunk + 8, channels), BF16),
+            jax.ShapeDtypeStruct((state_size + 16, channels), BF16),
         ),
-        (
-            pltpu.VMEM((SPAN + 8, width), F32),
-            pltpu.VMEM((state_size, channels), F32),
-            pltpu.VMEM((8, heads), F32),
-        ),
+        (pltpu.VMEM((rows + 8, width), F32),),
     )(x_inner, bc_input, rim, conv_weight, bc_weight, step_t, decay_t)
 
 
@@ -138,7 +136,7 @@
     head_width = channels // heads
     blocks = rows // SPAN
 
-    def kernel(skip_ref, conv_ref, in_ref, step_ref, ld_ref, y_ref, e_ref, tot_ref):
+    def kernel(skip_ref, conv_ref, in_ref, step_ref, ld_ref, y_ref, e_ref):
         row_i = lax.broadcasted_iota(jnp.int32, (SPAN, SPAN), 0)
         col_i = lax.broadcasted_iota(jnp.int32, (SPAN, SPAN), 1)
         causal = row_i >= col_i
@@ -154,17 +152,24 @@
                 out = jnp.where(lane_row < i * head_width, out, skip_ref[group * per + i])
             skip.append(out)
         skip = jnp.concatenate(skip, axis=1)
-        tot_ref[...] = jnp.zeros_like(tot_ref)
-
-        def block(j, carry):
-            at = pl.multiple_of(j * SPAN, SPAN)
-            x_b = conv_ref[pl.ds(at, SPAN), :channels]
-            b_b = conv_ref[pl.ds(at, SPAN), channels : channels + state_size]
-            c_b = conv_ref[pl.ds(at, SPAN), channels + state_size :]
-            ld_b = ld_ref[:, pl.ds(at, SPAN)]
-            step_b = step_ref[:, pl.ds(at, SPAN)]
-            cum = mm(lower, ld_b, NT, HIGH)
-            cum_t = mm(ld_b, upper, NN, HIGH)
+        ld = stack_blocks(ld_ref[...], blocks)
+        ld = jnp.concatenate([ld, jnp.zeros((SPAN - blocks * heads, SPAN), F32)], axis=0)
+        cum = mm(lower, ld, NT, HIGH)
+        cum_t = mm(ld, upper, NN, HIGH)
+        group_lane = lax.broadcasted_iota(jnp.int32, (SPAN, SPAN), 1)
+        earlier = jnp.zeros((SPAN, SPAN), F32)
+        total = jnp.zeros((1, heads), F32)
+        for j in range(blocks):
+            for h in range(heads):
+                earlier = jnp.where(group_lane == j * heads + h, total[:, h : h + 1], earlier)
+            total = total + cum[SPAN - 1 : SPAN, j * heads : (j + 1) * heads]
+        e_ref[...] = jnp.exp(jnp.minimum(earlier + cum, 0.0))
+        e_cum = jnp.exp(jnp.minimum(cum, 0.0))
+        for j in range(blocks):
+            at = j * SPAN
+            x_b = conv_ref[at : at + SPAN, :channels]
+            b_b = conv_ref[at : at + SPAN, channels : channels + state_size]
+            c_b = conv_ref[at : at + SPAN, channels + state_size :]
             scores = mm(c_b, b_b, NT)
             within = []
             for group in range(channels // LANES):
@@ -172,109 +177,130 @@
                 out = None
                 for i in range(per):
                     h = group * per + i
-                    gap = cum[:, h : h + 1] - cum_t[h : h + 1, :]
-                    w = jnp.exp(jnp.where(causal, gap, -1e30)) * scores * step_b[h : h + 1, :]
+                    r = j * heads + h
+                    gap = cum[:, r : r + 1] - cum_t[r : r + 1, :]
+                    w = jnp.exp(jnp.where(causal, gap, -1e30)) * scores * step_ref[h : h + 1, at : at + SPAN]
                     y_h = mm(w.astype(BF16), x_g, NN)
                     out = y_h if out is None else jnp.where(lane < i * head_width, out, y_h)
                 within.append(out)
             within = jnp.concatenate(within, axis=1)
-            carried = mm(c_b, in_ref[pl.ds(at, SPAN), :], NN) * spread(jnp.exp(cum), 0, heads, head_width)
-            y_ref[pl.ds(at, SPAN), :] = within + carried + skip * x_b.astype(F32)
-            tot = tot_ref[0:1, :]
-            e_ref[pl.ds(at, SPAN), :] = jnp.exp(jnp.minimum(tot + cum, 0.0))
-            tot_ref[...] = tot_ref[...] + cum[SPAN - 1 : SPAN, :]
-            return carry
-
-        lax.fori_loop(0, blocks, block, 0)
+            y = within + skip * x_b.astype(F32)
+            if j > 0:
+                y = y + mm(c_b, in_ref[at : at + SPAN, :], NN) * spread(e_cum, j * heads, heads, head_width)
+            y_ref[at : at + SPAN, :] = y
 
     vmem = pl.BlockSpec(memory_space=pltpu.VMEM)
     return pl.pallas_call(
         kernel,
         out_shape=(
             jax.ShapeDtypeStruct((rows, channels), F32),
-            jax.ShapeDtypeStruct((rows, heads), F32),
+            jax.ShapeDtypeStruct((SPAN, SPAN), F32),
         ),
         in_specs=[pl.BlockSpec(memory_space=pltpu.SMEM)] + [vmem] * 4,
         out_specs=(vmem, vmem),
-        scratch_shapes=[pltpu.VMEM((8, heads), F32)],
         compiler_params=pltpu.CompilerParams(vmem_limit_bytes=58 << 20),
     )(skip_gain, conv, entering, step_t, decay_t)
 
 
-def state_scan(received, chunk):
-    count, _, channels = received.shape
-
-    def kernel(r_ref, o_ref):
-        arriving = jnp.zeros((chunk, channels), F32)
-        for s in range(count):
-            part = r_ref[s].astype(F32)
-            o_ref[s] = arriving
-            total = part[chunk : chunk + 1] + part[chunk + 1 : chunk + 2] + part[chunk + 2 : chunk + 3]
-            arriving = jnp.exp(jnp.minimum(total, 0.0)) * arriving + part[:chunk]
-
-    return call(kernel, jax.ShapeDtypeStruct((count, chunk, channels), F32))(received)
-
-
-def gate_rows(y_local, conv, e_rows, arriving, gate_input, x_count, y_count):
+def total_of(ref, state_size):
+    rows = ref[state_size:, :].astype(F32)
+    return rows[0:1] + rows[1:2] + rows[2:3]
+
+
+def join_states(parts, state_size, last):
+    channels = parts[0].shape[1]
+
+    def kernel(*refs):
+        ins, o_ref = refs[:-1], refs[-1]
+        out = ins[0][:state_size, :].astype(F32)
+        total = total_of(ins[0], state_size)
+        for ref in ins[1:]:
+            out = out + jnp.exp(jnp.minimum(total, 0.0)) * ref[:state_size, :].astype(F32)
+            total = total + total_of(ref, state_size)
+        o_ref[:state_size, :] = out.astype(BF16)
+        if not last:
+            o_ref[state_size:, :] = three_rows(total, 16).astype(BF16)
+
+    height = state_size if last else state_size + 16
+    return call(kernel, jax.ShapeDtypeStruct((height, channels), BF16))(*parts)
+
+
+def gate_rows(y_at, y_local, conv, e_cols, arriving, gate_input, heads, x_count, y_count):
     rows, channels = y_local.shape
-    heads = e_rows.shape[1]
+    blocks = rows // SPAN
+    head_width = channels // heads
     state_size = arriving.shape[0]
-    head_width = channels // heads
     own = rows // (x_count * y_count)
 
-    def kernel(y_ref, c_ref, e_ref, a_ref, g_ref, o_ref):
-        state = a_ref[...].astype(BF16)
-        for x in range(x_count):
-            at = x * y_count * own
-            size = y_count * own
-            carried = mm(c_ref[at : at + size, channels + state_size :], state, NN) * spread(
-                e_ref[at : at + size, :], 0, heads, head_width
+    def kernel(at_ref, y_ref, c_ref, e_ref, a_ref, g_ref, *refs):
+        outs, s_ref = refs[:-1], refs[-1]
+        state = a_ref[...]
+        for j in range(blocks):
+            at = j * SPAN
+            carried = mm(c_ref[at : at + SPAN, channels + state_size :], state, NN) * spread(
+                e_ref[...], j * heads, heads, head_width
             )
-            gated = (y_ref[at : at + size, :] + carried) * silu(g_ref[at : at + size, :].astype(F32))
-            for y in range(y_count):
-                o_ref[y, x * own : (x + 1) * own, :] = gated[y * own : (y + 1) * own].astype(BF16)
-
-    return call(kernel, jax.ShapeDtypeStruct((y_count, x_count * own, channels), BF16))(
-        y_local, conv, e_rows, arriving, gate_input
-    )
-
-
-def project(gated, pieces, where, x_count):
-    y_count, rows, channels = gated.shape
-    out_width = pieces[0].shape[1]
+            gated = (y_ref[at : at + SPAN, :] + carried) * silu(g_ref[at : at + SPAN, :].astype(F32))
+            s_ref[at : at + SPAN, :] = gated.astype(BF16)
+        for k in range(y_count):
+            y = lax.rem(at_ref[0] + k, y_count)
+            for x in range(x_count):
+                first = pl.multiple_of((x * y_count + y) * own, own)
+                outs[k][x * own : (x + 1) * own, :] = s_ref[pl.ds(first, own), :]
+
+    vmem = pl.BlockSpec(memory_space=pltpu.VMEM)
+    shape = jax.ShapeDtypeStruct((x_count * own, channels), BF16)
+    return pl.pallas_call(
+        kernel,
+        out_shape=(shape,) * y_count,
+        in_specs=[pl.BlockSpec(memory_space=pltpu.SMEM)] + [vmem] * 5,
+        out_specs=(vmem,) * y_count,
+        scratch_shapes=[pltpu.VMEM((rows, channels), BF16)],
+        compiler_params=pltpu.CompilerParams(vmem_limit_bytes=58 << 20),
+    )(y_at, y_local, conv, e_cols, arriving, gate_input)
+
+
+def project(x_at, gated, weights, x_count):
+    rows, _ = gated[0].shape
+    out_width = weights[0][0].shape[1]
     own = rows // x_count
-
-    def kernel(where_ref, g_ref, *refs):
-        o_ref = refs[-1]
-        w_refs = refs[:-1]
-        total = jnp.zeros((rows, out_width), F32)
-        first = 0
+    count = len(gated)
+    sizes = [len(w) for w in weights]
+
+    def kernel(at_ref, *refs):
+        g_refs = refs[:count]
+        w_refs = refs[count : count + sum(sizes)]
+        outs, s_ref = refs[count + sum(sizes) : -1], refs[-1]
         squares = jnp.zeros((rows, 1), F32)
-        for y in range(y_count):
-            part = g_ref[y].astype(F32)
+        for g_ref in g_refs:
+            part = g_ref[...].astype(F32)
             squares = squares + jnp.sum(part * part, axis=1, keepdims=True)
-        for i, w_ref in enumerate(w_refs):
-            size = w_ref.shape[0]
-            lhs = g_ref[where_ref[i]]
-            total = total + mm(lhs[:, first : first + size], w_ref[...], NN)
-            first = (first + size) % channels
+        lhs = jnp.concatenate([g_ref[...] for g_ref in g_refs], axis=1)
+        size = 512
+        for first in range(0, out_width, size):
+            rhs = jnp.concatenate([w_ref[:, first : first + size] for w_ref in w_refs], axis=0)
+            s_ref[:, first : first + size] = mm(lhs, rhs, NN).astype(BF16)
         hi = squares.astype(BF16).astype(F32)
         mid = (squares - hi).astype(BF16).astype(F32)
         low = squares - hi - mid
         lane = lax.broadcasted_iota(jnp.int32, (rows, LANES), 1)
         extra = jnp.where(lane == 0, hi, jnp.where(lane == 1, mid, jnp.where(lane == 2, low, 0.0)))
-        for x in range(x_count):
-            o_ref[x, :, :out_width] = total[x * own : (x + 1) * own].astype(BF16)
-            o_ref[x, :, out_width:] = extra[x * own : (x + 1) * own].astype(BF16)
-
+        s_ref[:, out_width:] = extra.astype(BF16)
+        for k in range(x_count):
+            first = pl.multiple_of(lax.rem(at_ref[0] + k, x_count) * own, own)
+            outs[k][...] = s_ref[pl.ds(first, own), :]
+
+    flat = [w for group in weights for w in group]
     vmem = pl.BlockSpec(memory_space=pltpu.VMEM)
+    shape = jax.ShapeDtypeStruct((own, out_width + LANES), BF16)
     return pl.pallas_call(
         kernel,
-        out_shape=jax.ShapeDtypeStruct((x_count, own, out_width + LANES), BF16),
-        in_specs=[pl.BlockSpec(memory_space=pltpu.SMEM), vmem] + [vmem] * len(pieces),
-        out_specs=vmem,
+        out_shape=(shape,) * x_count,
+        in_specs=[pl.BlockSpec(memory_space=pltpu.SMEM)] + [vmem] * (count + len(flat)),
+        out_specs=(vmem,) * x_count,
+        scratch_shapes=[pltpu.VMEM((rows, out_width + LANES), BF16)],
         compiler_params=pltpu.CompilerParams(vmem_limit_bytes=58 << 20),
-    )(where, gated, *pieces)
+    )(x_at, *gated, *flat)
 
 
 def expert_of(row, owners, local_count):
@@ -348,7 +374,7 @@
 
 
 def dispatch_grads(ids, out_grad, expert_total, owners, local_count):
-    tokens, width = out_grad.shape
+    _, width = out_grad.shape
     slots = expert_total * CAP
     count = width // LANES
 
@@ -365,15 +391,16 @@
 
 
 def normalise(parts, residual, moe_gain, ids, inner_total, expert_total, owners, local_count):
-    x_count, tokens, _ = parts.shape
-    width = residual.shape[1]
+    tokens, width = residual.shape
     slots = expert_total * CAP
     count = width // LANES
-
-    def kernel(p_ref, r_ref, m_ref, i_ref, o_ref, h_ref, v_ref, s_ref):
-        summed = p_ref[0].astype(F32)
-        for x in range(1, x_count):
-            summed = summed + p_ref[x].astype(F32)
+    sources = len(parts)
+
+    def kernel(*refs):
+        r_ref, m_ref, i_ref, o_ref, h_ref, v_ref, s_ref = refs[sources:]
+        summed = refs[0][...].astype(F32)
+        for p_ref in refs[1:sources]:
+            summed = summed + p_ref[...].astype(F32)
         squares = summed[:, width : width + 1] + summed[:, width + 1 : width + 2] + summed[:, width + 2 : width + 3]
         hidden = r_ref[...].astype(F32) + summed[:, :width] * lax.rsqrt(squares / inner_total + 1e-05)
         hidden = hidden.astype(BF16)
@@ -394,11 +421,11 @@
             jax.ShapeDtypeStruct((tokens, LANES), F32),
         ),
         (pltpu.VMEM((slots * count, LANES), F32),),
-    )(parts, residual, moe_gain, ids)
+    )(*parts, residual, moe_gain, ids)
 
 
 def pack_weights(core, gate_up, down):
-    local_count, d_local, ff_both = gate_up.shape
+    _, d_local, ff_both = gate_up.shape
     ff_width = down.shape[1]
     tiles = ff_both // LANES
     height = tiles * d_local + ff_width
@@ -421,7 +448,7 @@
 
 
 def experts(core, rows_in, grads_in, weights, ff_width, gu_rows):
-    z_count, cores, height, _ = weights.shape
+    z_count, cores, _, _ = weights.shape
     count = z_count * cores
     slots = rows_in.shape[0] // count
     dests = slots // CAP
@@ -584,12 +611,10 @@
     owners = x_count * y_count
     heads = step_size.shape[1]
     channels = x_inner.shape[1]
-    head_width = channels // heads
     state_size = bc_input.shape[1] // 2
-    local_count, d_local, ff_both = gate_up_weight.shape
+    local_count, _, _ = gate_up_weight.shape
     ff_width = down_weight.shape[1]
     expert_total = local_count * owners
-    tokens, width = residual.shape
     exchange = ("core", "x", "y")
 
     ids_t, route_t = expert_ids.T, route_weights.T
@@ -604,36 +629,42 @@
     weights = lax.all_gather(jnp.stack([kept, swapped]), "z", axis=0, tiled=False)
     gu_rows = kept.shape[0] - ff_width
 
-    sent_grads = dispatch_grads(ids_t, out_grad, expert_total, owners, local_count)
-    rim, sent_grads = lax.optimization_barrier((rim, sent_grads))
-
-    conv, held_in, sent = mixer_state(
-        x_inner, bc_input, rim, conv_weight, bc_conv_weight, step_t, decay_t, ctx_count
-    )
-    received = lax.all_to_all(sent, ctx, split_axis=0, concat_axis=0, tiled=True)
-    grads_in = lax.all_to_all(
-        sent_grads.reshape(expert_total, -1, LANES), exchange, split_axis=0, concat_axis=0, tiled=True
-    )
-
     folded = (out_weight.astype(F32) * norm_gain[:, None]).astype(BF16)
-    folded, rim = lax.optimization_barrier((folded, rim))
     half = folded.shape[0] // 2
     from_prev = lax.ppermute(folded, "y", ring_route(y_count, 1))
     from_next = lax.ppermute(folded, "y", ring_route(y_count, -1))
-    y_local, e_rows = mixer_rows(conv, held_in, step_t, decay_t, skip_gain, channels)
-    received, from_prev, from_next, y_local = lax.optimization_barrier((received, from_prev, from_next, y_local))
     far_a = lax.ppermute(from_prev[:half], "y", ring_route(y_count, 1))
     far_b = lax.ppermute(from_next[half:], "y", ring_route(y_count, -1))
-    y_at = lax.axis_index("y")
-    where = jnp.stack([y_at, (y_at + y_count - 1) % y_count, (y_at + 1) % y_count, (y_at + 2) % y_count, (y_at + 2) % y_count]).astype(jnp.int32)
-
-    scanned = state_scan(received, state_size // ctx_count)
-    arriving = lax.all_to_all(scanned, ctx, split_axis=0, concat_axis=0, tiled=True).reshape(state_size, channels)
+
+    sent_grads = dispatch_grads(ids_t, out_grad, expert_total, owners, local_count)
+    rim, sent_grads = lax.optimization_barrier((rim, sent_grads))
+    grads_in = lax.all_to_all(
+        sent_grads.reshape(expert_total, -1, LANES), exchange, split_axis=0, concat_axis=0, tiled=True
+    )
+
+    conv, held_in, sent = mixer_state(x_inner, bc_input, rim, conv_weight, bc_conv_weight, step_t, decay_t)
+    reach = 4
+
+    def earlier(value, distance):
+        return lax.ppermute(value, ctx, [(i, i + distance) for i in range(ctx_count - distance)])
+
+    near = [earlier(sent, d) for d in range(1, reach + 1)]
+    y_local, e_cols = mixer_rows(conv, held_in, step_t, decay_t, skip_gain, channels)
+    window = join_states(near, state_size, False)
+    windows = [window] + [earlier(window, d) for d in range(reach, ctx_count, reach)]
+    arriving = join_states(windows, state_size, True)
     arriving, grads_in = lax.optimization_barrier((arriving, grads_in))
-    gated = gate_rows(y_local, conv, e_rows, arriving, gate_input, x_count, y_count)
-    gated = lax.all_to_all(gated, "y", split_axis=0, concat_axis=0, tiled=True)
-    parts = project(gated, [folded, from_prev, from_next, far_a, far_b], where, x_count)
-    parts = lax.all_to_all(parts, "x", split_axis=0, concat_axis=0, tiled=True)
+    y_at = lax.axis_index("y").astype(jnp.int32).reshape(1)
+    x_at = lax.axis_index("x").astype(jnp.int32).reshape(1)
+    gated = gate_rows(y_at, y_local, conv, e_cols, arriving, gate_input, heads, x_count, y_count)
+    gated = [gated[0]] + [
+        lax.ppermute(gated[k], "y", ring_route(y_count, k)) for k in range(1, y_count)
+    ]
+    pieces = [(folded,), (from_prev,), (far_a, far_b), (from_next,)]
+    parts = project(x_at, gated, pieces, x_count)
+    parts = [parts[0]] + [
+        lax.ppermute(parts[k], "x", ring_route(x_count, k)) for k in range(1, x_count)
+    ]
     sent_rows, hidden, inv_rms = normalise(
         parts, residual, moe_gain[None, :], ids_t, channels * owners, expert_total, owners, local_count
     )

time: 248 us -> 235 us (0.948)
  blocking collectives: 99.2 us -> 63.8 us
  starting transfers between devices: 25.2 us -> 53.6 us
  waiting for transfers between devices: 46.7 us -> 43.3 us
  Pallas kernels: 54.5 us -> 51.4 us
    all_to_all x2 -> x0, blocking collectives: 37.5 us -> none  [the longest x1 18.9 us: local(): parts = lax.all_to_all(parts, 'x', split_axis=0, concat_axis=0, tiled=True)]
    ppermute x0 -> x13, starting transfers between devices: none -> 36.2 us  [the longest x7 29.3 us: earlier(): lax.ppermute(value, ctx, [(i, i + distance) for i in range(ctx_count - di...]
    ppermute x0 -> x13, waiting for transfers between devices: none -> 21.8 us  [the longest x3 9.48 us: local(): lax.ppermute(parts[k], 'x', ring_route(x_count, k))]
    all_to_all x2 -> x0, waiting for transfers between devices: 15.9 us -> none  [the longest x1 8.79 us: local(): gated = lax.all_to_all(gated, 'y', split_axis=0, concat_axis=0, tiled=True)]
    ppermute x1, waiting for transfers between devices: 29.1 us -> 19.7 us  [local(): from_prev = lax.ppermute(folded, 'y', ring_route(y_count, 1))]
    all_to_all x2 -> x0, starting transfers between devices: 7.63 us -> none  [the longest x1 4.16 us: local(): lax.all_to_all(scanned, ctx, split_axis=0, concat_axis=0, tiled=True)]
    pallas_call x1, Pallas kernels: 8 us -> 4.92 us  [mixer_state(): call(kernel, (jax.ShapeDtypeStruct((rows, width), BF16), jax.ShapeDtypeSt...]
    pallas_call x3 -> x4, Pallas kernels: 9.87 us -> 11.9 us  [the longest x1 4.84 us: project(): pl.pallas_call(kernel, out_shape=(shape,) * x_count, in_specs=[pl.BlockSp...]
  transfers between devices with their start and end apart: 10 -> 21, of which waited for: 4 -> 10; matrix products, arithmetic and copies ran while one was open for 1% -> 1% of each run, Pallas kernels for 13% -> 12%
where the time goes in v2:
time: 235 us; the launch traced here: 234 us
  blocking collectives  63.8 us (27%)
  starting transfers between devices  53.6 us (23%)
  Pallas kernels  51.4 us (22%)
  waiting for transfers between devices  43.3 us (18%)
  between operations  14.3 us (6%)
  local copies, waits for them, and re-layouts  5.38 us (2%)
  other arithmetic  2.45 us (1%)
    all_to_all x1, blocking collectives, local(): lax.all_to_all(back, exchange, split_axis=0, concat_axis=0, tiled=True)  36.2 us
    ppermute x7, starting transfers between devices, earlier(): lax.ppermute(value, ctx, [(i, i + distance) for i in range(ctx_count - di...  29.3 us
    all_to_all x1, blocking collectives, local(): lax.all_to_all(sent_rows.reshape(expert_total, -1, LANES), exchange, spli...  27.6 us
    ppermute x1, waiting for transfers between devices, local(): from_prev = lax.ppermute(folded, 'y', ring_route(y_count, 1))  19.7 us
    pallas_call x1, Pallas kernels, experts(): pl.pallas_call(kernel, out_shape=jax.ShapeDtypeStruct((dests, 2 * each, L...  14.4 us
    ppermute x3, waiting for transfers between devices, local(): lax.ppermute(parts[k], 'x', ring_route(x_count, k))  9.48 us
    ppermute x3, waiting for transfers between devices, local(): lax.ppermute(gated[k], 'y', ring_route(y_count, k))  6.23 us
    ppermute x7, waiting for transfers between devices, earlier(): lax.ppermute(value, ctx, [(i, i + distance) for i in range(ctx_count - di...  6.11 us
  transfers between devices with their start and end apart: 21, of which 10 were waited for; matrix products, arithmetic and copies ran while one was open for 1% of the time, Pallas kernels for 12%

profile of v2, /device:TPU:1, one launch (start us, length us, event | category | flops | bytes accessed | tf_op | source)
XLA Modules:
  0.0 234.2 jit_solution(15938773703183287187)
XLA Ops:
  9.6 3.2 %collective-permute-start.18 = (bf16[2112,128]{1,0:T(8,128)(2,1)}, bf16[2112,128]{1,0:T(8,128)(2,1)S(1)}, u32[]{:S(2)}, u32[]{:S(2)}) collective-permute-start(bf16[2112,128]{1,0:T(8,128)(2,1)} %get-tuple-element.47), channel_id=1, source_target_pairs={{0,16},{16,0},{1,17},{17,1},{2,18},{18,2},{3,19},{19,3},{4,20},{20... | collective-permute-start | bytes 1622024 | tf_op jit(solution)/shard_map/ppermute | solution.py:628
  17.2 2.7 %collective-permute-start.13 = (bf16[256,2048]{1,0:T(8,128)(2,1)S(1)}, bf16[256,2048]{1,0:T(8,128)(2,1)}, u32[]{:S(2)}, u32[]{:S(2)}) collective-permute-start(bf16[256,2048]{1,0:T(8,128)(2,1)S(1)} %multiply_convert_fusion.refs_4_), channel_id=1, source_target_pairs={{0,3},{1,0},{2,1},{3,2},{4,7},{5,4},{6,5},{7,6},{8,11},{9,8},{10,9... | collective-permute-start | bytes 3145736 | tf_op jit(solution)/shard_map/ppermute | solution.py:635
  22.5 3.5 %shard_map.184 = bf16[4608,128]{1,0:T(8,128)(2,1)} custom-call(s32[4,64]{1,0:T(4,128)} %bitcast.29, bf16[64,2048]{1,0:T(8,128)(2,1)} %g_ref.7), custom_call_target="tpu_custom_call" | custom-call | tf_op jit(solution)/shard_map/pallas_call | solution.py:386
  26.6 6.0 %all-to-all-start = ((bf16[32,144,128]{2,1,0:T(8,128)(2,1)}), bf16[32,144,128]{2,1,0:T(8,128)(2,1)S(1)}, u32[]{:S(2)}, u32[]{:S(2)}) async-start(bf16[32,144,128]{2,1,0:T(8,128)(2,1)} %bitcast.17), calls=%async_computation | async-start | bytes 2359296 | tf_op jit(solution)/shard_map/all_to_all | solution.py:641
  32.6 19.7 %collective-permute-done.11.refs_5_ = bf16[256,2048]{1,0:T(8,128)(2,1)S(1)} collective-permute-done((bf16[256,2048]{1,0:T(8,128)(2,1)S(1)}, bf16[256,2048]{1,0:T(8,128)(2,1)S(1)}, u32[]{:S(2)}, u32[]{:S(2)}) %collective-permute-start.11) | collective-permute-done | bytes 1048608 | tf_op jit(solution)/shard_map/ppermute | solution.py:634
  54.3 2.8 %collective-permute-start.14 = (bf16[128,2048]{1,0:T(8,128)(2,1)S(1)}, bf16[128,2048]{1,0:T(8,128)(2,1)S(1)}, u32[]{:S(2)}, u32[]{:S(2)}) collective-permute-start(bf16[128,2048]{1,0:T(8,128)(2,1)S(1)} %slice.17), channel_id=1, source_target_pairs={{0,3},{1,0},{2,1},{3,2},{4,7},{5,4},{6,5},{7,6},{8,11},{9,8},{10,9... | collective-permute-start | bytes 1572872 | tf_op jit(solution)/shard_map/ppermute | solution.py:637
  57.0 4.9 %shard_map.185 = (bf16[1024,512]{1,0:T(8,128)(2,1)}, bf16[1024,256]{1,0:T(8,128)(2,1)}, bf16[144,256]{1,0:T(8,128)(2,1)}) custom-call(bf16[1024,256]{1,0:T(8,128)(2,1)} %x_ref.1, bf16[1024,256]{1,0:T(8,128)(2,1)} %bc_ref.1, bf16[8,512]{1,0:T(8,128)(2,1)} %copy-done.18, f32[4,256]{1,0:T(4,128)} %wx_ref.1, f32[4,256]{1,0:T(4,128)} %wb_ref.1, ...), custom_call_target="tpu_custom_call" | custom-call | tf_op jit(solution)/shard_map/pallas_call | solution.py:121
  62.0 4.4 %collective-permute-start.1 = (bf16[144,256]{1,0:T(8,128)(2,1)}, bf16[144,256]{1,0:T(8,128)(2,1)S(1)}, u32[]{:S(2)}, u32[]{:S(2)}) collective-permute-start(bf16[144,256]{1,0:T(8,128)(2,1)} %get-tuple-element.33), channel_id=1, source_target_pairs={{0,16},{16,32},{32,48},{48,64},{64,80},{80,96},{96,112},{112,128},... | collective-permute-start | bytes 221192 | tf_op jit(solution)/shard_map/ppermute | solution.py:649
  66.4 3.5 %collective-permute-start.2 = (bf16[144,256]{1,0:T(8,128)(2,1)}, bf16[144,256]{1,0:T(8,128)(2,1)S(1)}, u32[]{:S(2)}, u32[]{:S(2)}) collective-permute-start(bf16[144,256]{1,0:T(8,128)(2,1)} %get-tuple-element.33), channel_id=1, source_target_pairs={{0,32},{16,48},{32,64},{48,80},{64,96},{80,112},{96,128},{112,144}... | collective-permute-start | bytes 221192 | tf_op jit(solution)/shard_map/ppermute | solution.py:649
  70.0 3.5 %collective-permute-start.3 = (bf16[144,256]{1,0:T(8,128)(2,1)}, bf16[144,256]{1,0:T(8,128)(2,1)S(1)}, u32[]{:S(2)}, u32[]{:S(2)}) collective-permute-start(bf16[144,256]{1,0:T(8,128)(2,1)} %get-tuple-element.33), channel_id=1, source_target_pairs={{0,48},{16,64},{32,80},{48,96},{64,112},{80,128},{96,144},{112,160... | collective-permute-start | bytes 221192 | tf_op jit(solution)/shard_map/ppermute | solution.py:649
  73.5 5.2 %collective-permute-start.4 = (bf16[144,256]{1,0:T(8,128)(2,1)}, bf16[144,256]{1,0:T(8,128)(2,1)S(1)}, u32[]{:S(2)}, u32[]{:S(2)}) collective-permute-start(bf16[144,256]{1,0:T(8,128)(2,1)} %get-tuple-element.33), channel_id=1, source_target_pairs={{0,64},{16,80},{32,96},{48,112},{64,128},{80,144},{96,160},{112,17... | collective-permute-start | bytes 221192 | tf_op jit(solution)/shard_map/ppermute | solution.py:649
  78.8 3.8 %collective-permute-done.4.refs_3_ = bf16[144,256]{1,0:T(8,128)(2,1)S(1)} collective-permute-done((bf16[144,256]{1,0:T(8,128)(2,1)}, bf16[144,256]{1,0:T(8,128)(2,1)S(1)}, u32[]{:S(2)}, u32[]{:S(2)}) %collective-permute-start.4) | collective-permute-done | bytes 73760 | tf_op jit(solution)/shard_map/ppermute | solution.py:649
  84.9 4.9 %collective-permute-start.5 = (bf16[144,256]{1,0:T(8,128)(2,1)}, bf16[144,256]{1,0:T(8,128)(2,1)S(1)}, u32[]{:S(2)}, u32[]{:S(2)}) collective-permute-start(bf16[144,256]{1,0:T(8,128)(2,1)} %shard_map.187.refs_0_), channel_id=1, source_target_pairs={{0,64},{16,80},{32,96},{48,112},{64,128},{80,144},{96,160},{112,17... | collective-permute-start | bytes 221192 | tf_op jit(solution)/shard_map/ppermute | solution.py:649
  89.8 6.3 %collective-permute-start.6 = (bf16[144,256]{1,0:T(8,128)(2,1)}, bf16[144,256]{1,0:T(8,128)(2,1)S(1)}, u32[]{:S(2)}, u32[]{:S(2)}) collective-permute-start(bf16[144,256]{1,0:T(8,128)(2,1)} %shard_map.187.refs_0_), channel_id=1, source_target_pairs={{0,128},{16,144},{32,160},{48,176},{64,192},{80,208},{96,224},{112... | collective-permute-start | bytes 221192 | tf_op jit(solution)/shard_map/ppermute | solution.py:649
  97.6 4.4 %shard_map.186 = (f32[1024,256]{1,0:T(8,128)}, f32[128,128]{1,0:T(8,128)}) custom-call(f32[4]{0:T(128)} %skip_ref.1, bf16[1024,512]{1,0:T(8,128)(2,1)} %get-tuple-element.29.conv_ref.c_ref, bf16[1024,256]{1,0:T(8,128)(2,1)} %get-tuple-element.30.in_ref, f32[4,1024]{1,0:T(4,128)} %bitcast.24, f32[4,1024]{1,0:T(4,128)} %bitcast.26), custom_call_target="tpu_custom_call" | custom-call | tf_op jit(solution)/shard_map/pallas_call | solution.py:193
  106.6 3.7 %shard_map.189 = (bf16[256,256]{1,0:T(8,128)(2,1)}, bf16[256,256]{1,0:T(8,128)(2,1)}, bf16[256,256]{1,0:T(8,128)(2,1)}, bf16[256,256]{1,0:T(8,128)(2,1)}) custom-call(s32[1]{0:T(128)} %bitcast.2.at_ref, f32[1024,256]{1,0:T(8,128)} %get-tuple-element.31.y_ref, bf16[1024,512]{1,0:T(8,128)(2,1)} %get-tuple-element.29.conv_ref.c_ref, ...), custom_call_target="tpu_custom_call" | custom-call | tf_op jit(solution)/shard_map/pallas_call | solution.py:253
  115.9 2.7 %collective-permute-done.9.refs_2_ = bf16[256,256]{1,0:T(8,128)(2,1)S(1)} collective-permute-done((bf16[256,256]{1,0:T(8,128)(2,1)}, bf16[256,256]{1,0:T(8,128)(2,1)S(1)}, u32[]{:S(2)}, u32[]{:S(2)}) %collective-permute-start.9) | collective-permute-done | bytes 131104 | tf_op jit(solution)/shard_map/ppermute | solution.py:661
  119.4 4.8 %shard_map.190 = (bf16[64,2176]{1,0:T(8,128)(2,1)}, bf16[64,2176]{1,0:T(8,128)(2,1)}, bf16[64,2176]{1,0:T(8,128)(2,1)}, bf16[64,2176]{1,0:T(8,128)(2,1)}) custom-call(s32[1]{0:T(128)} %bitcast.1.at_ref, bf16[256,256]{1,0:T(8,128)(2,1)} %get-tuple-element.36.refs_0_, bf16[256,256]{1,0:T(8,128)(2,1)} %copy-done.9, bf16[256,256]{1,0:T(8,128)(2,1)} %copy-done.10, ...), custom_call_target="tpu_custom_call" | custom-call | tf_op jit(solution)/shard_map/pallas_call | solution.py:296
  131.1 6.8 %collective-permute-done.16.refs_2_ = bf16[64,2176]{1,0:T(8,128)(2,1)S(1)} collective-permute-done((bf16[64,2176]{1,0:T(8,128)(2,1)}, bf16[64,2176]{1,0:T(8,128)(2,1)S(1)}, u32[]{:S(2)}, u32[]{:S(2)}) %collective-permute-start.16) | collective-permute-done | bytes 278560 | tf_op jit(solution)/shard_map/ppermute | solution.py:666
  139.2 4.0 %shard_map.191 = (bf16[4608,128]{1,0:T(8,128)(2,1)}, bf16[64,2048]{1,0:T(8,128)(2,1)}, f32[64,128]{1,0:T(8,128)}) custom-call(bf16[64,2176]{1,0:T(8,128)(2,1)} %get-tuple-element.40.refs_0_, bf16[64,2176]{1,0:T(8,128)(2,1)} %copy-done.5, bf16[64,2176]{1,0:T(8,128)(2,1)} %copy-done.6, bf16[64,2176]{1,0:T(8,128)(2,1)} %copy-done.7, bf16[64,2048]{1,0:T(8,128)(2,1)} %refs_4_.1, ...), custom_call_target="tpu_custom_call" | custom-call | tf_op jit(solution)/shard_map/pallas_call | solution.py:416
  143.3 27.6 %all_to_all.15 = bf16[32,144,128]{2,1,0:T(8,128)(2,1)} all-to-all(bf16[32,144,128]{2,1,0:T(8,128)(2,1)} %bitcast.20), channel_id=1, replica_groups=mesh['z'=8,'core'=2,'x'=4,'y'=4] {'core','x','y'}, dimensions={0} | all-to-all | bytes 2359296 | tf_op jit(solution)/shard_map/all_to_all | solution.py:671
  170.8 14.4 %shard_map.193 = bf16[32,288,128]{2,1,0:T(8,128)(2,1)} custom-call(s32[1]{0:T(128)} %bitcast.core_ref, bf16[4608,128]{1,0:T(8,128)(2,1)} %bitcast.19, bf16[4608,128]{1,0:T(8,128)(2,1)} %bitcast.18, bf16[8,2,2112,128]{3,2,1,0:T(8,128)(2,1)} %bitcast.16), custom_call_target="tpu_custom_call" | custom-call | tf_op jit(solution)/shard_map/pallas_call | solution.py:516
  185.2 36.2 %all_to_all.16.r_ref = bf16[32,288,128]{2,1,0:T(8,128)(2,1)} all-to-all(bf16[32,288,128]{2,1,0:T(8,128)(2,1)} %shard_map.193), channel_id=1, replica_groups=mesh['z'=8,'core'=2,'x'=4,'y'=4] {'core','x','y'}, dimensions={0} | all-to-all | bytes 4718592 | tf_op jit(solution)/shard_map/all_to_all | solution.py:675
  221.5 5.9 %shard_map.194 = (bf16[64,2048]{1,0:T(8,128)(2,1)}, bf16[64,2048]{1,0:T(8,128)(2,1)}, f32[4,64]{1,0:T(4,128)}) custom-call(bf16[32,288,128]{2,1,0:T(8,128)(2,1)} %all_to_all.16.r_ref, bf16[64,2048]{1,0:T(8,128)(2,1)} %get-tuple-element.48.h_ref, f32[64,128]{1,0:T(8,128)} %get-tuple-element.49.v_ref, bf16[64,2048]{1,0:T(8,128)(2,1)} %g_ref.7, ...), custom_call_target="tpu_custom_call" | custom-call | tf_op jit(solution)/shard_map/pallas_call | solution.py:578
  (81 shorter events, 35.0 us)
Async XLA Ops:
  7.2 163.7 %all-gather.3.cloned.1.call-start = ((), (), s32[]{:S(2)}) async-start(), calls=%async_computation.3 | async-start | bytes 9732096 | tf_op jit(solution)/shard_map/all_gather | solution.py:629
  9.6 5.0 %collective-permute-start.18 = (bf16[2112,128]{1,0:T(8,128)(2,1)}, bf16[2112,128]{1,0:T(8,128)(2,1)S(1)}, u32[]{:S(2)}, u32[]{:S(2)}) collective-permute-start(bf16[2112,128]{1,0:T(8,128)(2,1)} %get-tuple-element.47), channel_id=1, source_target_pairs={{0,16},{16,0},{1,17},{17,1},{2,18},{18,2},{3,19},{19,3},{4,20},{20... | collective-permute-start | bytes 1622024 | tf_op jit(solution)/shard_map/ppermute | solution.py:628
  17.1 8.9 %copy-start.1 = (bf16[256,2048]{1,0:T(8,128)(2,1)}, bf16[256,2048]{1,0:T(8,128)(2,1)S(1)}, u32[]{:S(2)}) copy-start(bf16[256,2048]{1,0:T(8,128)(2,1)S(1)} %multiply_convert_fusion.refs_4_) | copy-start | bytes 3145732
  17.1 35.2 %collective-permute-start.11 = (bf16[256,2048]{1,0:T(8,128)(2,1)S(1)}, bf16[256,2048]{1,0:T(8,128)(2,1)S(1)}, u32[]{:S(2)}, u32[]{:S(2)}) collective-permute-start(bf16[256,2048]{1,0:T(8,128)(2,1)S(1)} %multiply_convert_fusion.refs_4_), channel_id=1, source_target_pairs={{0,1},{1,2},{2,3},{3,0},{4,5},{5,6},{6,7},{7,4},{8,9},{9,10},{10,1... | collective-permute-start | bytes 3145736 | tf_op jit(solution)/shard_map/ppermute | solution.py:634
  17.2 36.0 %collective-permute-start.13 = (bf16[256,2048]{1,0:T(8,128)(2,1)S(1)}, bf16[256,2048]{1,0:T(8,128)(2,1)}, u32[]{:S(2)}, u32[]{:S(2)}) collective-permute-start(bf16[256,2048]{1,0:T(8,128)(2,1)S(1)} %multiply_convert_fusion.refs_4_), channel_id=1, source_target_pairs={{0,3},{1,0},{2,1},{3,2},{4,7},{5,4},{6,5},{7,6},{8,11},{9,8},{10,9... | collective-permute-start | bytes 3145736 | tf_op jit(solution)/shard_map/ppermute | solution.py:635
  19.8 6.1 %collective-permute-start = (bf16[8,512]{1,0:T(8,128)(2,1)S(1)}, bf16[8,512]{1,0:T(8,128)(2,1)S(1)}, u32[]{:S(2)}, u32[]{:S(2)}) collective-permute-start(bf16[8,512]{1,0:T(8,128)(2,1)S(1)} %pad_maximum_fusion.1), channel_id=1, source_target_pairs={{0,16},{16,32},{32,48},{48,64},{64,80},{80,96},{96,112},{112,128},... | collective-permute-start | bytes 24584 | tf_op jit(solution)/shard_map/ppermute | solution.py:625
  26.6 80.0 %all-to-all-start = ((bf16[32,144,128]{2,1,0:T(8,128)(2,1)}), bf16[32,144,128]{2,1,0:T(8,128)(2,1)S(1)}, u32[]{:S(2)}, u32[]{:S(2)}) async-start(bf16[32,144,128]{2,1,0:T(8,128)(2,1)} %bitcast.17), calls=%async_computation | async-start | bytes 2359296 | tf_op jit(solution)/shard_map/all_to_all | solution.py:641
  52.3 9.7 %copy-start.2 = (bf16[256,2048]{1,0:T(8,128)(2,1)}, bf16[256,2048]{1,0:T(8,128)(2,1)S(1)}, u32[]{:S(2)}) copy-start(bf16[256,2048]{1,0:T(8,128)(2,1)S(1)} %collective-permute-done.11.refs_5_) | copy-start | bytes 3145732
  53.2 65.4 %collective-permute-start.12 = (bf16[128,2048]{1,0:T(8,128)(2,1)}, bf16[128,2048]{1,0:T(8,128)(2,1)}, u32[]{:S(2)}, u32[]{:S(2)}) collective-permute-start(bf16[128,2048]{1,0:T(8,128)(2,1)} %slice.16), channel_id=1, source_target_pairs={{0,1},{1,2},{2,3},{3,0},{4,5},{5,6},{6,7},{7,4},{8,9},{9,10},{10,1... | collective-permute-start | bytes 1572872 | tf_op jit(solution)/shard_map/ppermute | solution.py:636
  54.3 64.3 %collective-permute-start.14 = (bf16[128,2048]{1,0:T(8,128)(2,1)S(1)}, bf16[128,2048]{1,0:T(8,128)(2,1)S(1)}, u32[]{:S(2)}, u32[]{:S(2)}) collective-permute-start(bf16[128,2048]{1,0:T(8,128)(2,1)S(1)} %slice.17), channel_id=1, source_target_pairs={{0,3},{1,0},{2,1},{3,2},{4,7},{5,4},{6,5},{7,6},{8,11},{9,8},{10,9... | collective-permute-start | bytes 1572872 | tf_op jit(solution)/shard_map/ppermute | solution.py:637
  62.0 11.5 %collective-permute-start.1 = (bf16[144,256]{1,0:T(8,128)(2,1)}, bf16[144,256]{1,0:T(8,128)(2,1)S(1)}, u32[]{:S(2)}, u32[]{:S(2)}) collective-permute-start(bf16[144,256]{1,0:T(8,128)(2,1)} %get-tuple-element.33), channel_id=1, source_target_pairs={{0,16},{16,32},{32,48},{48,64},{64,80},{80,96},{96,112},{112,128},... | collective-permute-start | bytes 221192 | tf_op jit(solution)/shard_map/ppermute | solution.py:649
  66.4 12.3 %collective-permute-start.2 = (bf16[144,256]{1,0:T(8,128)(2,1)}, bf16[144,256]{1,0:T(8,128)(2,1)S(1)}, u32[]{:S(2)}, u32[]{:S(2)}) collective-permute-start(bf16[144,256]{1,0:T(8,128)(2,1)} %get-tuple-element.33), channel_id=1, source_target_pairs={{0,32},{16,48},{32,64},{48,80},{64,96},{80,112},{96,128},{112,144}... | collective-permute-start | bytes 221192 | tf_op jit(solution)/shard_map/ppermute | solution.py:649
  70.0 8.8 %collective-permute-start.3 = (bf16[144,256]{1,0:T(8,128)(2,1)}, bf16[144,256]{1,0:T(8,128)(2,1)S(1)}, u32[]{:S(2)}, u32[]{:S(2)}) collective-permute-start(bf16[144,256]{1,0:T(8,128)(2,1)} %get-tuple-element.33), channel_id=1, source_target_pairs={{0,48},{16,64},{32,80},{48,96},{64,112},{80,128},{96,144},{112,160... | collective-permute-start | bytes 221192 | tf_op jit(solution)/shard_map/ppermute | solution.py:649
  73.5 9.1 %copy-start.12 = (bf16[144,256]{1,0:T(8,128)(2,1)}, bf16[144,256]{1,0:T(8,128)(2,1)S(1)}, u32[]{:S(2)}) copy-start(bf16[144,256]{1,0:T(8,128)(2,1)S(1)} %collective-permute-done.1.refs_0_) | copy-start | bytes 221188
  73.5 9.1 %collective-permute-start.4 = (bf16[144,256]{1,0:T(8,128)(2,1)}, bf16[144,256]{1,0:T(8,128)(2,1)S(1)}, u32[]{:S(2)}, u32[]{:S(2)}) collective-permute-start(bf16[144,256]{1,0:T(8,128)(2,1)} %get-tuple-element.33), channel_id=1, source_target_pairs={{0,64},{16,80},{32,96},{48,112},{64,128},{80,144},{96,160},{112,17... | collective-permute-start | bytes 221192 | tf_op jit(solution)/shard_map/ppermute | solution.py:649
  84.9 17.1 %collective-permute-start.5 = (bf16[144,256]{1,0:T(8,128)(2,1)}, bf16[144,256]{1,0:T(8,128)(2,1)S(1)}, u32[]{:S(2)}, u32[]{:S(2)}) collective-permute-start(bf16[144,256]{1,0:T(8,128)(2,1)} %shard_map.187.refs_0_), channel_id=1, source_target_pairs={{0,64},{16,80},{32,96},{48,112},{64,128},{80,144},{96,160},{112,17... | collective-permute-start | bytes 221192 | tf_op jit(solution)/shard_map/ppermute | solution.py:649
  89.8 12.2 %collective-permute-start.6 = (bf16[144,256]{1,0:T(8,128)(2,1)}, bf16[144,256]{1,0:T(8,128)(2,1)S(1)}, u32[]{:S(2)}, u32[]{:S(2)}) collective-permute-start(bf16[144,256]{1,0:T(8,128)(2,1)} %shard_map.187.refs_0_), channel_id=1, source_target_pairs={{0,128},{16,144},{32,160},{48,176},{64,192},{80,208},{96,224},{112... | collective-permute-start | bytes 221192 | tf_op jit(solution)/shard_map/ppermute | solution.py:649
  96.1 8.2 %collective-permute-start.7 = (bf16[144,256]{1,0:T(8,128)(2,1)}, bf16[144,256]{1,0:T(8,128)(2,1)S(1)}, u32[]{:S(2)}, u32[]{:S(2)}) collective-permute-start(bf16[144,256]{1,0:T(8,128)(2,1)} %shard_map.187.refs_0_), channel_id=1, source_target_pairs={{0,192},{16,208},{32,224},{48,240},{1,193},{17,209},{33,225},{49,2... | collective-permute-start | bytes 221192 | tf_op jit(solution)/shard_map/ppermute | solution.py:649
  110.3 4.4 %collective-permute-start.10 = (bf16[256,256]{1,0:T(8,128)(2,1)}, bf16[256,256]{1,0:T(8,128)(2,1)S(1)}, u32[]{:S(2)}, u32[]{:S(2)}) collective-permute-start(bf16[256,256]{1,0:T(8,128)(2,1)} %get-tuple-element.39), channel_id=1, source_target_pairs={{0,3},{1,0},{2,1},{3,2},{4,7},{5,4},{6,5},{7,6},{8,11},{9,8},{10,9... | collective-permute-start | bytes 393224 | tf_op jit(solution)/shard_map/ppermute | solution.py:661
  110.7 5.2 %collective-permute-start.8 = (bf16[256,256]{1,0:T(8,128)(2,1)}, bf16[256,256]{1,0:T(8,128)(2,1)S(1)}, u32[]{:S(2)}, u32[]{:S(2)}) collective-permute-start(bf16[256,256]{1,0:T(8,128)(2,1)} %get-tuple-element.37), channel_id=1, source_target_pairs={{0,1},{1,2},{2,3},{3,0},{4,5},{5,6},{6,7},{7,4},{8,9},{9,10},{10,1... | collective-permute-start | bytes 393224 | tf_op jit(solution)/shard_map/ppermute | solution.py:661
  111.8 6.8 %collective-permute-start.9 = (bf16[256,256]{1,0:T(8,128)(2,1)}, bf16[256,256]{1,0:T(8,128)(2,1)S(1)}, u32[]{:S(2)}, u32[]{:S(2)}) collective-permute-start(bf16[256,256]{1,0:T(8,128)(2,1)} %get-tuple-element.38), channel_id=1, source_target_pairs={{0,2},{1,3},{2,0},{3,1},{4,6},{5,7},{6,4},{7,5},{8,10},{9,11},{10,... | collective-permute-start | bytes 393224 | tf_op jit(solution)/shard_map/ppermute | solution.py:661
  124.3 6.8 %collective-permute-start.15 = (bf16[64,2176]{1,0:T(8,128)(2,1)}, bf16[64,2176]{1,0:T(8,128)(2,1)S(1)}, u32[]{:S(2)}, u32[]{:S(2)}) collective-permute-start(bf16[64,2176]{1,0:T(8,128)(2,1)} %get-tuple-element.41), channel_id=1, source_target_pairs={{0,4},{4,8},{8,12},{12,0},{1,5},{5,9},{9,13},{13,1},{2,6},{6,10},{... | collective-permute-start | bytes 835592 | tf_op jit(solution)/shard_map/ppermute | solution.py:666
  125.5 12.4 %collective-permute-start.16 = (bf16[64,2176]{1,0:T(8,128)(2,1)}, bf16[64,2176]{1,0:T(8,128)(2,1)S(1)}, u32[]{:S(2)}, u32[]{:S(2)}) collective-permute-start(bf16[64,2176]{1,0:T(8,128)(2,1)} %get-tuple-element.42), channel_id=1, source_target_pairs={{0,8},{4,12},{8,0},{12,4},{1,9},{5,13},{9,1},{13,5},{2,10},{6,14},... | collective-permute-start | bytes 835592 | tf_op jit(solution)/shard_map/ppermute | solution.py:666
  127.9 10.6 %collective-permute-start.17 = (bf16[64,2176]{1,0:T(8,128)(2,1)}, bf16[64,2176]{1,0:T(8,128)(2,1)S(1)}, u32[]{:S(2)}, u32[]{:S(2)}) collective-permute-start(bf16[64,2176]{1,0:T(8,128)(2,1)} %get-tuple-element.43), channel_id=1, source_target_pairs={{0,12},{4,0},{8,4},{12,8},{1,13},{5,1},{9,5},{13,9},{2,14},{6,2},{... | collective-permute-start | bytes 835592 | tf_op jit(solution)/shard_map/ppermute | solution.py:666
  (19 other events, 45.3 us)
Sparse Core Ops, SparseCore 0:
  16.9 101.1 all-gather.2

commit v3 on v2

--- a/solution.py
+++ b/solution.py
@@ -447,23 +447,28 @@
     )(core, gate_up, down)
 
 
+def weight_copies(w_hbm, w_ref, sems):
+    return [pltpu.make_async_copy(w_hbm.at[z], w_ref.at[z], sems.at[z]) for z in range(w_hbm.shape[0])]
+
+
+def columns_in_order(z_count, cores, core):
+    return [(z, s, z * cores + (core if s == 0 else 1 - core)) for z in range(z_count) for s in range(cores)]
+
+
 def experts(core, rows_in, grads_in, weights, ff_width, gu_rows):
     z_count, cores, _, _ = weights.shape
     count = z_count * cores
     slots = rows_in.shape[0] // count
-    dests = slots // CAP
     ff_tiles = 2 * ff_width // LANES
     block = gu_rows // ff_tiles
-    each = CAP * count
-
-    def kernel(core_ref, x_ref, g_ref, w_hbm, o_ref, x_s, g_s, xb_s, gb_s, w_ref, sems):
-        copies = [pltpu.make_async_copy(w_hbm.at[z], w_ref.at[z], sems.at[z]) for z in range(z_count)]
+
+    def kernel(core_ref, x_ref, g_ref, w_hbm, o_ref, b_ref, x_s, g_s, xb_s, gb_s, w_ref, sems):
+        copies = weight_copies(w_hbm, w_ref, sems)
         for copy in copies:
             copy.start()
-        core = core_ref[0]
+        order = columns_in_order(z_count, cores, core_ref[0])
         x_s[...] = x_ref[...].astype(F32)
         g_s[...] = g_ref[...].astype(F32)
-        order = [(z, s, z * cores + (core if s == 0 else 1 - core)) for z in range(z_count) for s in range(cores)]
         for i, (z, s, c) in enumerate(order):
             xb_s[:, i * LANES : (i + 1) * LANES] = x_s[pl.ds(c, slots, stride=count), :].astype(BF16)
             gb_s[:, i * LANES : (i + 1) * LANES] = g_s[pl.ds(c, slots, stride=count), :].astype(BF16)
@@ -496,28 +501,24 @@
         activated = (act * pre_up).astype(BF16)
         grad_gate = hidden_grad * pre_up * sig * (1.0 + pre_gate * (1.0 - sig))
         grad_up = hidden_grad * act
-        grad_both = jnp.concatenate([grad_gate, grad_up], axis=1).astype(BF16)
+        b_ref[...] = jnp.concatenate([grad_gate, grad_up], axis=1).astype(BF16)
         for z in range(z_count):
             rhs = jnp.concatenate([w_ref[z, s, gu_rows:, :] for s in range(cores)], axis=1)
             out = mm(activated, rhs, NN)
-            rhs = jnp.concatenate(
-                [jnp.concatenate([tile(z, s, i) for i in range(ff_tiles)], axis=1) for s in range(cores)], axis=0
-            )
-            grad = mm(grad_both, rhs, NT)
             for s in range(cores):
-                c = z * cores + (core if s == 0 else 1 - core)
+                c = order[z * cores + s][2]
                 x_s[pl.ds(c, slots, stride=count), :] = out[:, s * LANES : (s + 1) * LANES]
-                g_s[pl.ds(c, slots, stride=count), :] = grad[:, s * LANES : (s + 1) * LANES]
-        for d in range(dests):
-            o_ref[d, :each, :] = x_s[d * each : (d + 1) * each, :].astype(BF16)
-            o_ref[d, each:, :] = g_s[d * each : (d + 1) * each, :].astype(BF16)
+        o_ref[...] = x_s[...].astype(BF16)
 
     vmem = pl.BlockSpec(memory_space=pltpu.VMEM)
     return pl.pallas_call(
         kernel,
-        out_shape=jax.ShapeDtypeStruct((dests, 2 * each, LANES), BF16),
+        out_shape=(
+            jax.ShapeDtypeStruct(rows_in.shape, BF16),
+            jax.ShapeDtypeStruct((slots, 2 * ff_width), BF16),
+        ),
         in_specs=[pl.BlockSpec(memory_space=pltpu.SMEM), vmem, vmem, pl.BlockSpec(memory_space=pl.ANY)],
-        out_specs=vmem,
+        out_specs=(vmem, vmem),
         scratch_shapes=[
             pltpu.VMEM(rows_in.shape, F32),
             pltpu.VMEM(rows_in.shape, F32),
@@ -530,17 +531,65 @@
     )(core, rows_in, grads_in, weights)
 
 
-def combine(back, hidden, inv_rms, out_grad, moe_gain, ids_t, route_t, expert_total, owners, local_count):
+def expert_inputs(core, grad_both, weights, gu_rows):
+    z_count, cores, _, _ = weights.shape
+    count = z_count * cores
+    slots, ff_both = grad_both.shape
+    ff_tiles = ff_both // LANES
+    block = gu_rows // ff_tiles
+
+    def kernel(core_ref, b_ref, w_hbm, o_ref, s_ref, w_ref, sems):
+        copies = [
+            pltpu.make_async_copy(w_hbm.at[z, :, pl.ds(0, gu_rows), :], w_ref.at[z], sems.at[z])
+            for z in range(z_count)
+        ]
+        for copy in copies:
+            copy.start()
+        order = columns_in_order(z_count, cores, core_ref[0])
+        for z in range(z_count):
+            copies[z].wait()
+            rhs = jnp.concatenate(
+                [
+                    jnp.concatenate([w_ref[z, s, i * block : (i + 1) * block, :] for i in range(ff_tiles)], axis=1)
+                    for s in range(cores)
+                ],
+                axis=0,
+            )
+            grad = mm(b_ref[...], rhs, NT)
+            for s in range(cores):
+                c = order[z * cores + s][2]
+                s_ref[pl.ds(c, slots, stride=count), :] = grad[:, s * LANES : (s + 1) * LANES]
+        o_ref[...] = s_ref[...].astype(BF16)
+
+    vmem = pl.BlockSpec(memory_space=pltpu.VMEM)
+    return pl.pallas_call(
+        kernel,
+        out_shape=jax.ShapeDtypeStruct((slots * count, LANES), BF16),
+        in_specs=[pl.BlockSpec(memory_space=pltpu.SMEM), vmem, pl.BlockSpec(memory_space=pl.ANY)],
+        out_specs=vmem,
+        scratch_shapes=[
+            pltpu.VMEM((slots * count, LANES), F32),
+            pltpu.VMEM((z_count, cores, gu_rows, LANES), BF16),
+            pltpu.SemaphoreType.DMA((z_count,)),
+        ],
+        compiler_params=pltpu.CompilerParams(vmem_limit_bytes=58 << 20),
+    )(core, grad_both, weights)
+
+
+def gathered_rows(ref, slots, count):
+    return jnp.concatenate(
+        [ref[pl.ds(i, slots, stride=count), :].astype(BF16) for i in range(count)], axis=1
+    )
+
+
+def combine_outputs(outs, hidden, out_grad, ids_t, route_t, expert_total, owners, local_count):
     tokens, width = hidden.shape
     top = ids_t.shape[0]
     count = width // LANES
     slots = expert_total * CAP
-    each = CAP * count
-
-    def kernel(r_ref, h_ref, v_ref, g_ref, m_ref, i_ref, w_ref, layer_ref, res_ref, route_ref, o_s, b_s):
-        for d in range(expert_total):
-            o_s[d * each : (d + 1) * each, :] = r_ref[d, :each, :].astype(F32)
-            b_s[d * each : (d + 1) * each, :] = r_ref[d, each:, :].astype(F32)
+
+    def kernel(r_ref, h_ref, g_ref, i_ref, w_ref, layer_ref, route_ref, both_ref, o_s):
+        o_s[...] = r_ref[...].astype(F32)
         masks = slot_masks(i_ref[...], expert_total, owners, local_count)
         eye = id_columns(i_ref[...])[1]
         routes = columns_of(w_ref[...], eye)
@@ -549,37 +598,48 @@
             weight = weight + jnp.where(masks[k], routes[:, k : k + 1], 0.0)
         hi = weight.astype(BF16)
         both = jnp.concatenate([hi, (weight - hi.astype(F32)).astype(BF16)], axis=0)
-
-        def rows_of(ref):
-            return jnp.concatenate(
-                [ref[pl.ds(i, slots, stride=count), :].astype(BF16) for i in range(count)], axis=1
-            )
-
-        hidden = h_ref[...].astype(F32)
-        grad = g_ref[...]
-        outs = rows_of(o_s)
+        both_ref[...] = both
+        outs = gathered_rows(o_s, slots, count)
         mixed = mm(both, outs, NN)
-        layer_ref[...] = (hidden + (mixed[:tokens] + mixed[tokens:])).astype(BF16)
-        dots = mm(grad, outs, NT)
+        layer_ref[...] = (h_ref[...].astype(F32) + (mixed[:tokens] + mixed[tokens:])).astype(BF16)
+        dots = mm(g_ref[...], outs, NT)
         lane = lax.broadcasted_iota(jnp.int32, (tokens, top), 1)
         route = jnp.zeros((tokens, top), F32)
         for k in range(top):
             one = jnp.sum(jnp.where(masks[k], dots, 0.0), axis=1, keepdims=True)
             route = jnp.where(lane == k, one, route)
         route_ref[...] = mm(route, eye, TN, HIGH)
-        mixed = mm(both, rows_of(b_s), NN)
+
+    return call(
+        kernel,
+        (
+            jax.ShapeDtypeStruct((tokens, width), BF16),
+            jax.ShapeDtypeStruct((top, tokens), F32),
+            jax.ShapeDtypeStruct((2 * tokens, slots), BF16),
+        ),
+        (pltpu.VMEM((slots * count, LANES), F32),),
+    )(outs, hidden, out_grad, ids_t, route_t)
+
+
+def combine_grads(grads, both, hidden, inv_rms, out_grad, moe_gain):
+    tokens, width = hidden.shape
+    count = width // LANES
+    slots = both.shape[1]
+
+    def kernel(r_ref, both_ref, h_ref, v_ref, g_ref, m_ref, res_ref, b_s):
+        b_s[...] = r_ref[...].astype(F32)
+        mixed = mm(both_ref[...], gathered_rows(b_s, slots, count), NN)
         inv = v_ref[:, 0:1]
         unit_grad = (mixed[:tokens] + mixed[tokens:]) * m_ref[...]
-        unit_rows = hidden * inv
+        unit_rows = h_ref[...].astype(F32) * inv
         mean = jnp.mean(unit_grad * unit_rows, axis=1, keepdims=True)
-        res_ref[...] = (grad.astype(F32) + inv * (unit_grad - unit_rows * mean)).astype(BF16)
-
-    shape = jax.ShapeDtypeStruct((tokens, width), BF16)
+        res_ref[...] = (g_ref[...].astype(F32) + inv * (unit_grad - unit_rows * mean)).astype(BF16)
+
     return call(
         kernel,
-        (shape, shape, jax.ShapeDtypeStruct((top, tokens), F32)),
-        (pltpu.VMEM((slots * count, LANES), F32), pltpu.VMEM((slots * count, LANES), F32)),
-    )(back, hidden, inv_rms, out_grad, moe_gain, ids_t, route_t)
+        jax.ShapeDtypeStruct((tokens, width), BF16),
+        (pltpu.VMEM((slots * count, LANES), F32),),
+    )(grads, both, hidden, inv_rms, out_grad, moe_gain)
 
 
 def ring_route(count, shift):
@@ -624,11 +684,6 @@
     last = jnp.concatenate([x_inner[-8:], bc_input[-8:]], axis=1)
     rim = lax.ppermute(last, ctx, [(i, i + 1) for i in range(ctx_count - 1)])
 
-    kept, other = pack_weights(core, gate_up_weight, down_weight)
-    swapped = lax.ppermute(other, "core", [(0, 1), (1, 0)])
-    weights = lax.all_gather(jnp.stack([kept, swapped]), "z", axis=0, tiled=False)
-    gu_rows = kept.shape[0] - ff_width
-
     folded = (out_weight.astype(F32) * norm_gain[:, None]).astype(BF16)
     half = folded.shape[0] // 2
     from_prev = lax.ppermute(folded, "y", ring_route(y_count, 1))
@@ -636,11 +691,8 @@
     far_a = lax.ppermute(from_prev[:half], "y", ring_route(y_count, 1))
     far_b = lax.ppermute(from_next[half:], "y", ring_route(y_count, -1))
 
-    sent_grads = dispatch_grads(ids_t, out_grad, expert_total, owners, local_count)
-    rim, sent_grads = lax.optimization_barrier((rim, sent_grads))
-    grads_in = lax.all_to_all(
-        sent_grads.reshape(expert_total, -1, LANES), exchange, split_axis=0, concat_axis=0, tiled=True
-    )
+    kept, other = pack_weights(core, gate_up_weight, down_weight)
+    swapped = lax.ppermute(other, "core", [(0, 1), (1, 0)])
 
     conv, held_in, sent = mixer_state(x_inner, bc_input, rim, conv_weight, bc_conv_weight, step_t, decay_t)
     reach = 4
@@ -649,17 +701,27 @@
         return lax.ppermute(value, ctx, [(i, i + distance) for i in range(ctx_count - distance)])
 
     near = [earlier(sent, d) for d in range(1, reach + 1)]
+    kept, swapped, conv = lax.optimization_barrier((kept, swapped, conv))
+    stacked = jnp.stack([kept, swapped])
+    weights = lax.all_gather(stacked, "z", axis=0, tiled=False)
+    gu_rows = kept.shape[0] - ff_width
     y_local, e_cols = mixer_rows(conv, held_in, step_t, decay_t, skip_gain, channels)
     window = join_states(near, state_size, False)
     windows = [window] + [earlier(window, d) for d in range(reach, ctx_count, reach)]
+
+    sent_grads = dispatch_grads(ids_t, out_grad, expert_total, owners, local_count)
+    grads_in = lax.all_to_all(
+        sent_grads.reshape(expert_total, -1, LANES), exchange, split_axis=0, concat_axis=0, tiled=True
+    )
+
     arriving = join_states(windows, state_size, True)
-    arriving, grads_in = lax.optimization_barrier((arriving, grads_in))
     y_at = lax.axis_index("y").astype(jnp.int32).reshape(1)
     x_at = lax.axis_index("x").astype(jnp.int32).reshape(1)
     gated = gate_rows(y_at, y_local, conv, e_cols, arriving, gate_input, heads, x_count, y_count)
     gated = [gated[0]] + [
         lax.ppermute(gated[k], "y", ring_route(y_count, k)) for k in range(1, y_count)
     ]
+    gated, grads_in = lax.optimization_barrier((gated, grads_in))
     pieces = [(folded,), (from_prev,), (far_a, far_b), (from_next,)]
     parts = project(x_at, gated, pieces, x_count)
     parts = [parts[0]] + [
@@ -671,11 +733,18 @@
     rows_in = lax.all_to_all(
         sent_rows.reshape(expert_total, -1, LANES), exchange, split_axis=0, concat_axis=0, tiled=True
     )
-    back = experts(core, rows_in.reshape(-1, LANES), grads_in.reshape(-1, LANES), weights, ff_width, gu_rows)
-    back = lax.all_to_all(back, exchange, split_axis=0, concat_axis=0, tiled=True)
-    layer, res, route = combine(
-        back, hidden, inv_rms, out_grad, moe_gain[None, :], ids_t, route_t, expert_total, owners, local_count
-    )
+    outs, grad_both = experts(
+        core, rows_in.reshape(-1, LANES), grads_in.reshape(-1, LANES), weights, ff_width, gu_rows
+    )
+    outs = lax.all_to_all(
+        outs.reshape(expert_total, -1, LANES), exchange, split_axis=0, concat_axis=0, tiled=True
+    )
+    grads = expert_inputs(core, grad_both, weights, gu_rows)
+    grads = lax.all_to_all(grads.reshape(expert_total, -1, LANES), exchange, split_axis=0, concat_axis=0, tiled=True)
+    layer, route, both = combine_outputs(
+        outs.reshape(-1, LANES), hidden, out_grad, ids_t, route_t, expert_total, owners, local_count
+    )
+    res = combine_grads(grads.reshape(-1, LANES), both, hidden, inv_rms, out_grad, moe_gain[None, :])
     return layer, res, route.T
 
 

time: 235 us -> 250 us (1.064)
  blocking collectives: 63.8 us -> 25.3 us
  waiting for transfers between devices: 43.3 us -> 77.2 us
  starting transfers between devices: 53.6 us -> 62.2 us
  Pallas kernels: 51.4 us -> 59 us
  local copies, waits for them, and re-layouts: 5.38 us -> 9.46 us
    all_to_all x1 -> x0, blocking collectives: 36.2 us -> none  [local(): lax.all_to_all(back, exchange, split_axis=0, concat_axis=0, tiled=True)]
    all_to_all x0 -> x2, waiting for transfers between devices: none -> 21.9 us  [the longest x1 13.4 us: local(): lax.all_to_all(grads.reshape(expert_total, -1, LANES), exchange, split_ax...]
    all_to_all x0 -> x2, starting transfers between devices: none -> 9.51 us  [the longest x1 5.01 us: local(): lax.all_to_all(grads.reshape(expert_total, -1, LANES), exchange, split_ax...]
    pallas_call x2 -> x4, Pallas kernels: 20.3 us -> 28.4 us  [the longest x1 11.4 us: experts(): pl.pallas_call(kernel, out_shape=(jax.ShapeDtypeStruct(rows_in.shape, BF1...]
    ppermute x7, waiting for transfers between devices: 6.11 us -> 10.6 us  [earlier(): lax.ppermute(value, ctx, [(i, i + distance) for i in range(ctx_count - di...]
    ppermute x1, waiting for transfers between devices: 19.7 us -> 23.7 us  [local(): from_prev = lax.ppermute(folded, 'y', ring_route(y_count, 1))]
    ppermute x7, starting transfers between devices: 29.3 us -> 32.4 us  [earlier(): lax.ppermute(value, ctx, [(i, i + distance) for i in range(ctx_count - di...]
    ppermute x3, waiting for transfers between devices: 9.48 us -> 12.4 us  [local(): lax.ppermute(parts[k], 'x', ring_route(x_count, k))]
  transfers between devices with their start and end apart: 21 -> 23, of which waited for: 10 -> 12; matrix products, arithmetic and copies ran while one was open for 1% -> 1% of each run, Pallas kernels for 12% -> 17%
where the time goes in v3:
time: 250 us; the launch traced here: 249 us
  waiting for transfers between devices  77.2 us (31%)
  starting transfers between devices  62.2 us (25%)
  Pallas kernels  59 us (24%)
  blocking collectives  25.3 us (10%)
  between operations  14.3 us (6%)
  local copies, waits for them, and re-layouts  9.46 us (4%)
    ppermute x7, starting transfers between devices, earlier(): lax.ppermute(value, ctx, [(i, i + distance) for i in range(ctx_count - di...  32.4 us
    all_to_all x1, blocking collectives, local(): lax.all_to_all(sent_rows.reshape(expert_total, -1, LANES), exchange, spli...  25.3 us
    ppermute x1, waiting for transfers between devices, local(): from_prev = lax.ppermute(folded, 'y', ring_route(y_count, 1))  23.7 us
    all_to_all x1, waiting for transfers between devices, local(): lax.all_to_all(grads.reshape(expert_total, -1, LANES), exchange, split_ax...  13.4 us
    ppermute x3, waiting for transfers between devices, local(): lax.ppermute(parts[k], 'x', ring_route(x_count, k))  12.4 us
    pallas_call x1, Pallas kernels, experts(): pl.pallas_call(kernel, out_shape=(jax.ShapeDtypeStruct(rows_in.shape, BF1...  11.4 us
    ppermute x7, waiting for transfers between devices, earlier(): lax.ppermute(value, ctx, [(i, i + distance) for i in range(ctx_count - di...  10.6 us
    pallas_call x1, Pallas kernels, expert_inputs(): pl.pallas_call(kernel, out_shape=jax.ShapeDtypeStruct((slots * count, LAN...  9.22 us
  transfers between devices with their start and end apart: 23, of which 12 were waited for; matrix products, arithmetic and copies ran while one was open for 1% of the time, Pallas kernels for 17%

profile of v3, /device:TPU:1, one launch (start us, length us, event | category | flops | bytes accessed | tf_op | source)
XLA Modules:
  0.0 248.7 jit_solution(15502066300040205677)
XLA Ops:
  17.8 4.9 %shard_map.185 = (bf16[1024,512]{1,0:T(8,128)(2,1)}, bf16[1024,256]{1,0:T(8,128)(2,1)}, bf16[144,256]{1,0:T(8,128)(2,1)}) custom-call(bf16[1024,256]{1,0:T(8,128)(2,1)} %x_ref.1, bf16[1024,256]{1,0:T(8,128)(2,1)} %bc_ref.1, bf16[8,512]{1,0:T(8,128)(2,1)} %copy-done.21, f32[4,256]{1,0:T(4,128)} %wx_ref.1, f32[4,256]{1,0:T(4,128)} %wb_ref.1, ...), custom_call_target="tpu_custom_call" | custom-call | tf_op jit(solution)/shard_map/pallas_call | solution.py:121
  30.8 5.5 %all-to-all-start = ((bf16[32,144,128]{2,1,0:T(8,128)(2,1)}), bf16[32,144,128]{2,1,0:T(8,128)(2,1)S(1)}, u32[]{:S(2)}, u32[]{:S(2)}) async-start(bf16[32,144,128]{2,1,0:T(8,128)(2,1)} %bitcast.23), calls=%async_computation | async-start | bytes 2359296 | tf_op jit(solution)/shard_map/all_to_all | solution.py:713
  36.4 23.7 %collective-permute-done.12.refs_5_ = bf16[256,2048]{1,0:T(8,128)(2,1)S(1)} collective-permute-done((bf16[256,2048]{1,0:T(8,128)(2,1)S(1)}, bf16[256,2048]{1,0:T(8,128)(2,1)S(1)}, u32[]{:S(2)}, u32[]{:S(2)}) %collective-permute-start.12) | collective-permute-done | bytes 1048608 | tf_op jit(solution)/shard_map/ppermute | solution.py:689
  64.8 5.4 %collective-permute-start.2 = (bf16[144,256]{1,0:T(8,128)(2,1)S(1)}, bf16[144,256]{1,0:T(8,128)(2,1)S(1)}, u32[]{:S(2)}, u32[]{:S(2)}) collective-permute-start(bf16[144,256]{1,0:T(8,128)(2,1)S(1)} %copy-done.23), channel_id=1, source_target_pairs={{0,16},{16,32},{32,48},{48,64},{64,80},{80,96},{96,112},{112,128},... | collective-permute-start | bytes 221192 | tf_op jit(solution)/shard_map/ppermute | solution.py:701
  70.2 3.5 %collective-permute-start.3 = (bf16[144,256]{1,0:T(8,128)(2,1)S(1)}, bf16[144,256]{1,0:T(8,128)(2,1)S(1)}, u32[]{:S(2)}, u32[]{:S(2)}) collective-permute-start(bf16[144,256]{1,0:T(8,128)(2,1)S(1)} %copy-done.23), channel_id=1, source_target_pairs={{0,32},{16,48},{32,64},{48,80},{64,96},{80,112},{96,128},{112,144}... | collective-permute-start | bytes 221192 | tf_op jit(solution)/shard_map/ppermute | solution.py:701
  73.8 3.7 %collective-permute-start.4 = (bf16[144,256]{1,0:T(8,128)(2,1)S(1)}, bf16[144,256]{1,0:T(8,128)(2,1)S(1)}, u32[]{:S(2)}, u32[]{:S(2)}) collective-permute-start(bf16[144,256]{1,0:T(8,128)(2,1)S(1)} %copy-done.23), channel_id=1, source_target_pairs={{0,48},{16,64},{32,80},{48,96},{64,112},{80,128},{96,144},{112,160... | collective-permute-start | bytes 221192 | tf_op jit(solution)/shard_map/ppermute | solution.py:701
  77.5 6.5 %collective-permute-start.5 = (bf16[144,256]{1,0:T(8,128)(2,1)S(1)}, bf16[144,256]{1,0:T(8,128)(2,1)S(1)}, u32[]{:S(2)}, u32[]{:S(2)}) collective-permute-start(bf16[144,256]{1,0:T(8,128)(2,1)S(1)} %copy-done.23), channel_id=1, source_target_pairs={{0,64},{16,80},{32,96},{48,112},{64,128},{80,144},{96,160},{112,17... | collective-permute-start | bytes 221192 | tf_op jit(solution)/shard_map/ppermute | solution.py:701
  89.9 5.0 %collective-permute-start.6 = (bf16[144,256]{1,0:T(8,128)(2,1)}, bf16[144,256]{1,0:T(8,128)(2,1)S(1)}, u32[]{:S(2)}, u32[]{:S(2)}) collective-permute-start(bf16[144,256]{1,0:T(8,128)(2,1)} %shard_map.187.refs_0_), channel_id=1, source_target_pairs={{0,64},{16,80},{32,96},{48,112},{64,128},{80,144},{96,160},{112,17... | collective-permute-start | bytes 221192 | tf_op jit(solution)/shard_map/ppermute | solution.py:701
  94.9 6.8 %collective-permute-start.7 = (bf16[144,256]{1,0:T(8,128)(2,1)}, bf16[144,256]{1,0:T(8,128)(2,1)S(1)}, u32[]{:S(2)}, u32[]{:S(2)}) collective-permute-start(bf16[144,256]{1,0:T(8,128)(2,1)} %shard_map.187.refs_0_), channel_id=1, source_target_pairs={{0,128},{16,144},{32,160},{48,176},{64,192},{80,208},{96,224},{112... | collective-permute-start | bytes 221192 | tf_op jit(solution)/shard_map/ppermute | solution.py:701
  105.3 5.0 %collective-permute-done.8.refs_3_ = bf16[144,256]{1,0:T(8,128)(2,1)S(1)} collective-permute-done((bf16[144,256]{1,0:T(8,128)(2,1)}, bf16[144,256]{1,0:T(8,128)(2,1)S(1)}, u32[]{:S(2)}, u32[]{:S(2)}) %collective-permute-start.8) | collective-permute-done | bytes 73760 | tf_op jit(solution)/shard_map/ppermute | solution.py:701
  112.6 4.5 %shard_map.186 = (f32[1024,256]{1,0:T(8,128)}, f32[128,128]{1,0:T(8,128)}) custom-call(f32[4]{0:T(128)} %skip_ref.1, bf16[1024,512]{1,0:T(8,128)(2,1)} %get-tuple-element.37.conv_ref.c_ref, bf16[1024,256]{1,0:T(8,128)(2,1)} %get-tuple-element.38.in_ref, f32[4,1024]{1,0:T(4,128)} %bitcast.33, f32[4,1024]{1,0:T(4,128)} %bitcast.35), custom_call_target="tpu_custom_call" | custom-call | tf_op jit(solution)/shard_map/pallas_call | solution.py:193
  121.8 4.2 %collective-permute-done.10.refs_2_ = bf16[256,256]{1,0:T(8,128)(2,1)S(1)} collective-permute-done((bf16[256,256]{1,0:T(8,128)(2,1)}, bf16[256,256]{1,0:T(8,128)(2,1)S(1)}, u32[]{:S(2)}, u32[]{:S(2)}) %collective-permute-start.10) | collective-permute-done | bytes 131104 | tf_op jit(solution)/shard_map/ppermute | solution.py:722
  130.1 4.8 %shard_map.191 = (bf16[64,2176]{1,0:T(8,128)(2,1)}, bf16[64,2176]{1,0:T(8,128)(2,1)}, bf16[64,2176]{1,0:T(8,128)(2,1)}, bf16[64,2176]{1,0:T(8,128)(2,1)}) custom-call(s32[1]{0:T(128)} %bitcast.1.at_ref, bf16[256,256]{1,0:T(8,128)(2,1)} %get-tuple-element.46.refs_0_, bf16[256,256]{1,0:T(8,128)(2,1)} %copy-done.13, bf16[256,256]{1,0:T(8,128)(2,1)} %copy-done.11, ...), custom_call_target="tpu_custom_call" | custom-call | tf_op jit(solution)/shard_map/pallas_call | solution.py:296
  137.6 6.2 %collective-permute-done.16.refs_1_ = bf16[64,2176]{1,0:T(8,128)(2,1)S(1)} collective-permute-done((bf16[64,2176]{1,0:T(8,128)(2,1)}, bf16[64,2176]{1,0:T(8,128)(2,1)S(1)}, u32[]{:S(2)}, u32[]{:S(2)}) %collective-permute-start.16) | collective-permute-done | bytes 278560 | tf_op jit(solution)/shard_map/ppermute | solution.py:728
  143.8 4.7 %collective-permute-done.17.refs_2_ = bf16[64,2176]{1,0:T(8,128)(2,1)S(1)} collective-permute-done((bf16[64,2176]{1,0:T(8,128)(2,1)}, bf16[64,2176]{1,0:T(8,128)(2,1)S(1)}, u32[]{:S(2)}, u32[]{:S(2)}) %collective-permute-start.17) | collective-permute-done | bytes 278560 | tf_op jit(solution)/shard_map/ppermute | solution.py:728
  150.7 4.0 %shard_map.192 = (bf16[4608,128]{1,0:T(8,128)(2,1)}, bf16[64,2048]{1,0:T(8,128)(2,1)}, f32[64,128]{1,0:T(8,128)}) custom-call(bf16[64,2176]{1,0:T(8,128)(2,1)} %get-tuple-element.50.refs_0_, bf16[64,2176]{1,0:T(8,128)(2,1)} %copy-done.8, bf16[64,2176]{1,0:T(8,128)(2,1)} %copy-done.9, bf16[64,2176]{1,0:T(8,128)(2,1)} %copy-done.10, bf16[64,2048]{1,0:T(8,128)(2,1)} %refs_4_.1, ...), custom_call_target="tpu_custom_call" | custom-call | tf_op jit(solution)/shard_map/pallas_call | solution.py:416
  154.7 25.3 %all_to_all.20 = bf16[32,144,128]{2,1,0:T(8,128)(2,1)} all-to-all(bf16[32,144,128]{2,1,0:T(8,128)(2,1)} %bitcast.29), channel_id=1, replica_groups=mesh['z'=8,'core'=2,'x'=4,'y'=4] {'core','x','y'}, dimensions={0} | all-to-all | bytes 2359296 | tf_op jit(solution)/shard_map/all_to_all | solution.py:733
  180.0 11.4 %shard_map.193 = (bf16[4608,128]{1,0:T(8,128)(2,1)}, bf16[288,1408]{1,0:T(8,128)(2,1)}) custom-call(s32[1]{0:T(128)} %bitcast.core_ref, bf16[4608,128]{1,0:T(8,128)(2,1)} %bitcast.27, bf16[4608,128]{1,0:T(8,128)(2,1)} %bitcast.26, bf16[8,2,2112,128]{3,2,1,0:T(8,128)(2,1)} %bitcast.20), custom_call_target="tpu_custom_call" | custom-call | tf_op jit(solution)/shard_map/pallas_call | solution.py:514
  191.4 4.5 %all-to-all-start.2 = ((bf16[32,144,128]{2,1,0:T(8,128)(2,1)}), bf16[32,144,128]{2,1,0:T(8,128)(2,1)S(1)}, u32[]{:S(2)}, u32[]{:S(2)}) async-start(bf16[32,144,128]{2,1,0:T(8,128)(2,1)} %bitcast.28), calls=%async_computation.2 | async-start | bytes 2359296 | tf_op jit(solution)/shard_map/all_to_all | solution.py:739
  195.9 9.2 %shard_map.195 = bf16[4608,128]{1,0:T(8,128)(2,1)} custom-call(s32[1]{0:T(128)} %bitcast.core_ref, bf16[288,1408]{1,0:T(8,128)(2,1)} %get-tuple-element.61.b_ref, bf16[8,2,2112,128]{3,2,1,0:T(8,128)(2,1)} %bitcast.21), custom_call_target="tpu_custom_call" | custom-call | tf_op jit(solution)/shard_map/pallas_call | solution.py:565
  205.1 8.5 %all-to-all-done.2 = bf16[32,144,128]{2,1,0:T(8,128)(2,1)S(1)} async-done(((bf16[32,144,128]{2,1,0:T(8,128)(2,1)}), bf16[32,144,128]{2,1,0:T(8,128)(2,1)S(1)}, u32[]{:S(2)}, u32[]{:S(2)}) %all-to-all-start.2) | async-done | bytes 1179680 | tf_op jit(solution)/shard_map/all_to_all | solution.py:739
  214.7 5.0 %all-to-all-start.3 = ((bf16[32,144,128]{2,1,0:T(8,128)(2,1)}), bf16[32,144,128]{2,1,0:T(8,128)(2,1)S(1)}, u32[]{:S(2)}, u32[]{:S(2)}) async-start(bf16[32,144,128]{2,1,0:T(8,128)(2,1)} %bitcast.22), calls=%async_computation.3 | async-start | bytes 2359296 | tf_op jit(solution)/shard_map/all_to_all | solution.py:743
  219.7 4.4 %shard_map.194 = (bf16[64,2048]{1,0:T(8,128)(2,1)}, f32[4,64]{1,0:T(4,128)}, bf16[128,288]{1,0:T(8,128)(2,1)}) custom-call(bf16[4608,128]{1,0:T(8,128)(2,1)} %bitcast.24, bf16[64,2048]{1,0:T(8,128)(2,1)} %get-tuple-element.59.h_ref, bf16[64,2048]{1,0:T(8,128)(2,1)} %g_ref.9, s32[4,64]{1,0:T(4,128)} %bitcast.40, f32[4,64]{1,0:T(4,128)} %bitcast.41), custom_call_target="tpu_custom_call" | custom-call | tf_op jit(solution)/shard_map/pallas_call | solution.py:613
  224.1 13.4 %all-to-all-done.3 = bf16[32,144,128]{2,1,0:T(8,128)(2,1)S(1)} async-done(((bf16[32,144,128]{2,1,0:T(8,128)(2,1)}), bf16[32,144,128]{2,1,0:T(8,128)(2,1)S(1)}, u32[]{:S(2)}, u32[]{:S(2)}) %all-to-all-start.3) | async-done | bytes 1179680 | tf_op jit(solution)/shard_map/all_to_all | solution.py:743
  (92 shorter events, 54.5 us)
Async XLA Ops:
  7.2 172.8 %all-gather.3.cloned.1.call-start = ((), (), s32[]{:S(2)}) async-start(), calls=%async_computation.4 | async-start | bytes 9732096 | tf_op jit(solution)/shard_map/all_gather | solution.py:706
  9.6 13.1 %collective-permute-start = (bf16[2112,128]{1,0:T(8,128)(2,1)}, bf16[2112,128]{1,0:T(8,128)(2,1)S(1)}, u32[]{:S(2)}, u32[]{:S(2)}) collective-permute-start(bf16[2112,128]{1,0:T(8,128)(2,1)} %get-tuple-element.35), channel_id=1, source_target_pairs={{0,16},{16,0},{1,17},{17,1},{2,18},{18,2},{3,19},{19,3},{4,20},{20... | collective-permute-start | bytes 1622024 | tf_op jit(solution)/shard_map/ppermute | solution.py:695
  14.2 3.1 %collective-permute-start.1 = (bf16[8,512]{1,0:T(8,128)(2,1)S(1)}, bf16[8,512]{1,0:T(8,128)(2,1)S(1)}, u32[]{:S(2)}, u32[]{:S(2)}) collective-permute-start(bf16[8,512]{1,0:T(8,128)(2,1)S(1)} %pad_maximum_fusion.1), channel_id=1, source_target_pairs={{0,16},{16,32},{32,48},{48,64},{64,80},{80,96},{96,112},{112,128},... | collective-permute-start | bytes 24584 | tf_op jit(solution)/shard_map/ppermute | solution.py:685
  24.6 35.4 %collective-permute-start.12 = (bf16[256,2048]{1,0:T(8,128)(2,1)S(1)}, bf16[256,2048]{1,0:T(8,128)(2,1)S(1)}, u32[]{:S(2)}, u32[]{:S(2)}) collective-permute-start(bf16[256,2048]{1,0:T(8,128)(2,1)S(1)} %multiply_convert_fusion.refs_4_), channel_id=1, source_target_pairs={{0,1},{1,2},{2,3},{3,0},{4,5},{5,6},{6,7},{7,4},{8,9},{9,10},{10,1... | collective-permute-start | bytes 3145736 | tf_op jit(solution)/shard_map/ppermute | solution.py:689
  25.5 35.7 %collective-permute-start.14 = (bf16[256,2048]{1,0:T(8,128)(2,1)S(1)}, bf16[256,2048]{1,0:T(8,128)(2,1)}, u32[]{:S(2)}, u32[]{:S(2)}) collective-permute-start(bf16[256,2048]{1,0:T(8,128)(2,1)S(1)} %multiply_convert_fusion.refs_4_), channel_id=1, source_target_pairs={{0,3},{1,0},{2,1},{3,2},{4,7},{5,4},{6,5},{7,6},{8,11},{9,8},{10,9... | collective-permute-start | bytes 3145736 | tf_op jit(solution)/shard_map/ppermute | solution.py:690
  30.8 98.4 %all-to-all-start = ((bf16[32,144,128]{2,1,0:T(8,128)(2,1)}), bf16[32,144,128]{2,1,0:T(8,128)(2,1)S(1)}, u32[]{:S(2)}, u32[]{:S(2)}) async-start(bf16[32,144,128]{2,1,0:T(8,128)(2,1)} %bitcast.23), calls=%async_computation | async-start | bytes 2359296 | tf_op jit(solution)/shard_map/all_to_all | solution.py:713
  60.0 29.8 %copy-start.4 = (bf16[256,2048]{1,0:T(8,128)(2,1)}, bf16[256,2048]{1,0:T(8,128)(2,1)S(1)}, u32[]{:S(2)}) copy-start(bf16[256,2048]{1,0:T(8,128)(2,1)S(1)} %collective-permute-done.12.refs_5_) | copy-start | bytes 3145732
  60.9 68.3 %collective-permute-start.13 = (bf16[128,2048]{1,0:T(8,128)(2,1)}, bf16[128,2048]{1,0:T(8,128)(2,1)}, u32[]{:S(2)}, u32[]{:S(2)}) collective-permute-start(bf16[128,2048]{1,0:T(8,128)(2,1)} %slice.16), channel_id=1, source_target_pairs={{0,1},{1,2},{2,3},{3,0},{4,5},{5,6},{6,7},{7,4},{8,9},{9,10},{10,1... | collective-permute-start | bytes 1572872 | tf_op jit(solution)/shard_map/ppermute | solution.py:691
  62.2 67.0 %collective-permute-start.15 = (bf16[128,2048]{1,0:T(8,128)(2,1)S(1)}, bf16[128,2048]{1,0:T(8,128)(2,1)S(1)}, u32[]{:S(2)}, u32[]{:S(2)}) collective-permute-start(bf16[128,2048]{1,0:T(8,128)(2,1)S(1)} %slice.17), channel_id=1, source_target_pairs={{0,3},{1,0},{2,1},{3,2},{4,7},{5,4},{6,5},{7,6},{8,11},{9,8},{10,9... | collective-permute-start | bytes 1572872 | tf_op jit(solution)/shard_map/ppermute | solution.py:692
  64.8 12.7 %collective-permute-start.2 = (bf16[144,256]{1,0:T(8,128)(2,1)S(1)}, bf16[144,256]{1,0:T(8,128)(2,1)S(1)}, u32[]{:S(2)}, u32[]{:S(2)}) collective-permute-start(bf16[144,256]{1,0:T(8,128)(2,1)S(1)} %copy-done.23), channel_id=1, source_target_pairs={{0,16},{16,32},{32,48},{48,64},{64,80},{80,96},{96,112},{112,128},... | collective-permute-start | bytes 221192 | tf_op jit(solution)/shard_map/ppermute | solution.py:701
  70.2 13.8 %collective-permute-start.3 = (bf16[144,256]{1,0:T(8,128)(2,1)S(1)}, bf16[144,256]{1,0:T(8,128)(2,1)S(1)}, u32[]{:S(2)}, u32[]{:S(2)}) collective-permute-start(bf16[144,256]{1,0:T(8,128)(2,1)S(1)} %copy-done.23), channel_id=1, source_target_pairs={{0,32},{16,48},{32,64},{48,80},{64,96},{80,112},{96,128},{112,144}... | collective-permute-start | bytes 221192 | tf_op jit(solution)/shard_map/ppermute | solution.py:701
  73.8 10.3 %collective-permute-start.4 = (bf16[144,256]{1,0:T(8,128)(2,1)S(1)}, bf16[144,256]{1,0:T(8,128)(2,1)S(1)}, u32[]{:S(2)}, u32[]{:S(2)}) collective-permute-start(bf16[144,256]{1,0:T(8,128)(2,1)S(1)} %copy-done.23), channel_id=1, source_target_pairs={{0,48},{16,64},{32,80},{48,96},{64,112},{80,128},{96,144},{112,160... | collective-permute-start | bytes 221192 | tf_op jit(solution)/shard_map/ppermute | solution.py:701
  77.5 10.0 %collective-permute-start.5 = (bf16[144,256]{1,0:T(8,128)(2,1)S(1)}, bf16[144,256]{1,0:T(8,128)(2,1)S(1)}, u32[]{:S(2)}, u32[]{:S(2)}) collective-permute-start(bf16[144,256]{1,0:T(8,128)(2,1)S(1)} %copy-done.23), channel_id=1, source_target_pairs={{0,64},{16,80},{32,96},{48,112},{64,128},{80,144},{96,160},{112,17... | collective-permute-start | bytes 221192 | tf_op jit(solution)/shard_map/ppermute | solution.py:701
  89.9 13.3 %collective-permute-start.6 = (bf16[144,256]{1,0:T(8,128)(2,1)}, bf16[144,256]{1,0:T(8,128)(2,1)S(1)}, u32[]{:S(2)}, u32[]{:S(2)}) collective-permute-start(bf16[144,256]{1,0:T(8,128)(2,1)} %shard_map.187.refs_0_), channel_id=1, source_target_pairs={{0,64},{16,80},{32,96},{48,112},{64,128},{80,144},{96,160},{112,17... | collective-permute-start | bytes 221192 | tf_op jit(solution)/shard_map/ppermute | solution.py:701
  94.9 10.4 %collective-permute-start.7 = (bf16[144,256]{1,0:T(8,128)(2,1)}, bf16[144,256]{1,0:T(8,128)(2,1)S(1)}, u32[]{:S(2)}, u32[]{:S(2)}) collective-permute-start(bf16[144,256]{1,0:T(8,128)(2,1)} %shard_map.187.refs_0_), channel_id=1, source_target_pairs={{0,128},{16,144},{32,160},{48,176},{64,192},{80,208},{96,224},{112... | collective-permute-start | bytes 221192 | tf_op jit(solution)/shard_map/ppermute | solution.py:701
  101.7 8.6 %collective-permute-start.8 = (bf16[144,256]{1,0:T(8,128)(2,1)}, bf16[144,256]{1,0:T(8,128)(2,1)S(1)}, u32[]{:S(2)}, u32[]{:S(2)}) collective-permute-start(bf16[144,256]{1,0:T(8,128)(2,1)} %shard_map.187.refs_0_), channel_id=1, source_target_pairs={{0,192},{16,208},{32,224},{48,240},{1,193},{17,209},{33,225},{49,2... | collective-permute-start | bytes 221192 | tf_op jit(solution)/shard_map/ppermute | solution.py:701
  120.3 5.6 %collective-permute-start.10 = (bf16[256,256]{1,0:T(8,128)(2,1)}, bf16[256,256]{1,0:T(8,128)(2,1)S(1)}, u32[]{:S(2)}, u32[]{:S(2)}) collective-permute-start(bf16[256,256]{1,0:T(8,128)(2,1)} %get-tuple-element.44), channel_id=1, source_target_pairs={{0,2},{1,3},{2,0},{3,1},{4,6},{5,7},{6,4},{7,5},{8,10},{9,11},{10,... | collective-permute-start | bytes 393224 | tf_op jit(solution)/shard_map/ppermute | solution.py:722
  120.3 5.6 %collective-permute-start.11 = (bf16[256,256]{1,0:T(8,128)(2,1)}, bf16[256,256]{1,0:T(8,128)(2,1)S(1)}, u32[]{:S(2)}, u32[]{:S(2)}) collective-permute-start(bf16[256,256]{1,0:T(8,128)(2,1)} %get-tuple-element.45), channel_id=1, source_target_pairs={{0,3},{1,0},{2,1},{3,2},{4,7},{5,4},{6,5},{7,6},{8,11},{9,8},{10,9... | collective-permute-start | bytes 393224 | tf_op jit(solution)/shard_map/ppermute | solution.py:722
  121.0 8.2 %collective-permute-start.9 = (bf16[256,256]{1,0:T(8,128)(2,1)}, bf16[256,256]{1,0:T(8,128)(2,1)S(1)}, u32[]{:S(2)}, u32[]{:S(2)}) collective-permute-start(bf16[256,256]{1,0:T(8,128)(2,1)} %get-tuple-element.43), channel_id=1, source_target_pairs={{0,1},{1,2},{2,3},{3,0},{4,5},{5,6},{6,7},{7,4},{8,9},{9,10},{10,1... | collective-permute-start | bytes 393224 | tf_op jit(solution)/shard_map/ppermute | solution.py:722
  134.9 8.8 %collective-permute-start.16 = (bf16[64,2176]{1,0:T(8,128)(2,1)}, bf16[64,2176]{1,0:T(8,128)(2,1)S(1)}, u32[]{:S(2)}, u32[]{:S(2)}) collective-permute-start(bf16[64,2176]{1,0:T(8,128)(2,1)} %get-tuple-element.51), channel_id=1, source_target_pairs={{0,4},{4,8},{8,12},{12,0},{1,5},{5,9},{9,13},{13,1},{2,6},{6,10},{... | collective-permute-start | bytes 835592 | tf_op jit(solution)/shard_map/ppermute | solution.py:728
  135.0 13.5 %collective-permute-start.17 = (bf16[64,2176]{1,0:T(8,128)(2,1)}, bf16[64,2176]{1,0:T(8,128)(2,1)S(1)}, u32[]{:S(2)}, u32[]{:S(2)}) collective-permute-start(bf16[64,2176]{1,0:T(8,128)(2,1)} %get-tuple-element.52), channel_id=1, source_target_pairs={{0,8},{4,12},{8,0},{12,4},{1,9},{5,13},{9,1},{13,5},{2,10},{6,14},... | collective-permute-start | bytes 835592 | tf_op jit(solution)/shard_map/ppermute | solution.py:728
  136.9 13.1 %collective-permute-start.18 = (bf16[64,2176]{1,0:T(8,128)(2,1)}, bf16[64,2176]{1,0:T(8,128)(2,1)S(1)}, u32[]{:S(2)}, u32[]{:S(2)}) collective-permute-start(bf16[64,2176]{1,0:T(8,128)(2,1)} %get-tuple-element.53), channel_id=1, source_target_pairs={{0,12},{4,0},{8,4},{12,8},{1,13},{5,1},{9,5},{13,9},{2,14},{6,2},{... | collective-permute-start | bytes 835592 | tf_op jit(solution)/shard_map/ppermute | solution.py:728
  191.4 22.3 %all-to-all-start.2 = ((bf16[32,144,128]{2,1,0:T(8,128)(2,1)}), bf16[32,144,128]{2,1,0:T(8,128)(2,1)S(1)}, u32[]{:S(2)}, u32[]{:S(2)}) async-start(bf16[32,144,128]{2,1,0:T(8,128)(2,1)} %bitcast.28), calls=%async_computation.2 | async-start | bytes 2359296 | tf_op jit(solution)/shard_map/all_to_all | solution.py:739
  214.7 22.8 %all-to-all-start.3 = ((bf16[32,144,128]{2,1,0:T(8,128)(2,1)}), bf16[32,144,128]{2,1,0:T(8,128)(2,1)S(1)}, u32[]{:S(2)}, u32[]{:S(2)}) async-start(bf16[32,144,128]{2,1,0:T(8,128)(2,1)} %bitcast.22), calls=%async_computation.3 | async-start | bytes 2359296 | tf_op jit(solution)/shard_map/all_to_all | solution.py:743
  (23 other events, 106.7 us)
Sparse Core Ops, SparseCore 0:
  24.0 103.9 all-gather.2

commit v4 on v2

--- a/solution.py
+++ b/solution.py
@@ -303,10 +303,33 @@
     )(x_at, *gated, *flat)
 
 
-def expert_of(row, owners, local_count):
-    dest = (row * 7282) >> 16
+def expert_of(row, expert_total, owners, local_count):
+    main = 8 * expert_total
+    dest = jnp.where(row < main, row >> 3, row - main)
+    slot = jnp.where(row < main, row & 7, 8)
     core = dest // owners
-    return local_count * (dest - core * owners) + core, row - dest * CAP
+    return local_count * (dest - core * owners) + core, slot
+
+
+def put_tiles(ref, value, dests, columns):
+    height = ref.shape[0] // dests
+    count = height // CAP
+    main = 8 * dests
+    wide = ref.reshape(dests, height, LANES)
+    for i, c in enumerate(columns):
+        part = value[:, i * LANES : (i + 1) * LANES]
+        start = 8 * c if isinstance(c, int) else pl.multiple_of(8 * c, 8)
+        wide[:, pl.ds(start, 8), :] = part[:main].reshape(dests, 8, LANES)
+        ref[pl.ds(8 * count + c, dests, stride=height), :] = part[main:]
+
+
+def take_tile(ref, dests, c):
+    height = ref.shape[0] // dests
+    count = height // CAP
+    start = 8 * c if isinstance(c, int) else pl.multiple_of(8 * c, 8)
+    wide = ref.reshape(dests, height, LANES)
+    main = wide[:, pl.ds(start, 8), :].reshape(8 * dests, LANES)
+    return jnp.concatenate([main, ref[pl.ds(8 * count + c, dests, stride=height), :]], axis=0)
 
 
 def id_columns(ids_t):
@@ -333,13 +356,15 @@
     )
     rank = mm(jnp.where(earlier, 1.0, 0.0).astype(BF16), member, NN)
     row = lax.broadcasted_iota(jnp.int32, (slots, expert_total), 0)
-    expert, _ = expert_of(row, owners, local_count)
+    expert, _ = expert_of(row, expert_total, owners, local_count)
     spreading = jnp.where(
         expert == lax.broadcasted_iota(jnp.int32, (slots, expert_total), 1), 1.0, 0.0
     ).astype(BF16)
     hit = mm(spreading, member, NT)
     rank_of = mm(spreading, rank.astype(BF16), NT)
-    _, slot = expert_of(lax.broadcasted_iota(jnp.int32, (slots, tokens), 0), owners, local_count)
+    _, slot = expert_of(
+        lax.broadcasted_iota(jnp.int32, (slots, tokens), 0), expert_total, owners, local_count
+    )
     return jnp.where(rank_of == slot.astype(F32), hit, 0.0).astype(BF16)
 
 
@@ -357,47 +382,57 @@
     )
     rank = mm(jnp.where(earlier, 1.0, 0.0).astype(BF16), member, NN)
     row = lax.broadcasted_iota(jnp.int32, (expert_total, slots), 1)
-    expert, _ = expert_of(row, owners, local_count)
+    expert, _ = expert_of(row, expert_total, owners, local_count)
     spreading = jnp.where(
         expert == lax.broadcasted_iota(jnp.int32, (expert_total, slots), 0), 1.0, 0.0
     ).astype(BF16)
     rank_of = mm(rank.astype(BF16), spreading, NN)
-    expert, slot = expert_of(lax.broadcasted_iota(jnp.int32, (tokens, slots), 1), owners, local_count)
+    expert, slot = expert_of(
+        lax.broadcasted_iota(jnp.int32, (tokens, slots), 1), expert_total, owners, local_count
+    )
     fits = rank_of == slot.astype(F32)
     return [fits & (expert == ids[:, k : k + 1]) for k in range(top)]
-
-
-def to_tiles(scratch, rows, value, first=0):
-    count = scratch.shape[0] // rows
-    for i in range(value.shape[1] // LANES):
-        scratch[pl.ds(first + i, rows, stride=count), :] = value[:, i * LANES : (i + 1) * LANES]
 
 
 def dispatch_grads(ids, out_grad, expert_total, owners, local_count):
     _, width = out_grad.shape
     slots = expert_total * CAP
     count = width // LANES
-
-    def kernel(i_ref, g_ref, o_ref, s_ref):
+    each = CAP * count
+
+    def kernel(i_ref, g_ref, o_hbm, s_ref, b_ref, sem):
         pick = routing_rows(i_ref[...], expert_total, owners, local_count)
-        to_tiles(s_ref, slots, mm(pick, g_ref[...], NN))
-        o_ref[...] = s_ref[...].astype(BF16)
-
-    return call(
-        kernel,
-        jax.ShapeDtypeStruct((slots * count, LANES), BF16),
-        (pltpu.VMEM((slots * count, LANES), F32),),
+        put_tiles(s_ref, mm(pick, g_ref[...], NN), expert_total, range(count))
+        b_ref[...] = s_ref[...].astype(BF16).reshape(expert_total, each, LANES)
+        copy = pltpu.make_async_copy(b_ref, o_hbm.at[:, pl.ds(each, each), :], sem.at[0])
+        copy.start()
+        copy.wait()
+
+    vmem = pl.BlockSpec(memory_space=pltpu.VMEM)
+    return pl.pallas_call(
+        kernel,
+        out_shape=jax.ShapeDtypeStruct((expert_total, 2 * each, LANES), BF16),
+        in_specs=[vmem, vmem],
+        out_specs=pl.BlockSpec(memory_space=pl.ANY),
+        scratch_shapes=[
+            pltpu.VMEM((slots * count, LANES), F32),
+            pltpu.VMEM((expert_total, each, LANES), BF16),
+            pltpu.SemaphoreType.DMA((1,)),
+        ],
+        compiler_params=pltpu.CompilerParams(vmem_limit_bytes=58 << 20),
     )(ids, out_grad)
 
 
-def normalise(parts, residual, moe_gain, ids, inner_total, expert_total, owners, local_count):
+def normalise(buffer, parts, residual, moe_gain, ids, inner_total, expert_total, owners, local_count):
     tokens, width = residual.shape
     slots = expert_total * CAP
     count = width // LANES
     sources = len(parts)
 
+    each = CAP * count
+
     def kernel(*refs):
-        r_ref, m_ref, i_ref, o_ref, h_ref, v_ref, s_ref = refs[sources:]
+        r_ref, m_ref, i_ref, _, o_hbm, h_ref, v_ref, s_ref, b_ref, sem = refs[sources:]
         summed = refs[0][...].astype(F32)
         for p_ref in refs[1:sources]:
             summed = summed + p_ref[...].astype(F32)
@@ -410,18 +445,31 @@
         v_ref[...] = jnp.broadcast_to(inv, (tokens, LANES))
         normed = (hidden * inv * m_ref[...]).astype(BF16)
         pick = routing_rows(i_ref[...], expert_total, owners, local_count)
-        to_tiles(s_ref, slots, mm(pick, normed, NN))
-        o_ref[...] = s_ref[...].astype(BF16)
-
-    return call(
-        kernel,
-        (
-            jax.ShapeDtypeStruct((slots * count, LANES), BF16),
+        put_tiles(s_ref, mm(pick, normed, NN), expert_total, range(count))
+        b_ref[...] = s_ref[...].astype(BF16).reshape(expert_total, each, LANES)
+        copy = pltpu.make_async_copy(b_ref, o_hbm.at[:, pl.ds(0, each), :], sem.at[0])
+        copy.start()
+        copy.wait()
+
+    vmem = pl.BlockSpec(memory_space=pltpu.VMEM)
+    anywhere = pl.BlockSpec(memory_space=pl.ANY)
+    return pl.pallas_call(
+        kernel,
+        out_shape=(
+            jax.ShapeDtypeStruct(buffer.shape, BF16),
             jax.ShapeDtypeStruct((tokens, width), BF16),
             jax.ShapeDtypeStruct((tokens, LANES), F32),
         ),
-        (pltpu.VMEM((slots * count, LANES), F32),),
-    )(*parts, residual, moe_gain, ids)
+        in_specs=[vmem] * (sources + 3) + [anywhere],
+        out_specs=(anywhere, vmem, vmem),
+        scratch_shapes=[
+            pltpu.VMEM((slots * count, LANES), F32),
+            pltpu.VMEM((expert_total, each, LANES), BF16),
+            pltpu.SemaphoreType.DMA((1,)),
+        ],
+        input_output_aliases={sources + 3: 0},
+        compiler_params=pltpu.CompilerParams(vmem_limit_bytes=58 << 20),
+    )(*parts, residual, moe_gain, ids, buffer)
 
 
 def pack_weights(core, gate_up, down):
@@ -447,26 +495,26 @@
     )(core, gate_up, down)
 
 
-def experts(core, rows_in, grads_in, weights, ff_width, gu_rows):
+def experts(core, rows_in, weights, ff_width, gu_rows):
     z_count, cores, _, _ = weights.shape
     count = z_count * cores
-    slots = rows_in.shape[0] // count
-    dests = slots // CAP
+    dests = rows_in.shape[0]
+    slots = dests * CAP
     ff_tiles = 2 * ff_width // LANES
     block = gu_rows // ff_tiles
     each = CAP * count
 
-    def kernel(core_ref, x_ref, g_ref, w_hbm, o_ref, x_s, g_s, xb_s, gb_s, w_ref, sems):
+    def kernel(core_ref, x_ref, w_hbm, o_ref, x_s, g_s, xb_s, gb_s, w_ref, sems):
         copies = [pltpu.make_async_copy(w_hbm.at[z], w_ref.at[z], sems.at[z]) for z in range(z_count)]
         for copy in copies:
             copy.start()
         core = core_ref[0]
-        x_s[...] = x_ref[...].astype(F32)
-        g_s[...] = g_ref[...].astype(F32)
+        x_s[...] = x_ref[:, :each, :].astype(F32).reshape(dests * each, LANES)
+        g_s[...] = x_ref[:, each:, :].astype(F32).reshape(dests * each, LANES)
         order = [(z, s, z * cores + (core if s == 0 else 1 - core)) for z in range(z_count) for s in range(cores)]
         for i, (z, s, c) in enumerate(order):
-            xb_s[:, i * LANES : (i + 1) * LANES] = x_s[pl.ds(c, slots, stride=count), :].astype(BF16)
-            gb_s[:, i * LANES : (i + 1) * LANES] = g_s[pl.ds(c, slots, stride=count), :].astype(BF16)
+            xb_s[:, i * LANES : (i + 1) * LANES] = take_tile(x_s, dests, c).astype(BF16)
+            gb_s[:, i * LANES : (i + 1) * LANES] = take_tile(g_s, dests, c).astype(BF16)
 
         def tile(z, s, i):
             return w_ref[z, s, i * block : (i + 1) * block, :]
@@ -504,30 +552,28 @@
                 [jnp.concatenate([tile(z, s, i) for i in range(ff_tiles)], axis=1) for s in range(cores)], axis=0
             )
             grad = mm(grad_both, rhs, NT)
-            for s in range(cores):
-                c = z * cores + (core if s == 0 else 1 - core)
-                x_s[pl.ds(c, slots, stride=count), :] = out[:, s * LANES : (s + 1) * LANES]
-                g_s[pl.ds(c, slots, stride=count), :] = grad[:, s * LANES : (s + 1) * LANES]
-        for d in range(dests):
-            o_ref[d, :each, :] = x_s[d * each : (d + 1) * each, :].astype(BF16)
-            o_ref[d, each:, :] = g_s[d * each : (d + 1) * each, :].astype(BF16)
+            places = [z * cores + core, z * cores + 1 - core]
+            put_tiles(x_s, out, dests, places)
+            put_tiles(g_s, grad, dests, places)
+        o_ref[:, :each, :] = x_s[...].astype(BF16).reshape(dests, each, LANES)
+        o_ref[:, each:, :] = g_s[...].astype(BF16).reshape(dests, each, LANES)
 
     vmem = pl.BlockSpec(memory_space=pltpu.VMEM)
     return pl.pallas_call(
         kernel,
         out_shape=jax.ShapeDtypeStruct((dests, 2 * each, LANES), BF16),
-        in_specs=[pl.BlockSpec(memory_space=pltpu.SMEM), vmem, vmem, pl.BlockSpec(memory_space=pl.ANY)],
+        in_specs=[pl.BlockSpec(memory_space=pltpu.SMEM), vmem, pl.BlockSpec(memory_space=pl.ANY)],
         out_specs=vmem,
         scratch_shapes=[
-            pltpu.VMEM(rows_in.shape, F32),
-            pltpu.VMEM(rows_in.shape, F32),
+            pltpu.VMEM((dests * each, LANES), F32),
+            pltpu.VMEM((dests * each, LANES), F32),
             pltpu.VMEM((slots, count * LANES), BF16),
             pltpu.VMEM((slots, count * LANES), BF16),
             pltpu.VMEM(weights.shape, BF16),
             pltpu.SemaphoreType.DMA((z_count,)),
         ],
         compiler_params=pltpu.CompilerParams(vmem_limit_bytes=58 << 20),
-    )(core, rows_in, grads_in, weights)
+    )(core, rows_in, weights)
 
 
 def combine(back, hidden, inv_rms, out_grad, moe_gain, ids_t, route_t, expert_total, owners, local_count):
@@ -538,9 +584,8 @@
     each = CAP * count
 
     def kernel(r_ref, h_ref, v_ref, g_ref, m_ref, i_ref, w_ref, layer_ref, res_ref, route_ref, o_s, b_s):
-        for d in range(expert_total):
-            o_s[d * each : (d + 1) * each, :] = r_ref[d, :each, :].astype(F32)
-            b_s[d * each : (d + 1) * each, :] = r_ref[d, each:, :].astype(F32)
+        o_s[...] = r_ref[:, :each, :].astype(F32).reshape(slots * count, LANES)
+        b_s[...] = r_ref[:, each:, :].astype(F32).reshape(slots * count, LANES)
         masks = slot_masks(i_ref[...], expert_total, owners, local_count)
         eye = id_columns(i_ref[...])[1]
         routes = columns_of(w_ref[...], eye)
@@ -552,7 +597,7 @@
 
         def rows_of(ref):
             return jnp.concatenate(
-                [ref[pl.ds(i, slots, stride=count), :].astype(BF16) for i in range(count)], axis=1
+                [take_tile(ref, expert_total, i).astype(BF16) for i in range(count)], axis=1
             )
 
         hidden = h_ref[...].astype(F32)
@@ -624,11 +669,6 @@
     last = jnp.concatenate([x_inner[-8:], bc_input[-8:]], axis=1)
     rim = lax.ppermute(last, ctx, [(i, i + 1) for i in range(ctx_count - 1)])
 
-    kept, other = pack_weights(core, gate_up_weight, down_weight)
-    swapped = lax.ppermute(other, "core", [(0, 1), (1, 0)])
-    weights = lax.all_gather(jnp.stack([kept, swapped]), "z", axis=0, tiled=False)
-    gu_rows = kept.shape[0] - ff_width
-
     folded = (out_weight.astype(F32) * norm_gain[:, None]).astype(BF16)
     half = folded.shape[0] // 2
     from_prev = lax.ppermute(folded, "y", ring_route(y_count, 1))
@@ -636,11 +676,8 @@
     far_a = lax.ppermute(from_prev[:half], "y", ring_route(y_count, 1))
     far_b = lax.ppermute(from_next[half:], "y", ring_route(y_count, -1))
 
-    sent_grads = dispatch_grads(ids_t, out_grad, expert_total, owners, local_count)
-    rim, sent_grads = lax.optimization_barrier((rim, sent_grads))
-    grads_in = lax.all_to_all(
-        sent_grads.reshape(expert_total, -1, LANES), exchange, split_axis=0, concat_axis=0, tiled=True
-    )
+    kept, other = pack_weights(core, gate_up_weight, down_weight)
+    swapped = lax.ppermute(other, "core", [(0, 1), (1, 0)])
 
     conv, held_in, sent = mixer_state(x_inner, bc_input, rim, conv_weight, bc_conv_weight, step_t, decay_t)
     reach = 4
@@ -649,11 +686,16 @@
         return lax.ppermute(value, ctx, [(i, i + distance) for i in range(ctx_count - distance)])
 
     near = [earlier(sent, d) for d in range(1, reach + 1)]
+    kept, swapped, conv = lax.optimization_barrier((kept, swapped, conv))
+    stacked = jnp.stack([kept, swapped])
+    weights = lax.all_gather(stacked, "z", axis=0, tiled=False)
+    gu_rows = kept.shape[0] - ff_width
     y_local, e_cols = mixer_rows(conv, held_in, step_t, decay_t, skip_gain, channels)
     window = join_states(near, state_size, False)
     windows = [window] + [earlier(window, d) for d in range(reach, ctx_count, reach)]
+
+    buffer = dispatch_grads(ids_t, out_grad, expert_total, owners, local_count)
     arriving = join_states(windows, state_size, True)
-    arriving, grads_in = lax.optimization_barrier((arriving, grads_in))
     y_at = lax.axis_index("y").astype(jnp.int32).reshape(1)
     x_at = lax.axis_index("x").astype(jnp.int32).reshape(1)
     gated = gate_rows(y_at, y_local, conv, e_cols, arriving, gate_input, heads, x_count, y_count)
@@ -666,12 +708,10 @@
         lax.ppermute(parts[k], "x", ring_route(x_count, k)) for k in range(1, x_count)
     ]
     sent_rows, hidden, inv_rms = normalise(
-        parts, residual, moe_gain[None, :], ids_t, channels * owners, expert_total, owners, local_count
-    )
-    rows_in = lax.all_to_all(
-        sent_rows.reshape(expert_total, -1, LANES), exchange, split_axis=0, concat_axis=0, tiled=True
-    )
-    back = experts(core, rows_in.reshape(-1, LANES), grads_in.reshape(-1, LANES), weights, ff_width, gu_rows)
+        buffer, parts, residual, moe_gain[None, :], ids_t, channels * owners, expert_total, owners, local_count
+    )
+    rows_in = lax.all_to_all(sent_rows, exchange, split_axis=0, concat_axis=0, tiled=True)
+    back = experts(core, rows_in, weights, ff_width, gu_rows)
     back = lax.all_to_all(back, exchange, split_axis=0, concat_axis=0, tiled=True)
     layer, res, route = combine(
         back, hidden, inv_rms, out_grad, moe_gain[None, :], ids_t, route_t, expert_total, owners, local_count

time: 235 us -> 244 us (1.038)
  blocking collectives: 63.8 us -> 74.3 us
  starting transfers between devices: 53.6 us -> 47.3 us
  waiting for transfers between devices: 43.3 us -> 49.1 us
    all_to_all x1, blocking collectives: 27.6 us -> 37.9 us  [local(): lax.all_to_all(sent_rows, exchange, split_axis=0, concat_axis=0, tiled=True)]
    all_to_all x1 -> x0, starting transfers between devices: 6 us -> none  [local(): lax.all_to_all(sent_grads.reshape(expert_total, -1, LANES), exchange, spl...]
    ppermute x7, waiting for transfers between devices: 6.11 us -> 10.6 us  [earlier(): lax.ppermute(value, ctx, [(i, i + distance) for i in range(ctx_count - di...]
    ppermute x1, waiting for transfers between devices: 19.7 us -> 23.2 us  [local(): from_prev = lax.ppermute(folded, 'y', ring_route(y_count, 1))]
  transfers between devices with their start and end apart: 21 -> 20, of which waited for: 10 -> 11; matrix products, arithmetic and copies ran while one was open for 1% -> 1% of each run, Pallas kernels for 12% -> 12%
where the time goes in v4:
time: 244 us; the launch traced here: 243 us
  blocking collectives  74.3 us (30%)
  waiting for transfers between devices  49.1 us (20%)
  Pallas kernels  49 us (20%)
  starting transfers between devices  47.3 us (19%)
  between operations  14.3 us (6%)
  local copies, waits for them, and re-layouts  6.53 us (3%)
    all_to_all x1, blocking collectives, local(): lax.all_to_all(sent_rows, exchange, split_axis=0, concat_axis=0, tiled=True)  37.9 us
    all_to_all x1, blocking collectives, local(): lax.all_to_all(back, exchange, split_axis=0, concat_axis=0, tiled=True)  36.4 us
    ppermute x7, starting transfers between devices, earlier(): lax.ppermute(value, ctx, [(i, i + distance) for i in range(ctx_count - di...  28.8 us
    ppermute x1, waiting for transfers between devices, local(): from_prev = lax.ppermute(folded, 'y', ring_route(y_count, 1))  23.2 us
    pallas_call x1, Pallas kernels, experts(): pl.pallas_call(kernel, out_shape=jax.ShapeDtypeStruct((dests, 2 * each, L...  13.2 us
    ppermute x7, waiting for transfers between devices, earlier(): lax.ppermute(value, ctx, [(i, i + distance) for i in range(ctx_count - di...  10.6 us
    ppermute x3, waiting for transfers between devices, local(): lax.ppermute(parts[k], 'x', ring_route(x_count, k))  7.63 us
    ppermute x3, waiting for transfers between devices, local(): lax.ppermute(gated[k], 'y', ring_route(y_count, k))  6.49 us
  transfers between devices with their start and end apart: 20, of which 11 were waited for; matrix products, arithmetic and copies ran while one was open for 1% of the time, Pallas kernels for 12%

profile of v4, /device:TPU:1, one launch (start us, length us, event | category | flops | bytes accessed | tf_op | source)
XLA Modules:
  0.0 242.9 jit_solution(17938686537331637106)
XLA Ops:
  9.6 3.2 %collective-permute-start = (bf16[2112,128]{1,0:T(8,128)(2,1)}, bf16[2112,128]{1,0:T(8,128)(2,1)S(1)}, u32[]{:S(2)}, u32[]{:S(2)}) collective-permute-start(bf16[2112,128]{1,0:T(8,128)(2,1)} %get-tuple-element.28), channel_id=1, source_target_pairs={{0,16},{16,0},{1,17},{17,1},{2,18},{18,2},{3,19},{19,3},{4,20},{20... | collective-permute-start | bytes 1622024 | tf_op jit(solution)/shard_map/ppermute | solution.py:680
  17.8 5.0 %shard_map.185 = (bf16[1024,512]{1,0:T(8,128)(2,1)}, bf16[1024,256]{1,0:T(8,128)(2,1)}, bf16[144,256]{1,0:T(8,128)(2,1)}) custom-call(bf16[1024,256]{1,0:T(8,128)(2,1)} %x_ref.1, bf16[1024,256]{1,0:T(8,128)(2,1)} %bc_ref.1, bf16[8,512]{1,0:T(8,128)(2,1)} %copy-done.17, f32[4,256]{1,0:T(4,128)} %wx_ref.1, f32[4,256]{1,0:T(4,128)} %wb_ref.1, ...), custom_call_target="tpu_custom_call" | custom-call | tf_op jit(solution)/shard_map/pallas_call | solution.py:121
  28.1 23.2 %collective-permute-done.12.refs_5_ = bf16[256,2048]{1,0:T(8,128)(2,1)S(1)} collective-permute-done((bf16[256,2048]{1,0:T(8,128)(2,1)S(1)}, bf16[256,2048]{1,0:T(8,128)(2,1)S(1)}, u32[]{:S(2)}, u32[]{:S(2)}) %collective-permute-start.12) | collective-permute-done | bytes 1048608 | tf_op jit(solution)/shard_map/ppermute | solution.py:674
  53.1 2.7 %collective-permute-start.15 = (bf16[128,2048]{1,0:T(8,128)(2,1)}, bf16[128,2048]{1,0:T(8,128)(2,1)}, u32[]{:S(2)}, u32[]{:S(2)}) collective-permute-start(bf16[128,2048]{1,0:T(8,128)(2,1)} %slice.17), channel_id=1, source_target_pairs={{0,3},{1,0},{2,1},{3,2},{4,7},{5,4},{6,5},{7,6},{8,11},{9,8},{10,9... | collective-permute-start | bytes 1572872 | tf_op jit(solution)/shard_map/ppermute | solution.py:677
  55.7 4.4 %collective-permute-start.2 = (bf16[144,256]{1,0:T(8,128)(2,1)S(1)}, bf16[144,256]{1,0:T(8,128)(2,1)S(1)}, u32[]{:S(2)}, u32[]{:S(2)}) collective-permute-start(bf16[144,256]{1,0:T(8,128)(2,1)S(1)} %copy-done.19), channel_id=1, source_target_pairs={{0,16},{16,32},{32,48},{48,64},{64,80},{80,96},{96,112},{112,128},... | collective-permute-start | bytes 221192 | tf_op jit(solution)/shard_map/ppermute | solution.py:686
  60.1 3.5 %collective-permute-start.3 = (bf16[144,256]{1,0:T(8,128)(2,1)S(1)}, bf16[144,256]{1,0:T(8,128)(2,1)S(1)}, u32[]{:S(2)}, u32[]{:S(2)}) collective-permute-start(bf16[144,256]{1,0:T(8,128)(2,1)S(1)} %copy-done.19), channel_id=1, source_target_pairs={{0,32},{16,48},{32,64},{48,80},{64,96},{80,112},{96,128},{112,144}... | collective-permute-start | bytes 221192 | tf_op jit(solution)/shard_map/ppermute | solution.py:686
  63.7 4.7 %collective-permute-start.4 = (bf16[144,256]{1,0:T(8,128)(2,1)S(1)}, bf16[144,256]{1,0:T(8,128)(2,1)S(1)}, u32[]{:S(2)}, u32[]{:S(2)}) collective-permute-start(bf16[144,256]{1,0:T(8,128)(2,1)S(1)} %copy-done.19), channel_id=1, source_target_pairs={{0,48},{16,64},{32,80},{48,96},{64,112},{80,128},{96,144},{112,160... | collective-permute-start | bytes 221192 | tf_op jit(solution)/shard_map/ppermute | solution.py:686
  68.4 3.2 %collective-permute-start.5 = (bf16[144,256]{1,0:T(8,128)(2,1)S(1)}, bf16[144,256]{1,0:T(8,128)(2,1)S(1)}, u32[]{:S(2)}, u32[]{:S(2)}) collective-permute-start(bf16[144,256]{1,0:T(8,128)(2,1)S(1)} %copy-done.19), channel_id=1, source_target_pairs={{0,64},{16,80},{32,96},{48,112},{64,128},{80,144},{96,160},{112,17... | collective-permute-start | bytes 221192 | tf_op jit(solution)/shard_map/ppermute | solution.py:686
  72.0 3.1 %collective-permute-done.5.refs_3_ = bf16[144,256]{1,0:T(8,128)(2,1)S(1)} collective-permute-done((bf16[144,256]{1,0:T(8,128)(2,1)S(1)}, bf16[144,256]{1,0:T(8,128)(2,1)S(1)}, u32[]{:S(2)}, u32[]{:S(2)}) %collective-permute-start.5) | collective-permute-done | bytes 73760 | tf_op jit(solution)/shard_map/ppermute | solution.py:686
  77.5 5.0 %collective-permute-start.6 = (bf16[144,256]{1,0:T(8,128)(2,1)}, bf16[144,256]{1,0:T(8,128)(2,1)S(1)}, u32[]{:S(2)}, u32[]{:S(2)}) collective-permute-start(bf16[144,256]{1,0:T(8,128)(2,1)} %shard_map.187.refs_0_), channel_id=1, source_target_pairs={{0,64},{16,80},{32,96},{48,112},{64,128},{80,144},{96,160},{112,17... | collective-permute-start | bytes 221192 | tf_op jit(solution)/shard_map/ppermute | solution.py:686
  82.5 6.7 %collective-permute-start.7 = (bf16[144,256]{1,0:T(8,128)(2,1)}, bf16[144,256]{1,0:T(8,128)(2,1)S(1)}, u32[]{:S(2)}, u32[]{:S(2)}) collective-permute-start(bf16[144,256]{1,0:T(8,128)(2,1)} %shard_map.187.refs_0_), channel_id=1, source_target_pairs={{0,128},{16,144},{32,160},{48,176},{64,192},{80,208},{96,224},{112... | collective-permute-start | bytes 221192 | tf_op jit(solution)/shard_map/ppermute | solution.py:686
  90.5 2.4 %collective-permute-done.7.refs_2_ = bf16[144,256]{1,0:T(8,128)(2,1)S(1)} collective-permute-done((bf16[144,256]{1,0:T(8,128)(2,1)}, bf16[144,256]{1,0:T(8,128)(2,1)S(1)}, u32[]{:S(2)}, u32[]{:S(2)}) %collective-permute-start.7) | collective-permute-done | bytes 73760 | tf_op jit(solution)/shard_map/ppermute | solution.py:686
  92.9 4.7 %collective-permute-done.8.refs_3_ = bf16[144,256]{1,0:T(8,128)(2,1)S(1)} collective-permute-done((bf16[144,256]{1,0:T(8,128)(2,1)}, bf16[144,256]{1,0:T(8,128)(2,1)S(1)}, u32[]{:S(2)}, u32[]{:S(2)}) %collective-permute-start.8) | collective-permute-done | bytes 73760 | tf_op jit(solution)/shard_map/ppermute | solution.py:686
  99.9 4.4 %shard_map.186 = (f32[1024,256]{1,0:T(8,128)}, f32[128,128]{1,0:T(8,128)}) custom-call(f32[4]{0:T(128)} %skip_ref.1, bf16[1024,512]{1,0:T(8,128)(2,1)} %get-tuple-element.30.conv_ref.c_ref, bf16[1024,256]{1,0:T(8,128)(2,1)} %get-tuple-element.31.in_ref, f32[4,1024]{1,0:T(4,128)} %bitcast.16, f32[4,1024]{1,0:T(4,128)} %bitcast.18), custom_call_target="tpu_custom_call" | custom-call | tf_op jit(solution)/shard_map/pallas_call | solution.py:193
  104.3 3.3 %shard_map.189 = (bf16[256,256]{1,0:T(8,128)(2,1)}, bf16[256,256]{1,0:T(8,128)(2,1)}, bf16[256,256]{1,0:T(8,128)(2,1)}, bf16[256,256]{1,0:T(8,128)(2,1)}) custom-call(s32[1]{0:T(128)} %bitcast.2.at_ref, f32[1024,256]{1,0:T(8,128)} %get-tuple-element.32.y_ref, bf16[1024,512]{1,0:T(8,128)(2,1)} %get-tuple-element.30.conv_ref.c_ref, ...), custom_call_target="tpu_custom_call" | custom-call | tf_op jit(solution)/shard_map/pallas_call | solution.py:253
  110.1 3.1 %collective-permute-done.10.refs_2_ = bf16[256,256]{1,0:T(8,128)(2,1)S(1)} collective-permute-done((bf16[256,256]{1,0:T(8,128)(2,1)}, bf16[256,256]{1,0:T(8,128)(2,1)S(1)}, u32[]{:S(2)}, u32[]{:S(2)}) %collective-permute-start.10) | collective-permute-done | bytes 131104 | tf_op jit(solution)/shard_map/ppermute | solution.py:703
  117.2 4.9 %shard_map.190 = (bf16[64,2176]{1,0:T(8,128)(2,1)}, bf16[64,2176]{1,0:T(8,128)(2,1)}, bf16[64,2176]{1,0:T(8,128)(2,1)}, bf16[64,2176]{1,0:T(8,128)(2,1)}) custom-call(s32[1]{0:T(128)} %bitcast.1.at_ref, bf16[256,256]{1,0:T(8,128)(2,1)} %get-tuple-element.35.refs_0_, bf16[256,256]{1,0:T(8,128)(2,1)} %copy-done.9, bf16[256,256]{1,0:T(8,128)(2,1)} %copy-done.7, ...), custom_call_target="tpu_custom_call" | custom-call | tf_op jit(solution)/shard_map/pallas_call | solution.py:296
  127.6 3.0 %shard_map.191.refs_7_ = bf16[32,288,128]{2,1,0:T(8,128)(2,1)} custom-call(s32[4,64]{1,0:T(4,128)} %bitcast.21, bf16[64,2048]{1,0:T(8,128)(2,1)} %g_ref.7), custom_call_target="tpu_custom_call" | custom-call | tf_op jit(solution)/shard_map/pallas_call | solution.py:412
  131.2 7.1 %collective-permute-done.17.refs_2_ = bf16[64,2176]{1,0:T(8,128)(2,1)S(1)} collective-permute-done((bf16[64,2176]{1,0:T(8,128)(2,1)}, bf16[64,2176]{1,0:T(8,128)(2,1)S(1)}, u32[]{:S(2)}, u32[]{:S(2)}) %collective-permute-start.17) | collective-permute-done | bytes 278560 | tf_op jit(solution)/shard_map/ppermute | solution.py:708
  139.1 4.3 %shard_map.192 = (bf16[32,288,128]{2,1,0:T(8,128)(2,1)}, bf16[64,2048]{1,0:T(8,128)(2,1)}, f32[64,128]{1,0:T(8,128)}) custom-call(bf16[64,2176]{1,0:T(8,128)(2,1)} %get-tuple-element.39.refs_0_, bf16[64,2176]{1,0:T(8,128)(2,1)} %copy-done.4, bf16[64,2176]{1,0:T(8,128)(2,1)} %copy-done.5, ...), custom_call_target="tpu_custom_call", output_to_operand_aliasing={{0}: (7, {})} | custom-call | tf_op jit(solution)/shard_map/pallas_call | solution.py:456
  143.4 37.9 %all_to_all.10.x_ref = bf16[32,288,128]{2,1,0:T(8,128)(2,1)} all-to-all(bf16[32,288,128]{2,1,0:T(8,128)(2,1)} %get-tuple-element.43), channel_id=1, replica_groups=mesh['z'=8,'core'=2,'x'=4,'y'=4] {'core','x','y'}, dimensions={0} | all-to-all | bytes 4718592 | tf_op jit(solution)/shard_map/all_to_all | solution.py:713
  181.3 13.2 %shard_map.193 = bf16[32,288,128]{2,1,0:T(8,128)(2,1)} custom-call(s32[1]{0:T(128)} %bitcast.core_ref, bf16[32,288,128]{2,1,0:T(8,128)(2,1)} %all_to_all.10.x_ref, bf16[8,2,2112,128]{3,2,1,0:T(8,128)(2,1)} %bitcast.12), custom_call_target="tpu_custom_call" | custom-call | tf_op jit(solution)/shard_map/pallas_call | solution.py:562
  194.5 36.4 %all_to_all.11.r_ref = bf16[32,288,128]{2,1,0:T(8,128)(2,1)} all-to-all(bf16[32,288,128]{2,1,0:T(8,128)(2,1)} %shard_map.193), channel_id=1, replica_groups=mesh['z'=8,'core'=2,'x'=4,'y'=4] {'core','x','y'}, dimensions={0} | all-to-all | bytes 4718592 | tf_op jit(solution)/shard_map/all_to_all | solution.py:715
  230.9 5.1 %shard_map.194 = (bf16[64,2048]{1,0:T(8,128)(2,1)}, bf16[64,2048]{1,0:T(8,128)(2,1)}, f32[4,64]{1,0:T(4,128)}) custom-call(bf16[32,288,128]{2,1,0:T(8,128)(2,1)} %all_to_all.11.r_ref, bf16[64,2048]{1,0:T(8,128)(2,1)} %get-tuple-element.46.h_ref, f32[64,128]{1,0:T(8,128)} %get-tuple-element.47.v_ref, bf16[64,2048]{1,0:T(8,128)(2,1)} %g_ref.7, ...), custom_call_target="tpu_custom_call" | custom-call | tf_op jit(solution)/shard_map/pallas_call | solution.py:623
  (77 shorter events, 34.1 us)
Async XLA Ops:
  7.2 174.1 %all-gather.3.cloned.1.call-start = ((), (), s32[]{:S(2)}) async-start(), calls=%async_computation.2 | async-start | bytes 9732096 | tf_op jit(solution)/shard_map/all_gather | solution.py:691
  9.6 13.3 %collective-permute-start = (bf16[2112,128]{1,0:T(8,128)(2,1)}, bf16[2112,128]{1,0:T(8,128)(2,1)S(1)}, u32[]{:S(2)}, u32[]{:S(2)}) collective-permute-start(bf16[2112,128]{1,0:T(8,128)(2,1)} %get-tuple-element.28), channel_id=1, source_target_pairs={{0,16},{16,0},{1,17},{17,1},{2,18},{18,2},{3,19},{19,3},{4,20},{20... | collective-permute-start | bytes 1622024 | tf_op jit(solution)/shard_map/ppermute | solution.py:680
  14.2 3.1 %collective-permute-start.1 = (bf16[8,512]{1,0:T(8,128)(2,1)S(1)}, bf16[8,512]{1,0:T(8,128)(2,1)S(1)}, u32[]{:S(2)}, u32[]{:S(2)}) collective-permute-start(bf16[8,512]{1,0:T(8,128)(2,1)S(1)} %pad_maximum_fusion.1), channel_id=1, source_target_pairs={{0,16},{16,32},{32,48},{48,64},{64,80},{80,96},{96,112},{112,128},... | collective-permute-start | bytes 24584 | tf_op jit(solution)/shard_map/ppermute | solution.py:670
  25.0 30.7 %copy-start.19 = (bf16[144,256]{1,0:T(8,128)(2,1)S(1)}, bf16[144,256]{1,0:T(8,128)(2,1)}, u32[]{:S(2)}) copy-start(bf16[144,256]{1,0:T(8,128)(2,1)} %get-tuple-element.34) | copy-start | bytes 221188
  25.3 79.0 %copy-start = (bf16[256,2048]{1,0:T(8,128)(2,1)}, bf16[256,2048]{1,0:T(8,128)(2,1)S(1)}, u32[]{:S(2)}) copy-start(bf16[256,2048]{1,0:T(8,128)(2,1)S(1)} %multiply_convert_fusion.refs_4_) | copy-start | bytes 3145732
  25.3 25.9 %collective-permute-start.12 = (bf16[256,2048]{1,0:T(8,128)(2,1)S(1)}, bf16[256,2048]{1,0:T(8,128)(2,1)S(1)}, u32[]{:S(2)}, u32[]{:S(2)}) collective-permute-start(bf16[256,2048]{1,0:T(8,128)(2,1)S(1)} %multiply_convert_fusion.refs_4_), channel_id=1, source_target_pairs={{0,1},{1,2},{2,3},{3,0},{4,5},{5,6},{6,7},{7,4},{8,9},{9,10},{10,1... | collective-permute-start | bytes 3145736 | tf_op jit(solution)/shard_map/ppermute | solution.py:674
  26.1 26.0 %collective-permute-start.14 = (bf16[256,2048]{1,0:T(8,128)(2,1)S(1)}, bf16[256,2048]{1,0:T(8,128)(2,1)S(1)}, u32[]{:S(2)}, u32[]{:S(2)}) collective-permute-start(bf16[256,2048]{1,0:T(8,128)(2,1)S(1)} %multiply_convert_fusion.refs_4_), channel_id=1, source_target_pairs={{0,3},{1,0},{2,1},{3,2},{4,7},{5,4},{6,5},{7,6},{8,11},{9,8},{10,9... | collective-permute-start | bytes 3145736 | tf_op jit(solution)/shard_map/ppermute | solution.py:675
  51.3 53.0 %copy-start.1 = (bf16[256,2048]{1,0:T(8,128)(2,1)}, bf16[256,2048]{1,0:T(8,128)(2,1)S(1)}, u32[]{:S(2)}) copy-start(bf16[256,2048]{1,0:T(8,128)(2,1)S(1)} %collective-permute-done.12.refs_5_) | copy-start | bytes 3145732
  52.2 64.4 %collective-permute-start.13 = (bf16[128,2048]{1,0:T(8,128)(2,1)}, bf16[128,2048]{1,0:T(8,128)(2,1)}, u32[]{:S(2)}, u32[]{:S(2)}) collective-permute-start(bf16[128,2048]{1,0:T(8,128)(2,1)} %slice.16), channel_id=1, source_target_pairs={{0,1},{1,2},{2,3},{3,0},{4,5},{5,6},{6,7},{7,4},{8,9},{9,10},{10,1... | collective-permute-start | bytes 1572872 | tf_op jit(solution)/shard_map/ppermute | solution.py:676
  52.2 55.4 %copy-start.2 = (bf16[256,2048]{1,0:T(8,128)(2,1)}, bf16[256,2048]{1,0:T(8,128)(2,1)S(1)}, u32[]{:S(2)}) copy-start(bf16[256,2048]{1,0:T(8,128)(2,1)S(1)} %collective-permute-done.14.refs_8_) | copy-start | bytes 3145732
  53.1 63.5 %collective-permute-start.15 = (bf16[128,2048]{1,0:T(8,128)(2,1)}, bf16[128,2048]{1,0:T(8,128)(2,1)}, u32[]{:S(2)}, u32[]{:S(2)}) collective-permute-start(bf16[128,2048]{1,0:T(8,128)(2,1)} %slice.17), channel_id=1, source_target_pairs={{0,3},{1,0},{2,1},{3,2},{4,7},{5,4},{6,5},{7,6},{8,11},{9,8},{10,9... | collective-permute-start | bytes 1572872 | tf_op jit(solution)/shard_map/ppermute | solution.py:677
  55.7 12.6 %collective-permute-start.2 = (bf16[144,256]{1,0:T(8,128)(2,1)S(1)}, bf16[144,256]{1,0:T(8,128)(2,1)S(1)}, u32[]{:S(2)}, u32[]{:S(2)}) collective-permute-start(bf16[144,256]{1,0:T(8,128)(2,1)S(1)} %copy-done.19), channel_id=1, source_target_pairs={{0,16},{16,32},{32,48},{48,64},{64,80},{80,96},{96,112},{112,128},... | collective-permute-start | bytes 221192 | tf_op jit(solution)/shard_map/ppermute | solution.py:686
  60.1 11.5 %collective-permute-start.3 = (bf16[144,256]{1,0:T(8,128)(2,1)S(1)}, bf16[144,256]{1,0:T(8,128)(2,1)S(1)}, u32[]{:S(2)}, u32[]{:S(2)}) collective-permute-start(bf16[144,256]{1,0:T(8,128)(2,1)S(1)} %copy-done.19), channel_id=1, source_target_pairs={{0,32},{16,48},{32,64},{48,80},{64,96},{80,112},{96,128},{112,144}... | collective-permute-start | bytes 221192 | tf_op jit(solution)/shard_map/ppermute | solution.py:686
  63.7 8.3 %collective-permute-start.4 = (bf16[144,256]{1,0:T(8,128)(2,1)S(1)}, bf16[144,256]{1,0:T(8,128)(2,1)S(1)}, u32[]{:S(2)}, u32[]{:S(2)}) collective-permute-start(bf16[144,256]{1,0:T(8,128)(2,1)S(1)} %copy-done.19), channel_id=1, source_target_pairs={{0,48},{16,64},{32,80},{48,96},{64,112},{80,128},{96,144},{112,160... | collective-permute-start | bytes 221192 | tf_op jit(solution)/shard_map/ppermute | solution.py:686
  68.4 6.7 %collective-permute-start.5 = (bf16[144,256]{1,0:T(8,128)(2,1)S(1)}, bf16[144,256]{1,0:T(8,128)(2,1)S(1)}, u32[]{:S(2)}, u32[]{:S(2)}) collective-permute-start(bf16[144,256]{1,0:T(8,128)(2,1)S(1)} %copy-done.19), channel_id=1, source_target_pairs={{0,64},{16,80},{32,96},{48,112},{64,128},{80,144},{96,160},{112,17... | collective-permute-start | bytes 221192 | tf_op jit(solution)/shard_map/ppermute | solution.py:686
  77.5 13.0 %collective-permute-start.6 = (bf16[144,256]{1,0:T(8,128)(2,1)}, bf16[144,256]{1,0:T(8,128)(2,1)S(1)}, u32[]{:S(2)}, u32[]{:S(2)}) collective-permute-start(bf16[144,256]{1,0:T(8,128)(2,1)} %shard_map.187.refs_0_), channel_id=1, source_target_pairs={{0,64},{16,80},{32,96},{48,112},{64,128},{80,144},{96,160},{112,17... | collective-permute-start | bytes 221192 | tf_op jit(solution)/shard_map/ppermute | solution.py:686
  82.5 10.4 %collective-permute-start.7 = (bf16[144,256]{1,0:T(8,128)(2,1)}, bf16[144,256]{1,0:T(8,128)(2,1)S(1)}, u32[]{:S(2)}, u32[]{:S(2)}) collective-permute-start(bf16[144,256]{1,0:T(8,128)(2,1)} %shard_map.187.refs_0_), channel_id=1, source_target_pairs={{0,128},{16,144},{32,160},{48,176},{64,192},{80,208},{96,224},{112... | collective-permute-start | bytes 221192 | tf_op jit(solution)/shard_map/ppermute | solution.py:686
  89.1 8.4 %collective-permute-start.8 = (bf16[144,256]{1,0:T(8,128)(2,1)}, bf16[144,256]{1,0:T(8,128)(2,1)S(1)}, u32[]{:S(2)}, u32[]{:S(2)}) collective-permute-start(bf16[144,256]{1,0:T(8,128)(2,1)} %shard_map.187.refs_0_), channel_id=1, source_target_pairs={{0,192},{16,208},{32,224},{48,240},{1,193},{17,209},{33,225},{49,2... | collective-permute-start | bytes 221192 | tf_op jit(solution)/shard_map/ppermute | solution.py:686
  107.6 5.6 %collective-permute-start.10 = (bf16[256,256]{1,0:T(8,128)(2,1)}, bf16[256,256]{1,0:T(8,128)(2,1)S(1)}, u32[]{:S(2)}, u32[]{:S(2)}) collective-permute-start(bf16[256,256]{1,0:T(8,128)(2,1)} %get-tuple-element.37), channel_id=1, source_target_pairs={{0,2},{1,3},{2,0},{3,1},{4,6},{5,7},{6,4},{7,5},{8,10},{9,11},{10,... | collective-permute-start | bytes 393224 | tf_op jit(solution)/shard_map/ppermute | solution.py:703
  108.6 6.1 %collective-permute-start.11 = (bf16[256,256]{1,0:T(8,128)(2,1)}, bf16[256,256]{1,0:T(8,128)(2,1)S(1)}, u32[]{:S(2)}, u32[]{:S(2)}) collective-permute-start(bf16[256,256]{1,0:T(8,128)(2,1)} %get-tuple-element.38), channel_id=1, source_target_pairs={{0,3},{1,0},{2,1},{3,2},{4,7},{5,4},{6,5},{7,6},{8,11},{9,8},{10,9... | collective-permute-start | bytes 393224 | tf_op jit(solution)/shard_map/ppermute | solution.py:703
  108.7 7.9 %collective-permute-start.9 = (bf16[256,256]{1,0:T(8,128)(2,1)}, bf16[256,256]{1,0:T(8,128)(2,1)S(1)}, u32[]{:S(2)}, u32[]{:S(2)}) collective-permute-start(bf16[256,256]{1,0:T(8,128)(2,1)} %get-tuple-element.36), channel_id=1, source_target_pairs={{0,1},{1,2},{2,3},{3,0},{4,5},{5,6},{6,7},{7,4},{8,9},{9,10},{10,1... | collective-permute-start | bytes 393224 | tf_op jit(solution)/shard_map/ppermute | solution.py:703
  122.1 9.1 %collective-permute-start.16 = (bf16[64,2176]{1,0:T(8,128)(2,1)}, bf16[64,2176]{1,0:T(8,128)(2,1)S(1)}, u32[]{:S(2)}, u32[]{:S(2)}) collective-permute-start(bf16[64,2176]{1,0:T(8,128)(2,1)} %get-tuple-element.40), channel_id=1, source_target_pairs={{0,4},{4,8},{8,12},{12,0},{1,5},{5,9},{9,13},{13,1},{2,6},{6,10},{... | collective-permute-start | bytes 835592 | tf_op jit(solution)/shard_map/ppermute | solution.py:708
  124.0 14.2 %collective-permute-start.17 = (bf16[64,2176]{1,0:T(8,128)(2,1)}, bf16[64,2176]{1,0:T(8,128)(2,1)S(1)}, u32[]{:S(2)}, u32[]{:S(2)}) collective-permute-start(bf16[64,2176]{1,0:T(8,128)(2,1)} %get-tuple-element.41), channel_id=1, source_target_pairs={{0,8},{4,12},{8,0},{12,4},{1,9},{5,13},{9,1},{13,5},{2,10},{6,14},... | collective-permute-start | bytes 835592 | tf_op jit(solution)/shard_map/ppermute | solution.py:708
  126.4 11.9 %collective-permute-start.18 = (bf16[64,2176]{1,0:T(8,128)(2,1)}, bf16[64,2176]{1,0:T(8,128)(2,1)S(1)}, u32[]{:S(2)}, u32[]{:S(2)}) collective-permute-start(bf16[64,2176]{1,0:T(8,128)(2,1)} %get-tuple-element.42), channel_id=1, source_target_pairs={{0,12},{4,0},{8,4},{12,8},{1,13},{5,1},{9,5},{13,9},{2,14},{6,2},{... | collective-permute-start | bytes 835592 | tf_op jit(solution)/shard_map/ppermute | solution.py:708
  (16 other events, 56.1 us)
Sparse Core Ops, SparseCore 0:
  25.1 103.8 all-gather.2

commit v5 on v4

--- a/solution.py
+++ b/solution.py
@@ -69,7 +69,7 @@
     return jnp.where(pick == 0, hi, jnp.where(pick == 1, mid, jnp.where(pick == 2, low, 0.0)))
 
 
-def mixer_state(x_inner, bc_input, rim, conv_weight, bc_weight, step_t, decay_t):
+def mixer_state(x_inner, bc_input, rim, conv_weight, bc_weight, step_t, decay_t, copies):
     rows, channels = x_inner.shape
     heads = step_t.shape[0]
     state_size = bc_input.shape[1] // 2
@@ -114,16 +114,18 @@
                 in_ref[at : at + SPAN, :] = held.astype(BF16)
                 held = spread(decays, j * heads, heads, head_width)[0:1, :] * held + state
                 total = total + lasts[:, j * heads : (j + 1) * heads]
-        send_ref[:state_size, :] = held.astype(BF16)
-        extra = three_rows(spread(total, 0, heads, head_width)[0:1, :], 16)
-        send_ref[state_size:, :] = extra.astype(BF16)
+        state = held.astype(BF16)
+        extra = three_rows(spread(total, 0, heads, head_width)[0:1, :], 16).astype(BF16)
+        for i in range(copies):
+            send_ref[i, :state_size, :] = state
+            send_ref[i, state_size:, :] = extra
 
     return call(
         kernel,
         (
             jax.ShapeDtypeStruct((rows, width), BF16),
             jax.ShapeDtypeStruct((blocks * state_size, channels), BF16),
-            jax.ShapeDtypeStruct((state_size + 16, channels), BF16),
+            jax.ShapeDtypeStruct((copies, state_size + 16, channels), BF16),
         ),
         (pltpu.VMEM((rows + 8, width), F32),),
     )(x_inner, bc_input, rim, conv_weight, bc_weight, step_t, decay_t)
@@ -202,27 +204,72 @@
     )(skip_gain, conv, entering, step_t, decay_t)
 
 
-def total_of(ref, state_size):
-    rows = ref[state_size:, :].astype(F32)
+def total_of(ref, i, state_size):
+    rows = ref[i, state_size:, :].astype(F32)
     return rows[0:1] + rows[1:2] + rows[2:3]
 
 
-def join_states(parts, state_size, last):
-    channels = parts[0].shape[1]
-
-    def kernel(*refs):
-        ins, o_ref = refs[:-1], refs[-1]
-        out = ins[0][:state_size, :].astype(F32)
-        total = total_of(ins[0], state_size)
-        for ref in ins[1:]:
-            out = out + jnp.exp(jnp.minimum(total, 0.0)) * ref[:state_size, :].astype(F32)
-            total = total + total_of(ref, state_size)
-        o_ref[:state_size, :] = out.astype(BF16)
-        if not last:
-            o_ref[state_size:, :] = three_rows(total, 16).astype(BF16)
-
-    height = state_size if last else state_size + 16
-    return call(kernel, jax.ShapeDtypeStruct((height, channels), BF16))(*parts)
+def join_near(place, received, state_size, copies):
+    count, height, channels = received.shape
+
+    def kernel(at_ref, r_ref, own_ref, log_ref, send_ref):
+        whole = jnp.zeros((state_size, channels), F32)
+        total = jnp.zeros((1, channels), F32)
+        own_ref[...] = whole
+        log_ref[...] = jnp.zeros((8, channels), F32)
+        for i in range(count):
+            log = total_of(r_ref, i, state_size)
+            whole = jnp.exp(jnp.minimum(log, 0.0)) * whole + r_ref[i, :state_size, :].astype(F32)
+            total = total + log
+
+            @pl.when(at_ref[0] == i + 1)
+            def _(whole=whole, total=total):
+                own_ref[...] = whole
+                log_ref[...] = jnp.broadcast_to(total, (8, channels))
+
+        state = whole.astype(BF16)
+        extra = three_rows(total, 16).astype(BF16)
+        for i in range(copies):
+            send_ref[i, :state_size, :] = state
+            send_ref[i, state_size:, :] = extra
+
+    vmem = pl.BlockSpec(memory_space=pltpu.VMEM)
+    return pl.pallas_call(
+        kernel,
+        out_shape=(
+            jax.ShapeDtypeStruct((state_size, channels), F32),
+            jax.ShapeDtypeStruct((8, channels), F32),
+            jax.ShapeDtypeStruct((copies, height, channels), BF16),
+        ),
+        in_specs=[pl.BlockSpec(memory_space=pltpu.SMEM), vmem],
+        out_specs=(vmem, vmem, vmem),
+        compiler_params=pltpu.CompilerParams(vmem_limit_bytes=58 << 20),
+    )(place, received)
+
+
+def join_far(place, received, own, log):
+    count, _, channels = received.shape
+    state_size = own.shape[0]
+
+    def kernel(at_ref, r_ref, own_ref, log_ref, o_ref):
+        whole = jnp.zeros((state_size, channels), F32)
+        o_ref[...] = own_ref[...].astype(BF16)
+        for i in range(count - 1):
+            step = jnp.exp(jnp.minimum(total_of(r_ref, i, state_size), 0.0))
+            whole = step * whole + r_ref[i, :state_size, :].astype(F32)
+
+            @pl.when(at_ref[0] == i + 1)
+            def _(whole=whole):
+                o_ref[...] = (jnp.exp(jnp.minimum(log_ref[0:1, :], 0.0)) * whole + own_ref[...]).astype(BF16)
+
+    vmem = pl.BlockSpec(memory_space=pltpu.VMEM)
+    return pl.pallas_call(
+        kernel,
+        out_shape=jax.ShapeDtypeStruct((state_size, channels), BF16),
+        in_specs=[pl.BlockSpec(memory_space=pltpu.SMEM), vmem, vmem, vmem],
+        out_specs=vmem,
+        compiler_params=pltpu.CompilerParams(vmem_limit_bytes=58 << 20),
+    )(place, received, own, log)
 
 
 def gate_rows(y_at, y_local, conv, e_cols, arriving, gate_input, heads, x_count, y_count):
@@ -650,8 +697,10 @@
     down_weight,
     out_grad,
 ):
-    ctx = ("z", "core")
-    ctx_count = lax.axis_size("z") * lax.axis_size("core")
+    chips = ("zq", "zp")
+    ctx = chips + ("core",)
+    group = lax.axis_size("zp") * lax.axis_size("core")
+    ctx_count = lax.axis_size("zq") * group
     x_count, y_count = lax.axis_size("x"), lax.axis_size("y")
     owners = x_count * y_count
     heads = step_size.shape[1]
@@ -679,23 +728,20 @@
     kept, other = pack_weights(core, gate_up_weight, down_weight)
     swapped = lax.ppermute(other, "core", [(0, 1), (1, 0)])
 
-    conv, held_in, sent = mixer_state(x_inner, bc_input, rim, conv_weight, bc_conv_weight, step_t, decay_t)
-    reach = 4
-
-    def earlier(value, distance):
-        return lax.ppermute(value, ctx, [(i, i + distance) for i in range(ctx_count - distance)])
-
-    near = [earlier(sent, d) for d in range(1, reach + 1)]
+    conv, held_in, sent = mixer_state(x_inner, bc_input, rim, conv_weight, bc_conv_weight, step_t, decay_t, group)
+    near = lax.all_to_all(sent, ("zp", "core"), split_axis=0, concat_axis=0, tiled=True)
     kept, swapped, conv = lax.optimization_barrier((kept, swapped, conv))
     stacked = jnp.stack([kept, swapped])
-    weights = lax.all_gather(stacked, "z", axis=0, tiled=False)
+    weights = lax.all_gather(stacked, chips, axis=0, tiled=False)
     gu_rows = kept.shape[0] - ff_width
     y_local, e_cols = mixer_rows(conv, held_in, step_t, decay_t, skip_gain, channels)
-    window = join_states(near, state_size, False)
-    windows = [window] + [earlier(window, d) for d in range(reach, ctx_count, reach)]
+    place = (lax.axis_index("zp") * lax.axis_size("core") + lax.axis_index("core")).astype(jnp.int32).reshape(1)
+    far_place = lax.axis_index("zq").astype(jnp.int32).reshape(1)
+    own_state, own_log, window = join_near(place, near, state_size, lax.axis_size("zq"))
+    windows = lax.all_to_all(window, "zq", split_axis=0, concat_axis=0, tiled=True)
 
     buffer = dispatch_grads(ids_t, out_grad, expert_total, owners, local_count)
-    arriving = join_states(windows, state_size, True)
+    arriving = join_far(far_place, windows, own_state, own_log)
     y_at = lax.axis_index("y").astype(jnp.int32).reshape(1)
     x_at = lax.axis_index("x").astype(jnp.int32).reshape(1)
     gated = gate_rows(y_at, y_local, conv, e_cols, arriving, gate_input, heads, x_count, y_count)
@@ -722,9 +768,9 @@
 def solution(mesh):
     ctx_count, exp_count = mesh.devices.shape
     side = int(round(exp_count**0.5))
-    devices = mesh.devices.reshape(ctx_count // 2, 2, side, exp_count // side)
-    fine = Mesh(devices, ("z", "core", "x", "y"))
-    ctx, exp = ("z", "core"), ("x", "y")
+    devices = mesh.devices.reshape(ctx_count // 4, 2, 2, side, exp_count // side)
+    fine = Mesh(devices, ("zq", "zp", "core", "x", "y"))
+    ctx, exp = ("zq", "zp", "core"), ("x", "y")
     token = P(ctx + exp, None)
     return jax.shard_map(
         local,

time: 244 us -> 206 us (0.84)
  waiting for transfers between devices: 49.1 us -> 24.6 us
  starting transfers between devices: 47.3 us -> 32.2 us
    ppermute x7 -> x0, starting transfers between devices: 28.8 us -> none  [earlier(): lax.ppermute(value, ctx, [(i, i + distance) for i in range(ctx_count - di...]
    ppermute x1, waiting for transfers between devices: 23.2 us -> 1.63 us  [local(): from_prev = lax.ppermute(folded, 'y', ring_route(y_count, 1))]
    all_to_all x0 -> x2, starting transfers between devices: none -> 13.7 us  [the longest x1 9.58 us: local(): lax.all_to_all(window, 'zq', split_axis=0, concat_axis=0, tiled=True)]
    ppermute x7 -> x0, waiting for transfers between devices: 10.6 us -> none  [earlier(): lax.ppermute(value, ctx, [(i, i + distance) for i in range(ctx_count - di...]
    all_to_all x0 -> x2, waiting for transfers between devices: none -> 10.2 us  [the longest x1 5.26 us: local(): lax.all_to_all(sent, ('zp', 'core'), split_axis=0, concat_axis=0, tiled=T...]
  transfers between devices with their start and end apart: 20 -> 15, of which waited for: 11 -> 9; matrix products, arithmetic and copies ran while one was open for 1% -> 2% of each run, Pallas kernels for 12% -> 14%
where the time goes in v5:
time: 206 us; the launch traced here: 205 us
  blocking collectives  76.1 us (37%)
  Pallas kernels  49.4 us (24%)
  starting transfers between devices  32.2 us (16%)
  waiting for transfers between devices  24.6 us (12%)
  between operations  14.2 us (7%)
  local copies, waits for them, and re-layouts  6.53 us (3%)
  other arithmetic  2.38 us (1%)
    all_to_all x1, blocking collectives, local(): lax.all_to_all(sent_rows, exchange, split_axis=0, concat_axis=0, tiled=True)  39.7 us
    all_to_all x1, blocking collectives, local(): lax.all_to_all(back, exchange, split_axis=0, concat_axis=0, tiled=True)  36.4 us
    pallas_call x1, Pallas kernels, experts(): pl.pallas_call(kernel, out_shape=jax.ShapeDtypeStruct((dests, 2 * each, L...  13.2 us
    all_to_all x1, starting transfers between devices, local(): lax.all_to_all(window, 'zq', split_axis=0, concat_axis=0, tiled=True)  9.58 us
    ppermute x3, waiting for transfers between devices, local(): lax.ppermute(parts[k], 'x', ring_route(x_count, k))  7.56 us
    all_to_all x1, waiting for transfers between devices, local(): lax.all_to_all(sent, ('zp', 'core'), split_axis=0, concat_axis=0, tiled=T...  5.26 us
    pallas_call x1, Pallas kernels, mixer_state(): call(kernel, (jax.ShapeDtypeStruct((rows, width), BF16), jax.ShapeDtypeSt...  5.18 us
    pallas_call x1, Pallas kernels, combine(): call(kernel, (shape, shape, jax.ShapeDtypeStruct((top, tokens), F32)), (p...  5.13 us
  transfers between devices with their start and end apart: 15, of which 9 were waited for; matrix products, arithmetic and copies ran while one was open for 2% of the time, Pallas kernels for 14%

profile of v5, /device:TPU:1, one launch (start us, length us, event | category | flops | bytes accessed | tf_op | source)
XLA Modules:
  0.0 205.5 jit_solution(4889662710049489078)
XLA Ops:
  7.2 2.4 %shard_map.184 = (bf16[2112,128]{1,0:T(8,128)(2,1)}, bf16[2112,128]{1,0:T(8,128)(2,1)}) custom-call(s32[1]{0:T(128)} %bitcast.core_ref, bf16[2,128,1408]{2,1,0:T(8,128)(2,1)} %g_ref.4, bf16[2,704,128]{2,1,0:T(8,128)(2,1)} %d_ref.1), custom_call_target="tpu_custom_call" | custom-call | tf_op jit(solution)/shard_map/pallas_call | solution.py:536
  9.6 3.2 %collective-permute-start = (bf16[2112,128]{1,0:T(8,128)(2,1)}, bf16[2112,128]{1,0:T(8,128)(2,1)S(1)}, u32[]{:S(2)}, u32[]{:S(2)}) collective-permute-start(bf16[2112,128]{1,0:T(8,128)(2,1)} %get-tuple-element.31), channel_id=1, source_target_pairs={{0,16},{16,0},{1,17},{17,1},{2,18},{18,2},{3,19},{19,3},{4,20},{20... | collective-permute-start | bytes 1622024 | tf_op jit(solution)/shard_map/ppermute | solution.py:729
  14.2 1.9 collective-permute-start.1
  17.8 5.2 %shard_map.185 = (bf16[1024,512]{1,0:T(8,128)(2,1)}, bf16[1024,256]{1,0:T(8,128)(2,1)}, bf16[4,144,256]{2,1,0:T(8,128)(2,1)}) custom-call(bf16[1024,256]{1,0:T(8,128)(2,1)} %x_ref.1, bf16[1024,256]{1,0:T(8,128)(2,1)} %bc_ref.1, bf16[8,512]{1,0:T(8,128)(2,1)} %copy-done.12, f32[4,256]{1,0:T(4,128)} %wx_ref.1, f32[4,256]{1,0:T(4,128)} %wb_ref.1, ...), custom_call_target="tpu_custom_call" | custom-call | tf_op jit(solution)/shard_map/pallas_call | solution.py:123
  23.0 2.1 %pad_maximum_fusion = bf16[2,2112,128]{2,1,0:T(8,128)(2,1)} fusion(bf16[1,2112,128]{2,1,0:T(8,128)(2,1)S(1)} %bitcast.16, bf16[1,2112,128]{2,1,0:T(8,128)(2,1)} %bitcast.15), kind=kLoop, calls=%fused_computation.1 | loop fusion | flops 540672 | bytes 2162688 | tf_op jit(solution)/shard_map/stack | solution.py:734
  26.2 1.9 collective-permute-start.7
  28.2 4.1 %all-to-all-start = ((bf16[4,144,256]{2,1,0:T(8,128)(2,1)}), bf16[4,144,256]{2,1,0:T(8,128)(2,1)S(1)}, u32[]{:S(2)}, u32[]{:S(2)}) async-start(bf16[4,144,256]{2,1,0:T(8,128)(2,1)} %get-tuple-element.37), calls=%async_computation | async-start | bytes 589824 | tf_op jit(solution)/shard_map/all_to_all | solution.py:732
  32.3 5.3 %all-to-all-done.r_ref = bf16[4,144,256]{2,1,0:T(8,128)(2,1)S(1)} async-done(((bf16[4,144,256]{2,1,0:T(8,128)(2,1)}), bf16[4,144,256]{2,1,0:T(8,128)(2,1)S(1)}, u32[]{:S(2)}, u32[]{:S(2)}) %all-to-all-start) | async-done | bytes 294944 | tf_op jit(solution)/shard_map/all_to_all | solution.py:732
  40.1 9.6 %all-to-all-start.1 = ((bf16[4,144,256]{2,1,0:T(8,128)(2,1)}), bf16[4,144,256]{2,1,0:T(8,128)(2,1)S(1)}, u32[]{:S(2)}, u32[]{:S(2)}) async-start(bf16[4,144,256]{2,1,0:T(8,128)(2,1)} %get-tuple-element.38), calls=%async_computation.1 | async-start | bytes 589824 | tf_op jit(solution)/shard_map/all_to_all | solution.py:741
  53.1 2.7 %collective-permute-start.8 = (bf16[128,2048]{1,0:T(8,128)(2,1)}, bf16[128,2048]{1,0:T(8,128)(2,1)}, u32[]{:S(2)}, u32[]{:S(2)}) collective-permute-start(bf16[128,2048]{1,0:T(8,128)(2,1)} %slice.17), channel_id=1, source_target_pairs={{0,3},{1,0},{2,1},{3,2},{4,7},{5,4},{6,5},{7,6},{8,11},{9,8},{10,9... | collective-permute-start | bytes 1572872 | tf_op jit(solution)/shard_map/ppermute | solution.py:726
  55.8 4.4 %shard_map.186 = (f32[1024,256]{1,0:T(8,128)}, f32[128,128]{1,0:T(8,128)}) custom-call(f32[4]{0:T(128)} %skip_ref.1, bf16[1024,512]{1,0:T(8,128)(2,1)} %get-tuple-element.33.conv_ref.c_ref, bf16[1024,256]{1,0:T(8,128)(2,1)} %get-tuple-element.34.in_ref, f32[4,1024]{1,0:T(4,128)} %bitcast.18, f32[4,1024]{1,0:T(4,128)} %bitcast.20), custom_call_target="tpu_custom_call" | custom-call | tf_op jit(solution)/shard_map/pallas_call | solution.py:195
  60.3 4.9 %all-to-all-done.1.r_ref = bf16[4,144,256]{2,1,0:T(8,128)(2,1)S(1)} async-done(((bf16[4,144,256]{2,1,0:T(8,128)(2,1)}), bf16[4,144,256]{2,1,0:T(8,128)(2,1)S(1)}, u32[]{:S(2)}, u32[]{:S(2)}) %all-to-all-start.1) | async-done | bytes 294944 | tf_op jit(solution)/shard_map/all_to_all | solution.py:741
  67.6 3.3 %shard_map.189 = (bf16[256,256]{1,0:T(8,128)(2,1)}, bf16[256,256]{1,0:T(8,128)(2,1)}, bf16[256,256]{1,0:T(8,128)(2,1)}, bf16[256,256]{1,0:T(8,128)(2,1)}) custom-call(s32[1]{0:T(128)} %bitcast.2.at_ref, f32[1024,256]{1,0:T(8,128)} %get-tuple-element.35.y_ref, bf16[1024,512]{1,0:T(8,128)(2,1)} %get-tuple-element.33.conv_ref.c_ref, ...), custom_call_target="tpu_custom_call" | custom-call | tf_op jit(solution)/shard_map/pallas_call | solution.py:300
  70.9 2.6 %collective-permute-start.3 = (bf16[256,256]{1,0:T(8,128)(2,1)}, bf16[256,256]{1,0:T(8,128)(2,1)S(1)}, u32[]{:S(2)}, u32[]{:S(2)}) collective-permute-start(bf16[256,256]{1,0:T(8,128)(2,1)} %get-tuple-element.43), channel_id=1, source_target_pairs={{0,2},{1,3},{2,0},{3,1},{4,6},{5,7},{6,4},{7,5},{8,10},{9,11},{10,... | collective-permute-start | bytes 393224 | tf_op jit(solution)/shard_map/ppermute | solution.py:749
  74.6 1.9 collective-permute-done.2.refs_1_
  79.4 4.9 %shard_map.190 = (bf16[64,2176]{1,0:T(8,128)(2,1)}, bf16[64,2176]{1,0:T(8,128)(2,1)}, bf16[64,2176]{1,0:T(8,128)(2,1)}, bf16[64,2176]{1,0:T(8,128)(2,1)}) custom-call(s32[1]{0:T(128)} %bitcast.1.at_ref, bf16[256,256]{1,0:T(8,128)(2,1)} %get-tuple-element.41.refs_0_, bf16[256,256]{1,0:T(8,128)(2,1)} %copy-done.9, bf16[256,256]{1,0:T(8,128)(2,1)} %copy-done.10, ...), custom_call_target="tpu_custom_call" | custom-call | tf_op jit(solution)/shard_map/pallas_call | solution.py:343
  84.3 2.7 %collective-permute-start.10 = (bf16[64,2176]{1,0:T(8,128)(2,1)}, bf16[64,2176]{1,0:T(8,128)(2,1)S(1)}, u32[]{:S(2)}, u32[]{:S(2)}) collective-permute-start(bf16[64,2176]{1,0:T(8,128)(2,1)} %get-tuple-element.47), channel_id=1, source_target_pairs={{0,8},{4,12},{8,0},{12,4},{1,9},{5,13},{9,1},{13,5},{2,10},{6,14},... | collective-permute-start | bytes 835592 | tf_op jit(solution)/shard_map/ppermute | solution.py:754
  88.5 3.1 %shard_map.191.refs_7_ = bf16[32,288,128]{2,1,0:T(8,128)(2,1)} custom-call(s32[4,64]{1,0:T(4,128)} %bitcast.23, bf16[64,2048]{1,0:T(8,128)(2,1)} %g_ref.7), custom_call_target="tpu_custom_call" | custom-call | tf_op jit(solution)/shard_map/pallas_call | solution.py:459
  91.6 7.4 %collective-permute-done.11.refs_3_ = bf16[64,2176]{1,0:T(8,128)(2,1)S(1)} collective-permute-done((bf16[64,2176]{1,0:T(8,128)(2,1)}, bf16[64,2176]{1,0:T(8,128)(2,1)S(1)}, u32[]{:S(2)}, u32[]{:S(2)}) %collective-permute-start.11) | collective-permute-done | bytes 278560 | tf_op jit(solution)/shard_map/ppermute | solution.py:754
  99.8 4.3 %shard_map.192 = (bf16[32,288,128]{2,1,0:T(8,128)(2,1)}, bf16[64,2048]{1,0:T(8,128)(2,1)}, f32[64,128]{1,0:T(8,128)}) custom-call(bf16[64,2176]{1,0:T(8,128)(2,1)} %get-tuple-element.45.refs_0_, bf16[64,2176]{1,0:T(8,128)(2,1)} %copy-done.8, bf16[64,2176]{1,0:T(8,128)(2,1)} %copy-done.6, ...), custom_call_target="tpu_custom_call", output_to_operand_aliasing={{0}: (7, {})} | custom-call | tf_op jit(solution)/shard_map/pallas_call | solution.py:503
  104.1 39.7 %all_to_all.20.x_ref = bf16[32,288,128]{2,1,0:T(8,128)(2,1)} all-to-all(bf16[32,288,128]{2,1,0:T(8,128)(2,1)} %get-tuple-element.49), channel_id=1, replica_groups=mesh['zq'=4,'zp'=2,'core'=2,'x'=4,'y'=4] {'core','x','y'}, dimensions={0} | all-to-all | bytes 4718592 | tf_op jit(solution)/shard_map/all_to_all | solution.py:759
  143.8 13.2 %shard_map.193 = bf16[32,288,128]{2,1,0:T(8,128)(2,1)} custom-call(s32[1]{0:T(128)} %bitcast.core_ref, bf16[32,288,128]{2,1,0:T(8,128)(2,1)} %all_to_all.20.x_ref, bf16[8,2,2112,128]{3,2,1,0:T(8,128)(2,1)} %bitcast.14), custom_call_target="tpu_custom_call" | custom-call | tf_op jit(solution)/shard_map/pallas_call | solution.py:609
  157.1 36.4 %all_to_all.21.r_ref = bf16[32,288,128]{2,1,0:T(8,128)(2,1)} all-to-all(bf16[32,288,128]{2,1,0:T(8,128)(2,1)} %shard_map.193), channel_id=1, replica_groups=mesh['zq'=4,'zp'=2,'core'=2,'x'=4,'y'=4] {'core','x','y'}, dimensions={0} | all-to-all | bytes 4718592 | tf_op jit(solution)/shard_map/all_to_all | solution.py:761
  193.5 5.1 %shard_map.194 = (bf16[64,2048]{1,0:T(8,128)(2,1)}, bf16[64,2048]{1,0:T(8,128)(2,1)}, f32[4,64]{1,0:T(4,128)}) custom-call(bf16[32,288,128]{2,1,0:T(8,128)(2,1)} %all_to_all.21.r_ref, bf16[64,2048]{1,0:T(8,128)(2,1)} %get-tuple-element.52.h_ref, f32[64,128]{1,0:T(8,128)} %get-tuple-element.53.v_ref, bf16[64,2048]{1,0:T(8,128)(2,1)} %g_ref.7, ...), custom_call_target="tpu_custom_call" | custom-call | tf_op jit(solution)/shard_map/pallas_call | solution.py:670
  (55 shorter events, 18.9 us)
Async XLA Ops:
  7.2 136.7 %all-gather.3.cloned.1.call-start = ((), (), s32[]{:S(2)}) async-start(), calls=%async_computation.4 | async-start | bytes 9732096 | tf_op jit(solution)/shard_map/all_gather | solution.py:735
  9.6 13.4 %collective-permute-start = (bf16[2112,128]{1,0:T(8,128)(2,1)}, bf16[2112,128]{1,0:T(8,128)(2,1)S(1)}, u32[]{:S(2)}, u32[]{:S(2)}) collective-permute-start(bf16[2112,128]{1,0:T(8,128)(2,1)} %get-tuple-element.31), channel_id=1, source_target_pairs={{0,16},{16,0},{1,17},{17,1},{2,18},{18,2},{3,19},{19,3},{4,20},{20... | collective-permute-start | bytes 1622024 | tf_op jit(solution)/shard_map/ppermute | solution.py:729
  14.2 3.1 %collective-permute-start.1 = (bf16[8,512]{1,0:T(8,128)(2,1)S(1)}, bf16[8,512]{1,0:T(8,128)(2,1)S(1)}, u32[]{:S(2)}, u32[]{:S(2)}) collective-permute-start(bf16[8,512]{1,0:T(8,128)(2,1)S(1)} %pad_maximum_fusion.1), channel_id=1, source_target_pairs={{0,16},{16,32},{32,48},{48,64},{64,80},{80,96},{96,112},{112,128},... | collective-permute-start | bytes 24584 | tf_op jit(solution)/shard_map/ppermute | solution.py:719
  17.8 7.3 %copy-start.5 = (bf16[256,2048]{1,0:T(8,128)(2,1)S(1)}, bf16[256,2048]{1,0:T(8,128)(2,1)}, u32[]{:S(2)}) copy-start(bf16[256,2048]{1,0:T(8,128)(2,1)} %param.26) | copy-start | bytes 3145732
  17.8 7.4 %copy-start.13 = (f32[256]{0:T(256)S(1)}, f32[256]{0:T(256)}, u32[]{:S(2)}) copy-start(f32[256]{0:T(256)} %param.25) | copy-start | bytes 3076
  25.4 34.8 %copy-start = (bf16[256,2048]{1,0:T(8,128)(2,1)}, bf16[256,2048]{1,0:T(8,128)(2,1)S(1)}, u32[]{:S(2)}) copy-start(bf16[256,2048]{1,0:T(8,128)(2,1)S(1)} %multiply_convert_fusion.refs_4_) | copy-start | bytes 3145732
  25.4 25.9 %collective-permute-start.5 = (bf16[256,2048]{1,0:T(8,128)(2,1)S(1)}, bf16[256,2048]{1,0:T(8,128)(2,1)S(1)}, u32[]{:S(2)}, u32[]{:S(2)}) collective-permute-start(bf16[256,2048]{1,0:T(8,128)(2,1)S(1)} %multiply_convert_fusion.refs_4_), channel_id=1, source_target_pairs={{0,1},{1,2},{2,3},{3,0},{4,5},{5,6},{6,7},{7,4},{8,9},{9,10},{10,1... | collective-permute-start | bytes 3145736 | tf_op jit(solution)/shard_map/ppermute | solution.py:723
  26.2 26.0 %collective-permute-start.7 = (bf16[256,2048]{1,0:T(8,128)(2,1)S(1)}, bf16[256,2048]{1,0:T(8,128)(2,1)S(1)}, u32[]{:S(2)}, u32[]{:S(2)}) collective-permute-start(bf16[256,2048]{1,0:T(8,128)(2,1)S(1)} %multiply_convert_fusion.refs_4_), channel_id=1, source_target_pairs={{0,3},{1,0},{2,1},{3,2},{4,7},{5,4},{6,5},{7,6},{8,11},{9,8},{10,9... | collective-permute-start | bytes 3145736 | tf_op jit(solution)/shard_map/ppermute | solution.py:724
  28.2 9.4 %all-to-all-start = ((bf16[4,144,256]{2,1,0:T(8,128)(2,1)}), bf16[4,144,256]{2,1,0:T(8,128)(2,1)S(1)}, u32[]{:S(2)}, u32[]{:S(2)}) async-start(bf16[4,144,256]{2,1,0:T(8,128)(2,1)} %get-tuple-element.37), calls=%async_computation | async-start | bytes 589824 | tf_op jit(solution)/shard_map/all_to_all | solution.py:732
  37.6 0.7 copy-start.4
  40.1 25.0 %all-to-all-start.1 = ((bf16[4,144,256]{2,1,0:T(8,128)(2,1)}), bf16[4,144,256]{2,1,0:T(8,128)(2,1)S(1)}, u32[]{:S(2)}, u32[]{:S(2)}) async-start(bf16[4,144,256]{2,1,0:T(8,128)(2,1)} %get-tuple-element.38), calls=%async_computation.1 | async-start | bytes 589824 | tf_op jit(solution)/shard_map/all_to_all | solution.py:741
  51.4 16.2 %copy-start.1 = (bf16[256,2048]{1,0:T(8,128)(2,1)}, bf16[256,2048]{1,0:T(8,128)(2,1)S(1)}, u32[]{:S(2)}) copy-start(bf16[256,2048]{1,0:T(8,128)(2,1)S(1)} %collective-permute-done.5.refs_5_) | copy-start | bytes 3145732
  52.3 26.5 %collective-permute-start.6 = (bf16[128,2048]{1,0:T(8,128)(2,1)}, bf16[128,2048]{1,0:T(8,128)(2,1)}, u32[]{:S(2)}, u32[]{:S(2)}) collective-permute-start(bf16[128,2048]{1,0:T(8,128)(2,1)} %slice.16), channel_id=1, source_target_pairs={{0,1},{1,2},{2,3},{3,0},{4,5},{5,6},{6,7},{7,4},{8,9},{9,10},{10,1... | collective-permute-start | bytes 1572872 | tf_op jit(solution)/shard_map/ppermute | solution.py:725
  52.3 18.6 %copy-start.2 = (bf16[256,2048]{1,0:T(8,128)(2,1)}, bf16[256,2048]{1,0:T(8,128)(2,1)S(1)}, u32[]{:S(2)}) copy-start(bf16[256,2048]{1,0:T(8,128)(2,1)S(1)} %collective-permute-done.7.refs_8_) | copy-start | bytes 3145732
  53.1 25.6 %collective-permute-start.8 = (bf16[128,2048]{1,0:T(8,128)(2,1)}, bf16[128,2048]{1,0:T(8,128)(2,1)}, u32[]{:S(2)}, u32[]{:S(2)}) collective-permute-start(bf16[128,2048]{1,0:T(8,128)(2,1)} %slice.17), channel_id=1, source_target_pairs={{0,3},{1,0},{2,1},{3,2},{4,7},{5,4},{6,5},{7,6},{8,11},{9,8},{10,9... | collective-permute-start | bytes 1572872 | tf_op jit(solution)/shard_map/ppermute | solution.py:726
  65.2 0.7 copy-start.3
  70.9 5.7 %collective-permute-start.2 = (bf16[256,256]{1,0:T(8,128)(2,1)}, bf16[256,256]{1,0:T(8,128)(2,1)S(1)}, u32[]{:S(2)}, u32[]{:S(2)}) collective-permute-start(bf16[256,256]{1,0:T(8,128)(2,1)} %get-tuple-element.42), channel_id=1, source_target_pairs={{0,1},{1,2},{2,3},{3,0},{4,5},{5,6},{6,7},{7,4},{8,9},{9,10},{10,1... | collective-permute-start | bytes 393224 | tf_op jit(solution)/shard_map/ppermute | solution.py:749
  70.9 7.1 %collective-permute-start.3 = (bf16[256,256]{1,0:T(8,128)(2,1)}, bf16[256,256]{1,0:T(8,128)(2,1)S(1)}, u32[]{:S(2)}, u32[]{:S(2)}) collective-permute-start(bf16[256,256]{1,0:T(8,128)(2,1)} %get-tuple-element.43), channel_id=1, source_target_pairs={{0,2},{1,3},{2,0},{3,1},{4,6},{5,7},{6,4},{7,5},{8,10},{9,11},{10,... | collective-permute-start | bytes 393224 | tf_op jit(solution)/shard_map/ppermute | solution.py:749
  73.6 5.1 %collective-permute-start.4 = (bf16[256,256]{1,0:T(8,128)(2,1)}, bf16[256,256]{1,0:T(8,128)(2,1)S(1)}, u32[]{:S(2)}, u32[]{:S(2)}) collective-permute-start(bf16[256,256]{1,0:T(8,128)(2,1)} %get-tuple-element.44), channel_id=1, source_target_pairs={{0,3},{1,0},{2,1},{3,2},{4,7},{5,4},{6,5},{7,6},{8,11},{9,8},{10,9... | collective-permute-start | bytes 393224 | tf_op jit(solution)/shard_map/ppermute | solution.py:749
  76.6 2.2 %copy-start.9 = (bf16[256,256]{1,0:T(8,128)(2,1)}, bf16[256,256]{1,0:T(8,128)(2,1)S(1)}, u32[]{:S(2)}) copy-start(bf16[256,256]{1,0:T(8,128)(2,1)S(1)} %collective-permute-done.2.refs_1_) | copy-start | bytes 393220
  84.3 7.3 %collective-permute-start.10 = (bf16[64,2176]{1,0:T(8,128)(2,1)}, bf16[64,2176]{1,0:T(8,128)(2,1)S(1)}, u32[]{:S(2)}, u32[]{:S(2)}) collective-permute-start(bf16[64,2176]{1,0:T(8,128)(2,1)} %get-tuple-element.47), channel_id=1, source_target_pairs={{0,8},{4,12},{8,0},{12,4},{1,9},{5,13},{9,1},{13,5},{2,10},{6,14},... | collective-permute-start | bytes 835592 | tf_op jit(solution)/shard_map/ppermute | solution.py:754
  87.0 12.0 %collective-permute-start.11 = (bf16[64,2176]{1,0:T(8,128)(2,1)}, bf16[64,2176]{1,0:T(8,128)(2,1)S(1)}, u32[]{:S(2)}, u32[]{:S(2)}) collective-permute-start(bf16[64,2176]{1,0:T(8,128)(2,1)} %get-tuple-element.48), channel_id=1, source_target_pairs={{0,12},{4,0},{8,4},{12,8},{1,13},{5,1},{9,5},{13,9},{2,14},{6,2},{... | collective-permute-start | bytes 835592 | tf_op jit(solution)/shard_map/ppermute | solution.py:754
  87.9 11.3 %collective-permute-start.9 = (bf16[64,2176]{1,0:T(8,128)(2,1)}, bf16[64,2176]{1,0:T(8,128)(2,1)S(1)}, u32[]{:S(2)}, u32[]{:S(2)}) collective-permute-start(bf16[64,2176]{1,0:T(8,128)(2,1)} %get-tuple-element.46), channel_id=1, source_target_pairs={{0,4},{4,8},{8,12},{12,0},{1,5},{5,9},{9,13},{13,1},{2,6},{6,10},{... | collective-permute-start | bytes 835592 | tf_op jit(solution)/shard_map/ppermute | solution.py:754
  91.6 7.6 %copy-start.6 = (bf16[64,2176]{1,0:T(8,128)(2,1)}, bf16[64,2176]{1,0:T(8,128)(2,1)S(1)}, u32[]{:S(2)}) copy-start(bf16[64,2176]{1,0:T(8,128)(2,1)S(1)} %collective-permute-done.10.refs_2_) | copy-start | bytes 835588
  (5 other events, 3.4 us)
Sparse Core Ops, SparseCore 0:
  25.3 106.3 all-gather.2
